TPU v7x, 128 devices: a whole 4x4x4 slice. The times are simulated.
128 devices in a mesh: ctx: 16 (over x_lo, y, core), head: 8 (over x_hi, z).
Axes of the slice: x: 4 (x_hi: 2, x_lo: 2; x = x_hi * 2 + x_lo), y: 4, z: 4, core: 2. Of those that a mesh axis runs over, the one named last changes fastest.
Arguments:
- q_latent: bfloat16 [4096, 1536], P('ctx', 'head'), may hold values from -70 to 70
- kv_latent: bfloat16 [4096, 576], P('ctx', 'head'), may hold values from -6 to 6
- w_query: bfloat16 [1536, 24576], P(None, 'head'), may hold values from -0.15625 to 0.15625
- w_key: bfloat16 [512, 16384], P(None, 'head'), may hold values from -0.25 to 0.25
- w_value: bfloat16 [512, 16384], P(None, 'head'), may hold values from -0.25 to 0.25
- d_out: bfloat16 [4096, 16384], P('ctx', 'head'), may hold values from -6 to 6
Outputs:
- attn_out: bfloat16 [4096, 16384], P('ctx', 'head')
- grad_qlat: float32 [4096, 1536], P('ctx', 'head')
- grad_kvlat: float32 [4096, 576], P('ctx', 'head')
All inputs are finite; a program needn't handle non-finite values.
Results may differ from a plain program's by a relative error of at most 0.023.
The roundings to bfloat16 on the way count: a program that leaves them out, or rounds other values in their place, can miss the bound.
Values may be sent and summed in bfloat16 or wider, within the bound.
No kernel may reach another device: no remote copies, remote signals or barrier semaphores. Data moves between devices by JAX's collectives and lax.ppermute only.
A program may use at most 128 MiB of HBM per device.

v0:
```python
import jax
import jax.numpy as jnp
from jax import lax
from jax.sharding import PartitionSpec as P

KVL = 512
ROPE = 64
NOPE = 128
VDIM = 128
HEAD_DEV = 16


def in_order(blocks, dim):
    blocks = jnp.moveaxis(blocks, 0, dim)
    shape = blocks.shape
    return blocks.reshape(*shape[:dim], shape[dim] * shape[dim + 1], *shape[dim + 2 :])


def sent_to_all(array, axis):
    copies = jnp.broadcast_to(array, (lax.axis_size(axis), *array.shape))
    return lax.all_to_all(copies, axis, split_axis=0, concat_axis=0, tiled=True)


def collect(array, axis, dim):
    return in_order(sent_to_all(array, axis), dim)


def from_behind(array, axis, by):
    peers = lax.axis_size(axis)
    pairs = [(i, i + by) for i in range(peers) if 0 <= i + by < peers]
    return lax.ppermute(array, axis, pairs)


def split_up(array, dim, peers):
    shape = array.shape
    blocks = array.reshape(*shape[:dim], peers, shape[dim] // peers, *shape[dim + 1 :])
    return jnp.moveaxis(blocks, dim, 0)


def sent_and_summed(array, axis, dim):
    peers = lax.axis_size(axis)
    blocks = lax.all_to_all(split_up(array, dim, peers), axis, 0, 0, tiled=True)
    return jnp.sum(blocks.astype(jnp.float32), axis=0)


def on_device(q_latent, kv_latent, w_query, w_key, w_value, d_out):
    block_rows = q_latent.shape[0]
    per_dev = HEAD_DEV
    width = NOPE + ROPE
    softmax_scale = width ** (-0.5)
    queries = jnp.dot(collect(q_latent, "head", 1), w_query, preferred_element_type=jnp.float32)
    queries = queries.astype(jnp.bfloat16).reshape(block_rows, per_dev, width)
    latent = collect(kv_latent, "head", 1)

    def expand(latent_rows):
        main_cols = latent_rows[:, :KVL]
        keys_nope = jnp.dot(main_cols, w_key, preferred_element_type=jnp.float32).astype(
            jnp.bfloat16
        )
        values = jnp.dot(main_cols, w_value, preferred_element_type=jnp.float32).astype(
            jnp.bfloat16
        )
        return (
            keys_nope.reshape(block_rows, per_dev, NOPE),
            latent_rows[:, KVL:],
            values.reshape(block_rows, per_dev, VDIM),
        )

    own_keys = expand(latent)
    previous = expand(from_behind(latent, "ctx", 1))
    keys_all = jnp.concatenate([previous[0], own_keys[0]], 0)
    rope_all = jnp.concatenate([previous[1], own_keys[1]], 0)
    values_all = jnp.concatenate([previous[2], own_keys[2]], 0)
    leading = lax.axis_index("ctx") == 0
    query_pos = jnp.arange(block_rows)[:, None]
    key_pos = jnp.arange(2 * block_rows)[None, :]
    visible = jnp.where(
        key_pos < block_rows, jnp.logical_not(leading), key_pos - block_rows <= query_pos
    )[None]
    query_nope = queries[..., :NOPE]
    query_rope = queries[..., NOPE:]
    scores = jnp.einsum("qhd,khd->hqk", query_nope, keys_all, preferred_element_type=jnp.float32)
    scores = (
        scores + jnp.einsum("qhr,kr->hqk", query_rope, rope_all, preferred_element_type=jnp.float32)
    ) * softmax_scale
    scores = jnp.where(visible, scores, jnp.float32(-1e30))
    maxima = jnp.max(scores, -1, keepdims=True)
    expons = jnp.where(visible, jnp.exp(scores - maxima), jnp.float32(0.0))
    probs = expons / jnp.sum(expons, -1, keepdims=True)
    probs_b = probs.astype(jnp.bfloat16)
    output = jnp.einsum(
        "hqk,khd->qhd", probs_b, values_all, preferred_element_type=jnp.float32
    ).astype(jnp.bfloat16)
    grad_out = d_out.reshape(block_rows, per_dev, VDIM)
    dprob = jnp.einsum("qhd,khd->hqk", grad_out, values_all, preferred_element_type=jnp.float32)
    row_dot = jnp.sum(grad_out.astype(jnp.float32) * output.astype(jnp.float32), -1).T[..., None]
    dscore = (probs * (dprob - row_dot) * softmax_scale).astype(jnp.bfloat16)
    grad_qnope = jnp.einsum("hqk,khd->qhd", dscore, keys_all, preferred_element_type=jnp.float32)
    grad_qrope = jnp.einsum("hqk,kr->qhr", dscore, rope_all, preferred_element_type=jnp.float32)
    grad_query = (
        jnp.concatenate([grad_qnope, grad_qrope], -1)
        .astype(jnp.bfloat16)
        .reshape(block_rows, per_dev * width)
    )
    grad_qpart = jnp.dot(grad_query, w_query.T, preferred_element_type=jnp.float32)
    grad_knope = jnp.einsum(
        "hqk,qhd->khd", dscore, query_nope, preferred_element_type=jnp.float32
    ).astype(jnp.bfloat16)
    grad_krope = jnp.einsum(
        "hqk,qhr->khr", dscore, query_rope, preferred_element_type=jnp.float32
    ).astype(jnp.bfloat16)
    grad_value = jnp.einsum(
        "hqk,qhd->khd", probs_b, grad_out, preferred_element_type=jnp.float32
    ).astype(jnp.bfloat16)

    def project(knope_part, krope_part, value_part):
        main_cols = jnp.dot(
            knope_part.reshape(block_rows, per_dev * NOPE),
            w_key.T,
            preferred_element_type=jnp.float32,
        )
        main_cols = main_cols + jnp.dot(
            value_part.reshape(block_rows, per_dev * VDIM),
            w_value.T,
            preferred_element_type=jnp.float32,
        )
        rope_cols = jnp.sum(krope_part.astype(jnp.float32), axis=1)
        return jnp.concatenate([main_cols, rope_cols], -1)

    own_part = project(grad_knope[block_rows:], grad_krope[block_rows:], grad_value[block_rows:])
    earlier = project(grad_knope[:block_rows], grad_krope[:block_rows], grad_value[:block_rows])
    grad_kvpart = own_part + from_behind(earlier.astype(jnp.bfloat16), "ctx", -1).astype(
        earlier.dtype
    )
    grad_qlat, grad_kvlat = (
        sent_and_summed(grad_qpart.astype(jnp.bfloat16), "head", 1),
        sent_and_summed(grad_kvpart.astype(jnp.bfloat16), "head", 1),
    )
    return (output.reshape(block_rows, per_dev * VDIM), grad_qlat, grad_kvlat)


def solution(mesh):
    return jax.shard_map(
        on_device,
        mesh=mesh,
        in_specs=(
            P("ctx", "head"),
            P("ctx", "head"),
            P(None, "head"),
            P(None, "head"),
            P(None, "head"),
            P("ctx", "head"),
        ),
        out_specs=(P("ctx", "head"), P("ctx", "head"), P("ctx", "head")),
        check_vma=False,
    )
```

profile of v0, /device:TPU:16, one launch (start us, length us, event | category | flops | bytes accessed | tf_op | source)
XLA Modules:
  0.0 139.4 jit_solution(6800513961380084557)
XLA Ops:
  0.6 0.0 copy-start
  0.6 0.0 copy-start.12
  0.7 1.7 %broadcast_in_dim.42 = bf16[8,256,72]{1,2,0:T(8,128)(2,1)} broadcast(bf16[256,72]{0,1:T(8,128)(2,1)} %param.7), dimensions={1,2} | broadcast | bytes 331776 | tf_op jit(solution)/shard_map/broadcast_in_dim | solution.py:20
  2.3 7.8 %all-to-all-start = ((bf16[8,256,72]{1,2,0:T(8,128)(2,1)}), bf16[8,256,72]{1,2,0:T(8,128)(2,1)S(1)}, u32[]{:S(2)}, u32[]{:S(2)}) async-start(bf16[8,256,72]{1,2,0:T(8,128)(2,1)} %broadcast_in_dim.42), calls=%async_computation | async-start | bytes 589824 | tf_op jit(solution)/shard_map/all_to_all | solution.py:21
  10.1 2.3 %copy.47 = bf16[256,2048]{0,1:T(8,128)(2,1)} copy(bf16[256,2048]{1,0:T(8,128)(2,1)} %param.11) | data formatting | bytes 2097152 | tf_op args[5]
  12.4 0.7 fusion.16
  13.1 6.0 %all-to-all-done = bf16[8,256,72]{1,2,0:T(8,128)(2,1)S(1)} async-done(((bf16[8,256,72]{1,2,0:T(8,128)(2,1)}), bf16[8,256,72]{1,2,0:T(8,128)(2,1)S(1)}, u32[]{:S(2)}, u32[]{:S(2)}) %all-to-all-start) | async-done | bytes 294944 | tf_op jit(solution)/shard_map/all_to_all | solution.py:21
  19.1 0.0 copy-done.12
  19.1 1.0 broadcast_in_dim.46
  20.1 3.5 %all-to-all-start.1 = ((bf16[8,256,192]{1,2,0:T(8,128)(2,1)}), bf16[8,256,192]{1,2,0:T(8,128)(2,1)S(1)}, u32[]{:S(2)}, u32[]{:S(2)}) async-start(bf16[8,256,192]{1,2,0:T(8,128)(2,1)} %broadcast_in_dim.46), calls=%async_computation.1 | async-start | bytes 1572864 | tf_op jit(solution)/shard_map/all_to_all | solution.py:21
  23.7 1.9 %collective-permute-start = (bf16[256,576]{0,1:T(8,128)(2,1)S(1)}, bf16[256,576]{0,1:T(8,128)(2,1)S(1)}, u32[]{:S(2)}, u32[]{:S(2)}) collective-permute-start(bf16[256,576]{0,1:T(8,128)(2,1)S(1)} %bitcast.101), channel_id=1, source_target_pairs={{0,8},{8,16},{16,24},{24,32},{32,40},{40,48},{48,56},{56,64},{64,7... | collective-permute-start | bytes 884744 | tf_op jit(solution)/shard_map/ppermute | solution.py:31
  25.6 3.3 %convolution_convert_fusion.4 = bf16[256,2048]{1,0:T(8,128)(2,1)} fusion(bf16[512,2048]{1,0:T(8,128)(2,1)} %param.10, bf16[256,576]{0,1:T(8,128)(2,1)S(1)} %bitcast.102), kind=kOutput, calls=%fused_computation.14 | convolution fusion | flops 537395200 | bytes 3407872 | tf_op jit(solution)/shard_map/dot_general | solution.py:60
  28.9 2.3 %copy.65 = bf16[256,2048]{0,1:T(8,128)(2,1)} copy(bf16[256,2048]{1,0:T(8,128)(2,1)} %convolution_convert_fusion.4) | data formatting | bytes 2097152 | tf_op jit(solution)/shard_map/reshape | solution.py:66
  31.2 1.7 %fusion.7 = bf16[32,16,8,128]{3,2,1,0:T(8,128)(2,1)} fusion(bf16[512,2048]{1,0:T(8,128)(2,1)S(1)} %copy-done, bf16[256,576]{0,1:T(8,128)(2,1)S(1)} %bitcast.104), kind=kOutput, calls=%fused_computation.26 | convolution fusion | flops 537395200 | bytes 3407872 | tf_op jit(solution)/shard_map/dot_general | solution.py:57
  32.9 0.0 collective-permute-done
  32.9 1.7 %convolution_convert_fusion.5 = bf16[256,2048]{1,0:T(8,128)(2,1)} fusion(bf16[512,2048]{1,0:T(8,128)(2,1)S(1)} %copy-done.1, bf16[256,576]{0,1:T(8,128)(2,1)S(1)} %collective-permute-done), kind=kOutput, calls=%fused_computation.15 | convolution fusion | flops 537395200 | bytes 3407872 | tf_op jit(solution)/shard_map/dot_general | solution.py:60
  34.6 2.3 %copy.64 = bf16[256,2048]{0,1:T(8,128)(2,1)} copy(bf16[256,2048]{1,0:T(8,128)(2,1)} %convolution_convert_fusion.5) | data formatting | bytes 2097152 | tf_op jit(solution)/shard_map/reshape | solution.py:66
  36.9 0.7 fusion.6
  37.7 1.3 bitcast_dynamic-update-slice_fusion.1
  39.0 1.3 bitcast_dynamic-update-slice_fusion
  40.2 0.0 all-to-all-done.1
  40.2 7.5 %convolution_convert_fusion = bf16[256,3072]{1,0:T(8,128)(2,1)} fusion(bf16[256,1536]{0,1:T(8,128)(2,1)S(1)} %bitcast.97, bf16[1536,3072]{1,0:T(8,128)(2,1)} %param.8), kind=kOutput, calls=%fused_computation.9 | convolution fusion | flops 2416705536 | bytes 11796480 | tf_op jit(solution)/shard_map/dot_general | solution.py:51
  47.7 2.6 %copy.42 = bf16[256,3072]{0,1:T(8,128)(2,1)} copy(bf16[256,3072]{1,0:T(8,128)(2,1)} %convolution_convert_fusion) | data formatting | bytes 3145728 | tf_op jit(solution)/shard_map/convert_element_type | solution.py:52
  50.3 6.5 %fusion.12 = f32[16,256,512]{2,1,0:T(8,128)} fusion(bf16[512,16,128]{2,0,1:T(8,128)(2,1)} %bitcast_dynamic-update-slice_fusion, bf16[256,16,192]{0,2,1:T(8,128)(2,1)} %bitcast.91), kind=kOutput, calls=%fused_computation.37 | convolution fusion | flops 536870912 | bytes 11534336 | tf_op jit(solution)/shard_map/qhd,khd->hqk/dot_general | solution.py:82
  56.8 10.6 %fusion.29 = (f32[16,256]{1,0:T(8,128)S(1)}, f32[16,256,512]{2,1,0:T(8,128)}) fusion(pred[256,512]{1,0:T(8,128)(4,1)S(1)} %copy-done.11, f32[16,256,512]{2,1,0:T(8,128)} %fusion.12, bf16[256,16,192]{0,2,1:T(8,128)(2,1)} %bitcast.92, bf16[256,64]{0,1:T(8,128)(2,1)S(1)} %slice.52, bf16[256,64]{0,1:T(8,128)(2,1)S(1)} %slice.51), kind=kOutput, calls=%fused_computation.62 | convolution fusion | flops 281149952 | bytes 17645568 | tf_op jit(solution)/shard_map/sub | solution.py:88
  67.4 3.9 %fusion.5 = bf16[16,256,512]{2,1,0:T(8,128)(2,1)S(1)} fusion(f32[16,256,512]{2,1,0:T(8,128)} %get-tuple-element.17, f32[16,256]{1,0:T(8,128)S(1)} %get-tuple-element.16), kind=kLoop, calls=%fused_computation.10 | loop fusion | flops 4194304 | bytes 12599296 | tf_op jit(solution)/shard_map/convert_element_type | solution.py:90
  71.3 0.0 copy-done.4
  71.4 0.0 copy-start.8
  71.4 0.0 slice-start
  71.4 0.7 convert_bitcast_fusion
  72.1 0.5 copy-done.8
  72.6 0.3 copy-done.9
  72.9 2.6 %multiply_reduce_fusion = (f32[256,16]{0,1:T(8,128)S(1)}, bf16[16,128,256]{2,1,0:T(8,128)(2,1)}) fusion(bf16[256,2048]{0,1:T(8,128)(2,1)S(1)} %copy-done.4, bf16[16,256,512]{2,1,0:T(8,128)(2,1)S(1)} %fusion.5, bf16[256,16,128]{0,2,1:T(8,128)(2,1)S(1)} %bitcast.107, bf16[256,16,128]{0,2,1:T(8,128)(2,1)S(1)} %bitcast.109), kind=kOutput, calls=%fused_computation.19 | convolution fusion | flops 543682560 | bytes 8404992 | tf_op jit(solution)/shard_map/hqk,khd->qhd/dot_general | solution.py:91
  75.5 0.1 slice-done.1
  75.6 2.3 %fusion.2 = bf16[16,256,512]{2,1,0:T(8,128)(2,1)S(1)} fusion(f32[16,256]{1,0:T(8,128)S(1)} %bitcast.114, f32[16,256,512]{2,1,0:T(8,128)S(1)} %bitcast.96, f32[16,256]{1,0:T(8,128)S(1)} %get-tuple-element.16, bf16[256,16,128]{0,2,1:T(8,128)(2,1)S(1)} %bitcast.99, bf16[256,16,128]{0,2,1:T(8,128)(2,1)S(1)} %bitcast.108, bf16[256,16,128]{0,2,1:T(8,128)(2,1)S(1)} %bitcast.110), kind=kOutput, calls=%fused_computation.3 | convolution fusion | flops 551550976 | bytes 15761408 | tf_op jit(solution)/shard_map/qhd,khd->hqk/dot_general | solution.py:95
  78.0 3.1 %fusion.8 = bf16[256,16,128]{0,2,1:T(8,128)(2,1)S(1)} fusion(bf16[512,16,128]{2,0,1:T(8,128)(2,1)} %bitcast_dynamic-update-slice_fusion, bf16[16,256,512]{2,1,0:T(8,128)(2,1)S(1)} %fusion.2), kind=kOutput, calls=%fused_computation.27 | convolution fusion | flops 537395200 | bytes 7340032 | tf_op jit(solution)/shard_map/hqk,khd->qhd/dot_general | solution.py:98
  81.1 2.2 %fusion.10 = bf16[256,16,64]{0,2,1:T(8,128)(2,1)} fusion(bf16[16,256,512]{2,1,0:T(8,128)(2,1)S(1)} %fusion.2, bf16[256,64]{0,1:T(8,128)(2,1)S(1)} %slice.52, bf16[256,64]{0,1:T(8,128)(2,1)S(1)} %slice.51), kind=kOutput, calls=%fused_computation.30 | convolution fusion | flops 268828672 | bytes 4784128 | tf_op jit(solution)/shard_map/hqk,kr->qhr/dot_general | solution.py:99
  83.2 0.8 fusion.9
  84.1 0.7 convert_bitcast_fusion.1
  84.8 0.1 slice_reduce_fusion
  84.9 0.1 convert_reduce_fusion.1
  85.0 1.6 %fusion.27 = (bf16[256,16,128]{0,2,1:T(8,128)(2,1)}, bf16[256,16,128]{0,2,1:T(8,128)(2,1)}) fusion(bf16[512,16,128]{0,2,1:T(8,128)(2,1)S(1)} %convert_bitcast_fusion), kind=kLoop, calls=%fused_computation.60 | loop fusion | bytes 4194304 | tf_op jit(solution)/shard_map/slice | solution.py:131
  86.6 0.3 fusion.28
  86.8 1.6 %fusion.33 = f32[256,512]{1,0:T(8,128)} fusion(bf16[256,2048]{0,1:T(8,128)(2,1)S(1)} %bitcast.113, bf16[512,2048]{1,0:T(8,128)(2,1)S(1)} %copy-done), kind=kOutput, calls=%fused_computation.64 | convolution fusion | flops 536870912 | bytes 3670016 | tf_op jit(solution)/shard_map/dot_general | solution.py:117
  88.4 1.6 %fusion.32 = f32[256,512]{1,0:T(8,128)} fusion(bf16[256,2048]{0,1:T(8,128)(2,1)S(1)} %bitcast.112, bf16[512,2048]{1,0:T(8,128)(2,1)S(1)} %copy-done), kind=kOutput, calls=%fused_computation.63 | convolution fusion | flops 536870912 | bytes 3670016 | tf_op jit(solution)/shard_map/dot_general | solution.py:117
  90.0 0.1 copy.55
  90.1 0.1 copy.54
  90.2 2.8 %fusion.11 = bf16[256,512]{1,0:T(8,128)(2,1)S(1)} fusion(f32[256,512]{1,0:T(8,128)} %fusion.33, bf16[256,2048]{0,1:T(8,128)(2,1)} %bitcast.111, bf16[512,2048]{1,0:T(8,128)(2,1)} %param.10), kind=kOutput, calls=%fused_computation.33 | convolution fusion | flops 537133056 | bytes 3932160 | tf_op jit(solution)/shard_map/dot_general | solution.py:122
  93.0 0.0 copy-start.2
  93.1 3.9 %collective-permute-start.1 = (bf16[256,576]{1,0:T(8,128)(2,1)S(1)}, bf16[256,576]{1,0:T(8,128)(2,1)S(1)}, u32[]{:S(2)}, u32[]{:S(2)}) collective-permute-start(bf16[256,576]{1,0:T(8,128)(2,1)S(1)} %pad_maximum_fusion.4), channel_id=1, source_target_pairs={{8,0},{16,8},{24,16},{32,24},{40,32},{48,40},{56,48},{64,56},{72,6... | collective-permute-start | bytes 884744 | tf_op jit(solution)/shard_map/ppermute | solution.py:31
  97.0 1.3 pad_maximum_fusion.1
  98.3 0.8 convolution_add_fusion.1
  99.1 2.5 %collective-permute-done.1 = bf16[256,576]{1,0:T(8,128)(2,1)S(1)} collective-permute-done((bf16[256,576]{1,0:T(8,128)(2,1)S(1)}, bf16[256,576]{1,0:T(8,128)(2,1)S(1)}, u32[]{:S(2)}, u32[]{:S(2)}) %collective-permute-start.1) | collective-permute-done | bytes 294944 | tf_op jit(solution)/shard_map/ppermute | solution.py:31
  101.6 0.1 fusion.15
  101.7 0.9 copy.56
  102.6 7.1 %all-to-all-start.3 = ((bf16[8,256,72]{1,2,0:T(8,128)(2,1)}), bf16[8,256,72]{1,2,0:T(8,128)(2,1)S(1)}, u32[]{:S(2)}, u32[]{:S(2)}) async-start(bf16[8,256,72]{1,2,0:T(8,128)(2,1)} %bitcast.28), calls=%async_computation.3 | async-start | bytes 589824 | tf_op jit(solution)/shard_map/all_to_all | solution.py:42
  109.7 6.8 %convolution_convert_fusion.1 = bf16[256,1536]{1,0:T(8,128)(2,1)S(1)} fusion(bf16[256,3072]{0,1:T(8,128)(2,1)} %bitcast.105, bf16[1536,3072]{1,0:T(8,128)(2,1)} %param.8), kind=kOutput, calls=%fused_computation.11 | convolution fusion | flops 2416312320 | bytes 11796480 | tf_op jit(solution)/shard_map/dot_general | solution.py:105
  116.5 1.2 copy.52
  117.7 1.6 %all-to-all-done.3 = bf16[8,256,72]{1,2,0:T(8,128)(2,1)S(1)} async-done(((bf16[8,256,72]{1,2,0:T(8,128)(2,1)}), bf16[8,256,72]{1,2,0:T(8,128)(2,1)S(1)}, u32[]{:S(2)}, u32[]{:S(2)}) %all-to-all-start.3) | async-done | bytes 294944 | tf_op jit(solution)/shard_map/all_to_all | solution.py:42
  119.3 5.6 %all-to-all-start.2 = ((bf16[8,256,192]{1,2,0:T(8,128)(2,1)}), bf16[8,256,192]{1,2,0:T(8,128)(2,1)S(1)}, u32[]{:S(2)}, u32[]{:S(2)}) async-start(bf16[8,256,192]{1,2,0:T(8,128)(2,1)} %bitcast.19), calls=%async_computation.2 | async-start | bytes 1572864 | tf_op jit(solution)/shard_map/all_to_all | solution.py:42
  124.9 2.3 %copy.57 = bf16[256,2048]{1,0:T(8,128)(2,1)} copy(bf16[256,2048]{0,1:T(8,128)(2,1)} %bitcast.106) | data formatting | bytes 2097152
  127.2 0.7 convert_reduce_fusion.2
  127.8 10.8 %all-to-all-done.2 = bf16[8,256,192]{1,2,0:T(8,128)(2,1)S(1)} async-done(((bf16[8,256,192]{1,2,0:T(8,128)(2,1)}), bf16[8,256,192]{1,2,0:T(8,128)(2,1)S(1)}, u32[]{:S(2)}, u32[]{:S(2)}) %all-to-all-start.2) | async-done | bytes 786464 | tf_op jit(solution)/shard_map/all_to_all | solution.py:42
  138.6 0.8 convert_reduce_fusion
  (26 shorter events, 0.1 us)
Async XLA Ops:
  0.6 30.6 %copy-start = (bf16[512,2048]{1,0:T(8,128)(2,1)S(1)}, bf16[512,2048]{1,0:T(8,128)(2,1)}, u32[]{:S(2)}) copy-start(bf16[512,2048]{1,0:T(8,128)(2,1)} %param.9) | copy-start | bytes 6291460
  0.6 18.5 %copy-start.12 = (bf16[256,192]{0,1:T(8,128)(2,1)S(1)}, bf16[256,192]{0,1:T(8,128)(2,1)}, u32[]{:S(2)}) copy-start(bf16[256,192]{0,1:T(8,128)(2,1)} %param.6) | copy-start | bytes 294916
  2.3 16.8 %all-to-all-start = ((bf16[8,256,72]{1,2,0:T(8,128)(2,1)}), bf16[8,256,72]{1,2,0:T(8,128)(2,1)S(1)}, u32[]{:S(2)}, u32[]{:S(2)}) async-start(bf16[8,256,72]{1,2,0:T(8,128)(2,1)} %broadcast_in_dim.42), calls=%async_computation | async-start | bytes 589824 | tf_op jit(solution)/shard_map/all_to_all | solution.py:21
  20.1 20.1 %all-to-all-start.1 = ((bf16[8,256,192]{1,2,0:T(8,128)(2,1)}), bf16[8,256,192]{1,2,0:T(8,128)(2,1)S(1)}, u32[]{:S(2)}, u32[]{:S(2)}) async-start(bf16[8,256,192]{1,2,0:T(8,128)(2,1)} %broadcast_in_dim.46), calls=%async_computation.1 | async-start | bytes 1572864 | tf_op jit(solution)/shard_map/all_to_all | solution.py:21
  23.7 9.2 %collective-permute-start = (bf16[256,576]{0,1:T(8,128)(2,1)S(1)}, bf16[256,576]{0,1:T(8,128)(2,1)S(1)}, u32[]{:S(2)}, u32[]{:S(2)}) collective-permute-start(bf16[256,576]{0,1:T(8,128)(2,1)S(1)} %bitcast.101), channel_id=1, source_target_pairs={{0,8},{8,16},{16,24},{24,32},{32,40},{40,48},{48,56},{56,64},{64,7... | collective-permute-start | bytes 884744 | tf_op jit(solution)/shard_map/ppermute | solution.py:31
  31.2 1.7 %copy-start.1 = (bf16[512,2048]{1,0:T(8,128)(2,1)S(1)}, bf16[512,2048]{1,0:T(8,128)(2,1)}, u32[]{:S(2)}) copy-start(bf16[512,2048]{1,0:T(8,128)(2,1)} %param.10) | copy-start | bytes 6291460
  36.9 2.1 %copy-start.5 = (bf16[32,16,8,128]{3,2,1,0:T(8,128)(2,1)S(1)}, bf16[32,16,8,128]{3,2,1,0:T(8,128)(2,1)}, u32[]{:S(2)}) copy-start(bf16[32,16,8,128]{3,2,1,0:T(8,128)(2,1)} %fusion.7) | copy-start | bytes 3145732
  50.3 6.5 %copy-start.11 = (pred[256,512]{1,0:T(8,128)(4,1)S(1)}, pred[256,512]{1,0:T(8,128)(4,1)}, u32[]{:S(2)}) copy-start(pred[256,512]{1,0:T(8,128)(4,1)} %fusion.16) | copy-start | bytes 393220
  67.4 3.9 %copy-start.4 = (bf16[256,2048]{0,1:T(8,128)(2,1)S(1)}, bf16[256,2048]{0,1:T(8,128)(2,1)}, u32[]{:S(2)}) copy-start(bf16[256,2048]{0,1:T(8,128)(2,1)} %copy.47) | copy-start | bytes 3145732
  71.4 1.2 copy-start.8
  71.4 1.5 %copy-start.9 = (bf16[256,2048]{0,1:T(8,128)(2,1)S(1)}, bf16[256,2048]{0,1:T(8,128)(2,1)}, u32[]{:S(2)}) copy-start(bf16[256,2048]{0,1:T(8,128)(2,1)} %copy.64) | copy-start | bytes 3145732
  71.4 4.1 %slice-start = ((s8[8388608]{0:T(1024)(128)(4,1)}), s8[4194304]{0:T(1024)(128)(4,1)S(1)}, s32[]{:S(2)}) async-start(s8[8388608]{0:T(1024)(128)(4,1)} %bitcast.95), calls=%async_computation.4 | async-start | bytes 8388608
  72.9 2.7 %slice-start.1 = ((s8[8388608]{0:T(1024)(128)(4,1)}), s8[4194304]{0:T(1024)(128)(4,1)S(1)}, s32[]{:S(2)}) async-start(s8[8388608]{0:T(1024)(128)(4,1)} %bitcast.95), calls=%async_computation.5 | async-start | bytes 8388608
  81.1 2.2 %copy-start.3 = (bf16[256,3072]{0,1:T(8,128)(2,1)S(1)}, bf16[256,3072]{0,1:T(8,128)(2,1)}, u32[]{:S(2)}) copy-start(bf16[256,3072]{0,1:T(8,128)(2,1)} %copy.42) | copy-start | bytes 4718596
  90.2 6.8 %copy-start.7 = (bf16[256,16,64]{0,2,1:T(8,128)(2,1)S(1)}, bf16[256,16,64]{0,2,1:T(8,128)(2,1)}, u32[]{:S(2)}) copy-start(bf16[256,16,64]{0,2,1:T(8,128)(2,1)} %fusion.10) | copy-start | bytes 1572868
  93.0 5.3 %copy-start.2 = (bf16[512,2048]{1,0:T(8,128)(2,1)S(1)}, bf16[512,2048]{1,0:T(8,128)(2,1)}, u32[]{:S(2)}) copy-start(bf16[512,2048]{1,0:T(8,128)(2,1)} %param.10) | copy-start | bytes 6291460
  93.0 5.2 %copy-start.6 = (bf16[256,16,128]{0,2,1:T(8,128)(2,1)S(1)}, bf16[256,16,128]{0,2,1:T(8,128)(2,1)}, u32[]{:S(2)}) copy-start(bf16[256,16,128]{0,2,1:T(8,128)(2,1)} %get-tuple-element.13) | copy-start | bytes 3145732
  93.1 5.2 %copy-start.10 = (f32[256,512]{1,0:T(8,128)S(1)}, f32[256,512]{1,0:T(8,128)}, u32[]{:S(2)}) copy-start(f32[256,512]{1,0:T(8,128)} %fusion.32) | copy-start | bytes 1572868
  93.1 8.5 %collective-permute-start.1 = (bf16[256,576]{1,0:T(8,128)(2,1)S(1)}, bf16[256,576]{1,0:T(8,128)(2,1)S(1)}, u32[]{:S(2)}, u32[]{:S(2)}) collective-permute-start(bf16[256,576]{1,0:T(8,128)(2,1)S(1)} %pad_maximum_fusion.4), channel_id=1, source_target_pairs={{8,0},{16,8},{24,16},{32,24},{40,32},{48,40},{56,48},{64,56},{72,6... | collective-permute-start | bytes 884744 | tf_op jit(solution)/shard_map/ppermute | solution.py:31
  102.6 16.7 %all-to-all-start.3 = ((bf16[8,256,72]{1,2,0:T(8,128)(2,1)}), bf16[8,256,72]{1,2,0:T(8,128)(2,1)S(1)}, u32[]{:S(2)}, u32[]{:S(2)}) async-start(bf16[8,256,72]{1,2,0:T(8,128)(2,1)} %bitcast.28), calls=%async_computation.3 | async-start | bytes 589824 | tf_op jit(solution)/shard_map/all_to_all | solution.py:42
  119.3 19.3 %all-to-all-start.2 = ((bf16[8,256,192]{1,2,0:T(8,128)(2,1)}), bf16[8,256,192]{1,2,0:T(8,128)(2,1)S(1)}, u32[]{:S(2)}, u32[]{:S(2)}) async-start(bf16[8,256,192]{1,2,0:T(8,128)(2,1)} %bitcast.19), calls=%async_computation.2 | async-start | bytes 1572864 | tf_op jit(solution)/shard_map/all_to_all | solution.py:42
where the time goes:
time: 141 us; the launch traced here: 139 us
  matrix products  58 us (41%)
  starting transfers between devices  29.9 us (21%)
  local copies, waits for them, and re-layouts  22 us (16%)
  waiting for transfers between devices  21 us (15%)
  other arithmetic  7.7 us (5%)
    all_to_all x2, starting transfers between devices, sent_and_summed(): blocks = lax.all_to_all(split_up(array, dim, peers), axis, 0, 0, tiled=True)  12.7 us
    all_to_all x2, waiting for transfers between devices, sent_and_summed(): blocks = lax.all_to_all(split_up(array, dim, peers), axis, 0, 0, tiled=True)  12.4 us
    all_to_all x2, starting transfers between devices, sent_to_all(): return lax.all_to_all(copies, axis, split_axis=0, concat_axis=0, tiled=True)  11.3 us
    sub x1, matrix products, on_device(): expons = jnp.where(visible, jnp.exp(scores - maxima), jnp.float32(0.0))  10.6 us
    dot_general x1, matrix products, on_device(): jnp.dot(collect(q_latent, 'head', 1), w_query, preferred_element_type=jnp...  7.47 us
    unnamed x33, local copies, waits for them, and re-layouts  6.84 us
    dot_general x1, matrix products, on_device(): jnp.dot(grad_query, w_query.T, preferred_element_type=jnp.float32)  6.82 us
    dot_general x1, matrix products, on_device(): jnp.einsum('qhd,khd->hqk', query_nope, keys_all, preferred_element_type=j...  6.49 us
  transfers between devices with their start and end apart: 6, of which 4 were waited for; matrix products, arithmetic and copies ran while one was open for 22% of the time, Pallas kernels for 0%

commit v1 on v0

v1 whole, which is shorter than its diff:
```python
import math

import jax
import jax.numpy as jnp
from jax import lax
from jax.experimental import pallas as pl
from jax.experimental.pallas import tpu as pltpu
from jax.sharding import PartitionSpec as P

QL = 1536
KVL = 512
ROPE = 64
NOPE = 128
VDIM = 128
WIDTH = NOPE + ROPE
PAD = 256
HEAD_DEV = 16
TOK = 256
SCALE = WIDTH ** (-0.5)
LOG2E = 1.0 / math.log(2.0)
VMEM_LIMIT = 48 * 1024 * 1024

NN = (((1,), (0,)), ((), ()))
NT = (((1,), (1,)), ((), ()))


def mm(a, b, dims=NN):
    return lax.dot_general(a, b, dims, preferred_element_type=jnp.float32)


def params():
    return pltpu.CompilerParams(vmem_limit_bytes=VMEM_LIMIT)


P_HEADS = 4


def project_kernel(g_ref, kvt_ref, wq_ref, wk_ref, wv_ref, wkt_ref, wvt_ref,
                   q_ref, k_ref, v_ref, kt_ref, vt_ref, qlat, kv):
    @pl.when(pl.program_id(0) == 0)
    def _():
        rows = g_ref[:, : QL // 8, :].reshape(QL, TOK)
        for i in range(QL // 256):
            qlat[:, i * 256 : (i + 1) * 256] = rows[i * 256 : (i + 1) * 256].T
        for i in range(KVL // 256):
            kv[:, i * 256 : (i + 1) * 256] = kvt_ref[i * 256 : (i + 1) * 256, :].T

    queries = mm(qlat[...], wq_ref[...]).astype(jnp.bfloat16)
    zeros = jnp.zeros((TOK, PAD - WIDTH), jnp.bfloat16)
    for h in range(P_HEADS):
        q_ref[:, h * PAD : (h + 1) * PAD] = jnp.concatenate(
            [queries[:, h * WIDTH : (h + 1) * WIDTH], zeros], 1
        )
    k_ref[...] = mm(kv[...], wk_ref[...]).astype(jnp.bfloat16)
    v_ref[...] = mm(kv[...], wv_ref[...]).astype(jnp.bfloat16)
    main = kvt_ref[:KVL, :]
    kt_ref[...] = mm(wkt_ref[...], main).astype(jnp.bfloat16)
    vt_ref[...] = mm(wvt_ref[...], main).astype(jnp.bfloat16)


def project(g, kvt, wq, wk, wv, wkt, wvt):
    n = HEAD_DEV // P_HEADS
    cols = P_HEADS * NOPE
    whole = lambda *shape: pl.BlockSpec(shape, lambda i: (0,) * len(shape))
    shape = jax.ShapeDtypeStruct
    return pl.pallas_call(
        project_kernel,
        grid=(n,),
        in_specs=[
            whole(8, (QL + KVL + ROPE) // 8, TOK),
            whole(KVL + ROPE, TOK),
            pl.BlockSpec((QL, P_HEADS * WIDTH), lambda i: (0, i)),
            pl.BlockSpec((KVL, cols), lambda i: (0, i)),
            pl.BlockSpec((KVL, cols), lambda i: (0, i)),
            pl.BlockSpec((cols, KVL), lambda i: (i, 0)),
            pl.BlockSpec((cols, KVL), lambda i: (i, 0)),
        ],
        out_specs=[
            pl.BlockSpec((TOK, P_HEADS * PAD), lambda i: (0, i)),
            pl.BlockSpec((TOK, cols), lambda i: (0, i)),
            pl.BlockSpec((TOK, cols), lambda i: (0, i)),
            pl.BlockSpec((cols, TOK), lambda i: (i, 0)),
            pl.BlockSpec((cols, TOK), lambda i: (i, 0)),
        ],
        out_shape=[
            shape((TOK, HEAD_DEV * PAD), jnp.bfloat16),
            shape((TOK, HEAD_DEV * NOPE), jnp.bfloat16),
            shape((TOK, HEAD_DEV * VDIM), jnp.bfloat16),
            shape((HEAD_DEV * NOPE, TOK), jnp.bfloat16),
            shape((HEAD_DEV * VDIM, TOK), jnp.bfloat16),
        ],
        scratch_shapes=[
            pltpu.VMEM((TOK, QL), jnp.bfloat16),
            pltpu.VMEM((TOK, KVL), jnp.bfloat16),
        ],
        compiler_params=params(),
        name="project",
    )(g, kvt, wq, wk, wv, wkt, wvt)


A_HEADS = 2


def attend_kernel(lead_ref, kvt_ref, pkvt_ref, q_ref, k_ref, v_ref, kt_ref, vt_ref,
                  dot_ref, wk_ref, wv_ref, wkt_ref, wvt_ref,
                  ot_ref, dqt_ref, dk_ref, dv_ref, early_ref, own_rope_ref,
                  bias, pkv, kx, vx, ktx, vtx, dkp, dvp, acc, rope):
    step = pl.program_id(0)

    @pl.when(step == 0)
    def _():
        key = lax.broadcasted_iota(jnp.int32, (2 * TOK, TOK), 0)
        query = lax.broadcasted_iota(jnp.int32, (2 * TOK, TOK), 1)
        hidden = jnp.where(key < TOK, jnp.where(lead_ref[0] > 0, key + TOK, key - TOK), key - TOK - query)
        bias[...] = jnp.where(hidden > 0, jnp.float32(-1e30), jnp.float32(0.0))
        for i in range(KVL // 256):
            pkv[:, i * 256 : (i + 1) * 256] = pkvt_ref[i * 256 : (i + 1) * 256, :].T
        ropes_t = jnp.concatenate([pkvt_ref[KVL:, :], kvt_ref[KVL:, :]], 1)
        padded = jnp.concatenate([ropes_t, jnp.zeros_like(ropes_t)], 0)
        ropes = padded.T
        for h in range(A_HEADS):
            kx[h, :, NOPE:] = ropes
            ktx[h, NOPE:, :] = ropes_t
        acc[...] = jnp.zeros_like(acc)
        rope[...] = jnp.zeros_like(rope)

    main = pkvt_ref[:KVL, :]
    keys = mm(pkv[...], wk_ref[...]).astype(jnp.bfloat16)
    vals = mm(pkv[...], wv_ref[...]).astype(jnp.bfloat16)
    keys_t = mm(wkt_ref[...], main).astype(jnp.bfloat16)
    vals_t = mm(wvt_ref[...], main).astype(jnp.bfloat16)
    for h in range(A_HEADS):
        at = slice(h * NOPE, (h + 1) * NOPE)
        kx[h, :TOK, :NOPE] = keys[:, at]
        kx[h, TOK:, :NOPE] = k_ref[:, at]
        vx[h, :TOK, :] = vals[:, at]
        vx[h, TOK:, :] = v_ref[:, at]
        ktx[h, :NOPE, :TOK] = keys_t[at, :]
        ktx[h, :NOPE, TOK:] = kt_ref[at, :]
        vtx[h, :, :TOK] = vals_t[at, :]
        vtx[h, :, TOK:] = vt_ref[at, :]

    for h in range(A_HEADS):
        at = slice(h * NOPE, (h + 1) * NOPE)
        q = q_ref[:, h * PAD : (h + 1) * PAD]
        d_out_t = dot_ref[at, :]
        scores = mm(kx[h], q, NT) * (SCALE * LOG2E) + bias[...]
        top = jnp.max(scores, 0, keepdims=True)
        expons = jnp.exp2(scores - top)
        probs = expons * (1.0 / jnp.sum(expons, 0, keepdims=True))
        probs_b = probs.astype(jnp.bfloat16)
        out_t = mm(vtx[h], probs_b).astype(jnp.bfloat16)
        ot_ref[at, :] = out_t
        row_dot = jnp.sum(
            d_out_t.astype(jnp.float32) * out_t.astype(jnp.float32), 0, keepdims=True
        )
        dprob = mm(vx[h], d_out_t)
        dscore = (probs * ((dprob - row_dot) * SCALE)).astype(jnp.bfloat16)
        dqt_ref[h * WIDTH : (h + 1) * WIDTH, :] = mm(ktx[h], dscore).astype(jnp.bfloat16)
        dk = mm(dscore, q).astype(jnp.bfloat16)
        dv = mm(probs_b, d_out_t, NT).astype(jnp.bfloat16)
        dkp[:, at] = dk[:TOK, :NOPE]
        dvp[:, at] = dv[:TOK]
        dk_ref[:, at] = dk[TOK:, :NOPE]
        dv_ref[:, at] = dv[TOK:]
        rope[...] += dk[:, NOPE:].astype(jnp.float32)

    acc[...] += mm(wk_ref[...], dkp[...], NT) + mm(wv_ref[...], dvp[...], NT)

    @pl.when(step == pl.num_programs(0) - 1)
    def _():
        rope_t = rope[...].T
        early_ref[:KVL, :] = acc[...].astype(jnp.bfloat16)
        early_ref[KVL:, :] = rope_t[:ROPE, :TOK].astype(jnp.bfloat16)
        own_rope_ref[...] = rope_t[:ROPE, TOK:]


def attend(lead, kvt, pkvt, q, k, v, kt, vt, d_out_t, wk, wv, wkt, wvt):
    n = HEAD_DEV // A_HEADS
    cols = A_HEADS * NOPE
    whole = lambda *shape: pl.BlockSpec(shape, lambda i: (0,) * len(shape))
    across = lambda rows, width: pl.BlockSpec((rows, width), lambda i: (0, i))
    down = lambda rows, width: pl.BlockSpec((rows, width), lambda i: (i, 0))
    shape = jax.ShapeDtypeStruct
    bf16 = jnp.bfloat16
    return pl.pallas_call(
        attend_kernel,
        grid=(n,),
        in_specs=[
            pl.BlockSpec(memory_space=pltpu.SMEM),
            whole(KVL + ROPE, TOK),
            whole(KVL + ROPE, TOK),
            across(TOK, A_HEADS * PAD),
            across(TOK, cols),
            across(TOK, cols),
            down(cols, TOK),
            down(cols, TOK),
            down(cols, TOK),
            across(KVL, cols),
            across(KVL, cols),
            down(cols, KVL),
            down(cols, KVL),
        ],
        out_specs=[
            down(cols, TOK),
            down(A_HEADS * WIDTH, TOK),
            across(TOK, cols),
            across(TOK, cols),
            whole(KVL + ROPE, TOK),
            whole(ROPE, TOK),
        ],
        out_shape=[
            shape((HEAD_DEV * VDIM, TOK), bf16),
            shape((HEAD_DEV * WIDTH, TOK), bf16),
            shape((TOK, HEAD_DEV * NOPE), bf16),
            shape((TOK, HEAD_DEV * VDIM), bf16),
            shape((KVL + ROPE, TOK), bf16),
            shape((ROPE, TOK), jnp.float32),
        ],
        scratch_shapes=[
            pltpu.VMEM((2 * TOK, TOK), jnp.float32),
            pltpu.VMEM((TOK, KVL), bf16),
            pltpu.VMEM((A_HEADS, 2 * TOK, PAD), bf16),
            pltpu.VMEM((A_HEADS, 2 * TOK, VDIM), bf16),
            pltpu.VMEM((A_HEADS, WIDTH, 2 * TOK), bf16),
            pltpu.VMEM((A_HEADS, VDIM, 2 * TOK), bf16),
            pltpu.VMEM((TOK, cols), bf16),
            pltpu.VMEM((TOK, cols), bf16),
            pltpu.VMEM((KVL, TOK), jnp.float32),
            pltpu.VMEM((2 * TOK, PAD - NOPE), jnp.float32),
        ],
        compiler_params=params(),
        name="attend",
    )(lead, kvt, pkvt, q, k, v, kt, vt, d_out_t, wk, wv, wkt, wvt)


G_STEPS = 4


def gradients_kernel(dqt_ref, dk_ref, dv_ref, wq_ref, wk_ref, wv_ref, gq_ref, gkv_ref):
    gq_ref[...] = mm(wq_ref[...], dqt_ref[...]).astype(jnp.bfloat16)
    gkv_ref[...] = mm(wk_ref[...], dk_ref[...], NT) + mm(wv_ref[...], dv_ref[...], NT)


def gradients(dqt, dk, dv, wq, wk, wv):
    whole = lambda *shape: pl.BlockSpec(shape, lambda i: (0,) * len(shape))
    down = lambda rows, width: pl.BlockSpec((rows // G_STEPS, width), lambda i: (i, 0))
    return pl.pallas_call(
        gradients_kernel,
        grid=(G_STEPS,),
        in_specs=[
            whole(HEAD_DEV * WIDTH, TOK),
            whole(TOK, HEAD_DEV * NOPE),
            whole(TOK, HEAD_DEV * VDIM),
            down(QL, HEAD_DEV * WIDTH),
            down(KVL, HEAD_DEV * NOPE),
            down(KVL, HEAD_DEV * VDIM),
        ],
        out_specs=[down(QL, TOK), down(KVL, TOK)],
        out_shape=[
            jax.ShapeDtypeStruct((QL, TOK), jnp.bfloat16),
            jax.ShapeDtypeStruct((KVL, TOK), jnp.float32),
        ],
        compiler_params=params(),
        name="gradients",
    )(dqt, dk, dv, wq, wk, wv)


def on_device(q_latent, kv_latent, w_query, w_key, w_value, d_out):
    peers = lax.axis_size("head")
    blocks = lax.axis_size("ctx")
    q_cols = q_latent.shape[1]
    own = jnp.concatenate([q_latent.T, kv_latent.T], 0)
    copies = jnp.broadcast_to(own, (peers, *own.shape))
    g = lax.all_to_all(copies, "head", 0, 0, tiled=True)
    kvt = g[:, q_cols:, :].reshape(KVL + ROPE, TOK)
    pkvt = lax.ppermute(kvt, "ctx", [(i, i + 1) for i in range(blocks - 1)])
    wkt, wvt, d_out_t = w_key.T, w_value.T, d_out.T
    q, k, v, kt, vt = project(g, kvt, w_query, w_key, w_value, wkt, wvt)
    lead = (lax.axis_index("ctx") == 0).astype(jnp.int32).reshape(1)
    out_t, dqt, dk, dv, early, own_rope = attend(
        lead, kvt, pkvt, q, k, v, kt, vt, d_out_t, w_key, w_value, wkt, wvt
    )
    later = lax.ppermute(early, "ctx", [(i, i - 1) for i in range(1, blocks)])
    gq, gkv = gradients(dqt, dk, dv, w_query, w_key, w_value)
    own_kv = jnp.concatenate([gkv, own_rope], 0)
    gkv = (own_kv + later.astype(jnp.float32)).astype(jnp.bfloat16)
    terms = jnp.concatenate(
        [gq.reshape(peers, q_cols, TOK), gkv.reshape(peers, -1, TOK)], 1
    )
    terms = lax.all_to_all(terms, "head", 0, 0, tiled=True)
    sums = jnp.sum(terms.astype(jnp.float32), 0)
    return out_t.T, sums[:q_cols].T, sums[q_cols:].T


def solution(mesh):
    return jax.shard_map(
        on_device,
        mesh=mesh,
        in_specs=(
            P("ctx", "head"),
            P("ctx", "head"),
            P(None, "head"),
            P(None, "head"),
            P(None, "head"),
            P("ctx", "head"),
        ),
        out_specs=(P("ctx", "head"), P("ctx", "head"), P("ctx", "head")),
        check_vma=False,
    )
```

time: 141 us -> 109 us (0.77); the launches traced: 139 us -> 109 us
  matrix products: 58 us -> 0 us
  Pallas kernels: 0 us -> 41.3 us
  blocking collectives: 0 us -> 25.3 us
  starting transfers between devices: 29.9 us -> 9.11 us
  local copies, waits for them, and re-layouts: 22 us -> 15.4 us
  waiting for transfers between devices: 21 us -> 14.7 us
  other arithmetic: 7.7 us -> 2.28 us
    dot_general x18 -> x0, matrix products: 47.4 us -> none  [the longest x1 7.47 us: on_device(): jnp.dot(collect(q_latent, 'head', 1), w_query, preferred_element_type=jnp...]
    pallas_call x0 -> x3, Pallas kernels: none -> 41.3 us  [the longest x1 23.4 us: attend(): pl.pallas_call(attend_kernel, grid=(n,), in_specs=[pl.BlockSpec(memory_sp...]
    all_to_all x0 -> x1, blocking collectives: none -> 25.3 us  [on_device(): g = lax.all_to_all(copies, 'head', 0, 0, tiled=True)]
    all_to_all x4 -> x1, starting transfers between devices: 24 us -> 3.56 us  [on_device(): terms = lax.all_to_all(terms, 'head', 0, 0, tiled=True)]
    sub x1 -> x0, matrix products: 10.6 us -> none  [on_device(): expons = jnp.where(visible, jnp.exp(scores - maxima), jnp.float32(0.0))]
    unnamed x33 -> x12, local copies, waits for them, and re-layouts: 6.84 us -> 14 us
    convert_element_type x3 -> x0, local copies, waits for them, and re-layouts: 4.62 us -> none  [the longest x1 2.59 us: on_device(): queries = queries.astype(jnp.bfloat16).reshape(block_rows, per_dev, width)]
    reshape x2 -> x0, local copies, waits for them, and re-layouts: 4.57 us -> none  [expand(): values.reshape(block_rows, per_dev, VDIM)]
  transfers between devices with their start and end apart: 6 -> 3, of which waited for: 4 -> 1; matrix products, arithmetic and copies ran while one was open for 22% -> 10% of each run, Pallas kernels for 0% -> 16%
where the time goes in v1:
time: 109 us
  Pallas kernels  41.3 us (38%)
  blocking collectives  25.3 us (23%)
  local copies, waits for them, and re-layouts  15.4 us (14%)
  waiting for transfers between devices  14.7 us (13%)
  starting transfers between devices  9.11 us (8%)
  other arithmetic  2.28 us (2%)
    all_to_all x1, blocking collectives, on_device(): g = lax.all_to_all(copies, 'head', 0, 0, tiled=True)  25.3 us
    pallas_call x1, Pallas kernels, attend(): pl.pallas_call(attend_kernel, grid=(n,), in_specs=[pl.BlockSpec(memory_sp...  23.4 us
    all_to_all x1, waiting for transfers between devices, on_device(): terms = lax.all_to_all(terms, 'head', 0, 0, tiled=True)  14.7 us
    unnamed x12, local copies, waits for them, and re-layouts  14 us
    pallas_call x1, Pallas kernels, project(): pl.pallas_call(project_kernel, grid=(n,), in_specs=[whole(8, (QL + KVL +...  9.89 us
    pallas_call x1, Pallas kernels, gradients(): pl.pallas_call(gradients_kernel, grid=(G_STEPS,), in_specs=[whole(HEAD_DE...  8.05 us
    ppermute x1, starting transfers between devices, on_device(): later = lax.ppermute(early, 'ctx', [(i, i - 1) for i in range(1, blocks)])  3.63 us
    all_to_all x1, starting transfers between devices, on_device(): terms = lax.all_to_all(terms, 'head', 0, 0, tiled=True)  3.56 us
  transfers between devices with their start and end apart: 3, of which 1 were waited for; matrix products, arithmetic and copies ran while one was open for 10% of the time, Pallas kernels for 16%

profile of v1, /device:TPU:16, one launch (start us, length us, event | category | flops | bytes accessed | tf_op | source)
XLA Modules:
  0.0 108.9 jit_solution(15899595178379960628)
XLA Ops:
  0.6 0.0 copy-start.3
  0.6 1.0 pad_maximum_fusion.1
  1.7 0.1 broadcast_in_dim.3
  1.7 25.3 %all_to_all.10.g_ref = bf16[8,264,256]{2,1,0:T(8,128)(2,1)S(1)} all-to-all(bf16[8,264,256]{2,1,0:T(8,128)(2,1)S(1)} %broadcast_in_dim.3), channel_id=1, replica_groups=mesh['ctx'=16,'head'=8] {'head'}, dimensions={0} | all-to-all | bytes 2162688 | tf_op jit(solution)/shard_map/all_to_all | solution.py:275
  27.1 1.9 %collective-permute-start = (bf16[576,256]{1,0:T(8,128)(2,1)S(1)}, bf16[576,256]{1,0:T(8,128)(2,1)S(1)}, u32[]{:S(2)}, u32[]{:S(2)}) collective-permute-start(bf16[576,256]{1,0:T(8,128)(2,1)S(1)} %bitcast.14), channel_id=1, source_target_pairs={{0,8},{8,16},{16,24},{24,32},{32,40},{40,48},{48,56},{56,64},{64,7... | collective-permute-start | bytes 884744 | tf_op jit(solution)/shard_map/ppermute | solution.py:277
  29.0 0.0 copy-done.3
  29.0 1.3 %copy.11 = bf16[256,2048]{0,1:T(8,128)(2,1)} copy(bf16[256,2048]{1,0:T(8,128)(2,1)S(1)} %copy-done.3) | data formatting | bytes 2097152 | tf_op args[5]
  30.3 3.9 %copy.9 = bf16[512,2048]{0,1:T(8,128)(2,1)} copy(bf16[512,2048]{1,0:T(8,128)(2,1)} %wk_ref.5) | data formatting | bytes 4194304 | tf_op args[3]
  34.3 3.9 %copy.10 = bf16[512,2048]{0,1:T(8,128)(2,1)} copy(bf16[512,2048]{1,0:T(8,128)(2,1)} %wv_ref.5) | data formatting | bytes 4194304 | tf_op args[4]
  38.2 9.9 %project.1 = (bf16[256,4096]{1,0:T(8,128)(2,1)}, bf16[256,2048]{1,0:T(8,128)(2,1)S(1)}, bf16[256,2048]{1,0:T(8,128)(2,1)S(1)}, bf16[2048,256]{1,0:T(8,128)(2,1)S(1)}, bf16[2048,256]{1,0:T(8,128)(2,1)S(1)}) custom-call(bf16[8,264,256]{2,1,0:T(8,128)(2,1)S(1)} %all_to_all.10.g_ref, bf16[576,256]{1,0:T(8,128)(2,1)S(1)} %bitcast.15, bf16[1536,3072]{1,0:T(8,128)(2,1)} %wq_ref.3, ...), custom_call_target="tpu_custom_call" | custom-call | tf_op jit(solution)/shard_map/project/pallas_call | solution.py:66
  48.1 0.0 copy-start.1
  48.1 1.0 copy-done.1
  49.0 0.0 copy-start.2
  49.0 1.1 copy-done.2
  50.1 0.0 collective-permute-done.pkvt_ref
  50.1 23.4 %attend.1 = (bf16[2048,256]{1,0:T(8,128)(2,1)S(1)}, bf16[3072,256]{1,0:T(8,128)(2,1)}, bf16[256,2048]{1,0:T(8,128)(2,1)S(1)}, bf16[256,2048]{1,0:T(8,128)(2,1)S(...) custom-call(s32[1]{0:T(128)} %bitcast.lead_ref, bf16[576,256]{1,0:T(8,128)(2,1)S(1)} %bitcast.16, ...), custom_call_target="tpu_custom_call" | custom-call | tf_op jit(solution)/shard_map/attend/pallas_call | solution.py:186
  73.5 3.6 %collective-permute-start.1 = (bf16[576,256]{1,0:T(8,128)(2,1)S(1)}, bf16[576,256]{1,0:T(8,128)(2,1)S(1)}, u32[]{:S(2)}, u32[]{:S(2)}) collective-permute-start(bf16[576,256]{1,0:T(8,128)(2,1)S(1)} %get-tuple-element.28), channel_id=1, source_target_pairs={{8,0},{16,8},{24,16},{32,24},{40,32},{48,40},{56,48},{64,56},{72,6... | collective-permute-start | bytes 884744 | tf_op jit(solution)/shard_map/ppermute | solution.py:284
  77.2 0.0 copy-start
  77.2 1.4 %copy-done = bf16[3072,256]{1,0:T(8,128)(2,1)S(1)} copy-done((bf16[3072,256]{1,0:T(8,128)(2,1)S(1)}, bf16[3072,256]{1,0:T(8,128)(2,1)}, u32[]{:S(2)}) %copy-start) | copy-done | bytes 1572888
  78.6 8.1 %gradients.1 = (bf16[1536,256]{1,0:T(8,128)(2,1)S(1)}, f32[512,256]{1,0:T(8,128)S(1)}) custom-call(bf16[3072,256]{1,0:T(8,128)(2,1)S(1)} %copy-done, bf16[256,2048]{1,0:T(8,128)(2,1)S(1)} %get-tuple-element.23.dk_ref, bf16[256,2048]{1,0:T(8,128)(2,1)S(1)} %get-tuple-element.24.dv_ref, bf16[1536,3072]{1,0:T(8,128)(2,1)} %wq_ref.3, bf16[512,2048]{1,0:T(8,128)(2,1)} %wk_ref.5, ...), custom_call_target="tpu_custom_call" | custom-call | tf_op jit(solution)/shard_map/gradients/pallas_call | solution.py:248
  86.6 0.0 collective-permute-done.1
  86.6 0.1 fusion
  86.7 1.1 pad_maximum_fusion
  87.8 3.6 %all-to-all-start.1 = ((bf16[8,264,256]{2,1,0:T(8,128)(2,1)}), bf16[8,264,256]{2,1,0:T(8,128)(2,1)S(1)}, u32[]{:S(2)}, u32[]{:S(2)}) async-start(bf16[8,264,256]{2,1,0:T(8,128)(2,1)} %pad_maximum_fusion), calls=%async_computation.1 | async-start | bytes 2162688 | tf_op jit(solution)/shard_map/all_to_all | solution.py:291
  91.3 1.4 %copy.12 = bf16[256,2048]{1,0:T(8,128)(2,1)} copy(bf16[256,2048]{0,1:T(8,128)(2,1)S(1)} %bitcast.17) | data formatting | bytes 2097152
  92.8 14.7 %all-to-all-done.1 = bf16[8,264,256]{2,1,0:T(8,128)(2,1)S(1)} async-done(((bf16[8,264,256]{2,1,0:T(8,128)(2,1)}), bf16[8,264,256]{2,1,0:T(8,128)(2,1)S(1)}, u32[]{:S(2)}, u32[]{:S(2)}) %all-to-all-start.1) | async-done | bytes 1081376 | tf_op jit(solution)/shard_map/all_to_all | solution.py:291
  107.4 0.1 convert_reduce_fusion
  107.6 0.6 slice_bitcast_fusion.1
  108.2 0.7 slice_bitcast_fusion
  (1 shorter events, 0.0 us)
Async XLA Ops:
  0.6 28.4 %copy-start.3 = (bf16[256,2048]{1,0:T(8,128)(2,1)S(1)}, bf16[256,2048]{1,0:T(8,128)(2,1)}, u32[]{:S(2)}) copy-start(bf16[256,2048]{1,0:T(8,128)(2,1)} %param.11) | copy-start | bytes 3145732
  27.1 23.0 %collective-permute-start = (bf16[576,256]{1,0:T(8,128)(2,1)S(1)}, bf16[576,256]{1,0:T(8,128)(2,1)S(1)}, u32[]{:S(2)}, u32[]{:S(2)}) collective-permute-start(bf16[576,256]{1,0:T(8,128)(2,1)S(1)} %bitcast.14), channel_id=1, source_target_pairs={{0,8},{8,16},{16,24},{24,32},{32,40},{40,48},{48,56},{56,64},{64,7... | collective-permute-start | bytes 884744 | tf_op jit(solution)/shard_map/ppermute | solution.py:277
  48.1 1.0 copy-start.1
  49.0 1.1 copy-start.2
  73.5 13.1 %collective-permute-start.1 = (bf16[576,256]{1,0:T(8,128)(2,1)S(1)}, bf16[576,256]{1,0:T(8,128)(2,1)S(1)}, u32[]{:S(2)}, u32[]{:S(2)}) collective-permute-start(bf16[576,256]{1,0:T(8,128)(2,1)S(1)} %get-tuple-element.28), channel_id=1, source_target_pairs={{8,0},{16,8},{24,16},{32,24},{40,32},{48,40},{56,48},{64,56},{72,6... | collective-permute-start | bytes 884744 | tf_op jit(solution)/shard_map/ppermute | solution.py:284
  77.2 1.4 %copy-start = (bf16[3072,256]{1,0:T(8,128)(2,1)S(1)}, bf16[3072,256]{1,0:T(8,128)(2,1)}, u32[]{:S(2)}) copy-start(bf16[3072,256]{1,0:T(8,128)(2,1)} %get-tuple-element.22.dqt_ref) | copy-start | bytes 4718596
  87.8 19.7 %all-to-all-start.1 = ((bf16[8,264,256]{2,1,0:T(8,128)(2,1)}), bf16[8,264,256]{2,1,0:T(8,128)(2,1)S(1)}, u32[]{:S(2)}, u32[]{:S(2)}) async-start(bf16[8,264,256]{2,1,0:T(8,128)(2,1)} %pad_maximum_fusion), calls=%async_computation.1 | async-start | bytes 2162688 | tf_op jit(solution)/shard_map/all_to_all | solution.py:291

commit v2 on v1

--- a/solution.py
+++ b/solution.py
@@ -18,7 +18,7 @@
 TOK = 256
 SCALE = WIDTH ** (-0.5)
 LOG2E = 1.0 / math.log(2.0)
-VMEM_LIMIT = 48 * 1024 * 1024
+MIB = 1024 * 1024
 
 NN = (((1,), (0,)), ((), ()))
 NT = (((1,), (1,)), ((), ()))
@@ -28,8 +28,8 @@
     return lax.dot_general(a, b, dims, preferred_element_type=jnp.float32)
 
 
-def params():
-    return pltpu.CompilerParams(vmem_limit_bytes=VMEM_LIMIT)
+def params(mib):
+    return pltpu.CompilerParams(vmem_limit_bytes=mib * MIB)
 
 
 P_HEADS = 4
@@ -93,7 +93,7 @@
             pltpu.VMEM((TOK, QL), jnp.bfloat16),
             pltpu.VMEM((TOK, KVL), jnp.bfloat16),
         ],
-        compiler_params=params(),
+        compiler_params=params(24),
         name="project",
     )(g, kvt, wq, wk, wv, wkt, wvt)
 
@@ -229,7 +229,7 @@
             pltpu.VMEM((KVL, TOK), jnp.float32),
             pltpu.VMEM((2 * TOK, PAD - NOPE), jnp.float32),
         ],
-        compiler_params=params(),
+        compiler_params=params(20),
         name="attend",
     )(lead, kvt, pkvt, q, k, v, kt, vt, d_out_t, wk, wv, wkt, wvt)
 
@@ -261,7 +261,7 @@
             jax.ShapeDtypeStruct((QL, TOK), jnp.bfloat16),
             jax.ShapeDtypeStruct((KVL, TOK), jnp.float32),
         ],
-        compiler_params=params(),
+        compiler_params=params(20),
         name="gradients",
     )(dqt, dk, dv, wq, wk, wv)
 
@@ -273,9 +273,10 @@
     own = jnp.concatenate([q_latent.T, kv_latent.T], 0)
     copies = jnp.broadcast_to(own, (peers, *own.shape))
     g = lax.all_to_all(copies, "head", 0, 0, tiled=True)
+    wkt, wvt, d_out_t = w_key.T, w_value.T, d_out.T
+    g, wkt, wvt, d_out_t = lax.optimization_barrier((g, wkt, wvt, d_out_t))
     kvt = g[:, q_cols:, :].reshape(KVL + ROPE, TOK)
     pkvt = lax.ppermute(kvt, "ctx", [(i, i + 1) for i in range(blocks - 1)])
-    wkt, wvt, d_out_t = w_key.T, w_value.T, d_out.T
     q, k, v, kt, vt = project(g, kvt, w_query, w_key, w_value, wkt, wvt)
     lead = (lax.axis_index("ctx") == 0).astype(jnp.int32).reshape(1)
     out_t, dqt, dk, dv, early, own_rope = attend(

time: 109 us -> 103 us (0.945); the launches traced: 109 us -> 101 us
  blocking collectives: 25.3 us -> 0 us
  starting transfers between devices: 9.11 us -> 17.6 us
  local copies, waits for them, and re-layouts: 15.4 us -> 23.2 us
  waiting for transfers between devices: 14.7 us -> 22.1 us
  Pallas kernels: 41.3 us -> 35.3 us
    all_to_all x1 -> x0, blocking collectives: 25.3 us -> none  [on_device(): g = lax.all_to_all(copies, 'head', 0, 0, tiled=True)]
    all_to_all x0 -> x1, starting transfers between devices: none -> 7.91 us  [on_device(): g = lax.all_to_all(copies, 'head', 0, 0, tiled=True)]
    all_to_all x0 -> x1, waiting for transfers between devices: none -> 7.44 us  [on_device(): g = lax.all_to_all(copies, 'head', 0, 0, tiled=True)]
    unnamed x12 -> x32, local copies, waits for them, and re-layouts: 14 us -> 20.8 us
    pallas_call x1, Pallas kernels: 9.89 us -> 6.97 us  [project(): pl.pallas_call(project_kernel, grid=(n,), in_specs=[whole(8, (QL + KVL +...]
    pallas_call x1, Pallas kernels: 8.05 us -> 5.43 us  [gradients(): pl.pallas_call(gradients_kernel, grid=(G_STEPS,), in_specs=[whole(HEAD_DE...]
  transfers between devices with their start and end apart: 3 -> 4, of which waited for: 1 -> 2; matrix products, arithmetic and copies ran while one was open for 10% -> 10% of each run, Pallas kernels for 16% -> 12%
where the time goes in v2:
time: 103 us; the launch traced here: 101 us
  Pallas kernels  35.3 us (34%)
  local copies, waits for them, and re-layouts  23.2 us (23%)
  waiting for transfers between devices  22.1 us (21%)
  starting transfers between devices  17.6 us (17%)
  other arithmetic  2.23 us (2%)
    pallas_call x1, Pallas kernels, attend(): pl.pallas_call(attend_kernel, grid=(n,), in_specs=[pl.BlockSpec(memory_sp...  22.9 us
    unnamed x32, local copies, waits for them, and re-layouts  20.8 us
    all_to_all x1, waiting for transfers between devices, on_device(): terms = lax.all_to_all(terms, 'head', 0, 0, tiled=True)  14.7 us
    all_to_all x1, starting transfers between devices, on_device(): g = lax.all_to_all(copies, 'head', 0, 0, tiled=True)  7.91 us
    all_to_all x1, waiting for transfers between devices, on_device(): g = lax.all_to_all(copies, 'head', 0, 0, tiled=True)  7.44 us
    pallas_call x1, Pallas kernels, project(): pl.pallas_call(project_kernel, grid=(n,), in_specs=[whole(8, (QL + KVL +...  6.97 us
    pallas_call x1, Pallas kernels, gradients(): pl.pallas_call(gradients_kernel, grid=(G_STEPS,), in_specs=[whole(HEAD_DE...  5.43 us
    all_to_all x1, starting transfers between devices, on_device(): terms = lax.all_to_all(terms, 'head', 0, 0, tiled=True)  4.09 us
  transfers between devices with their start and end apart: 4, of which 2 were waited for; matrix products, arithmetic and copies ran while one was open for 10% of the time, Pallas kernels for 12%

profile of v2, /device:TPU:16, one launch (start us, length us, event | category | flops | bytes accessed | tf_op | source)
XLA Modules:
  0.0 101.3 jit_solution(10369556431613007975)
XLA Ops:
  0.6 0.9 pad_maximum_fusion.1
  1.6 1.1 %broadcast_in_dim.3 = bf16[8,264,256]{2,1,0:T(8,128)(2,1)} broadcast(bf16[264,256]{1,0:T(8,128)(2,1)S(1)} %pad_maximum_fusion.1), dimensions={1,2} | broadcast | bytes 1216512 | tf_op jit(solution)/shard_map/broadcast_in_dim | solution.py:274
  2.6 0.0 copy-start.1
  2.6 7.9 %all-to-all-start = ((bf16[8,264,256]{2,1,0:T(8,128)(2,1)}), bf16[8,264,256]{2,1,0:T(8,128)(2,1)S(1)}, u32[]{:S(2)}, u32[]{:S(2)}) async-start(bf16[8,264,256]{2,1,0:T(8,128)(2,1)} %broadcast_in_dim.3), calls=%async_computation | async-start | bytes 2162688 | tf_op jit(solution)/shard_map/all_to_all | solution.py:275
  10.6 2.3 %copy.11 = bf16[256,2048]{0,1:T(8,128)(2,1)} copy(bf16[256,2048]{1,0:T(8,128)(2,1)} %param.11) | data formatting | bytes 2097152 | tf_op args[5]
  12.8 0.0 copy-done.1
  12.8 2.5 %copy.9 = bf16[512,2048]{0,1:T(8,128)(2,1)} copy(bf16[512,2048]{1,0:T(8,128)(2,1)S(1)} %copy-done.1) | data formatting | bytes 4194304 | tf_op args[3]
  15.3 3.9 %copy.10 = bf16[512,2048]{0,1:T(8,128)(2,1)} copy(bf16[512,2048]{1,0:T(8,128)(2,1)} %wv_ref.5) | data formatting | bytes 4194304 | tf_op args[4]
  19.3 7.4 %all-to-all-done.g_ref = bf16[8,264,256]{2,1,0:T(8,128)(2,1)S(1)} async-done(((bf16[8,264,256]{2,1,0:T(8,128)(2,1)}), bf16[8,264,256]{2,1,0:T(8,128)(2,1)S(1)}, u32[]{:S(2)}, u32[]{:S(2)}) %all-to-all-start) | async-done | bytes 1081376 | tf_op jit(solution)/shard_map/all_to_all | solution.py:275
  26.7 1.9 %collective-permute-start = (bf16[576,256]{1,0:T(8,128)(2,1)S(1)}, bf16[576,256]{1,0:T(8,128)(2,1)}, u32[]{:S(2)}, u32[]{:S(2)}) collective-permute-start(bf16[576,256]{1,0:T(8,128)(2,1)S(1)} %bitcast.21), channel_id=1, source_target_pairs={{0,8},{8,16},{16,24},{24,32},{32,40},{40,48},{48,56},{56,64},{64,7... | collective-permute-start | bytes 884744 | tf_op jit(solution)/shard_map/ppermute | solution.py:279
  28.7 0.0 copy-start
  28.7 3.7 %copy-done = bf16[1536,3072]{1,0:T(8,128)(2,1)S(1)} copy-done((bf16[1536,3072]{1,0:T(8,128)(2,1)S(1)}, bf16[1536,3072]{1,0:T(8,128)(2,1)}, u32[]{:S(2)}) %copy-start) | copy-done | bytes 9437208
  32.3 0.0 copy-start.2
  32.4 1.6 %copy-done.2 = bf16[512,2048]{1,0:T(8,128)(2,1)S(1)} copy-done((bf16[512,2048]{1,0:T(8,128)(2,1)S(1)}, bf16[512,2048]{1,0:T(8,128)(2,1)}, u32[]{:S(2)}) %copy-start.2) | copy-done | bytes 2097176
  33.9 0.0 copy-start.4
  33.9 1.6 %copy-done.4 = bf16[512,2048]{0,1:T(8,128)(2,1)S(1)} copy-done((bf16[512,2048]{0,1:T(8,128)(2,1)S(1)}, bf16[512,2048]{0,1:T(8,128)(2,1)}, u32[]{:S(2)}) %copy-start.4) | copy-done | bytes 2097176
  35.5 0.0 copy-start.6
  35.5 1.6 %copy-done.6 = bf16[512,2048]{0,1:T(8,128)(2,1)S(1)} copy-done((bf16[512,2048]{0,1:T(8,128)(2,1)S(1)}, bf16[512,2048]{0,1:T(8,128)(2,1)}, u32[]{:S(2)}) %copy-start.6) | copy-done | bytes 2097176
  37.1 0.0 copy-start.3
  37.1 0.0 copy-start.5
  37.1 0.0 copy-start.7
  37.1 0.0 copy-start.8
  37.1 0.0 slice-start
  37.1 0.0 slice-start.1
  37.2 7.0 %project.1 = (bf16[256,4096]{1,0:T(8,128)(2,1)S(1)}, bf16[256,2048]{1,0:T(8,128)(2,1)S(1)}, bf16[256,2048]{1,0:T(8,128)(2,1)S(1)}, bf16[2048,256]{1,0:T(8,128)(2,1)S(1)}, bf16[2048,256]{1,0:T(8,128)(2,1)S(1)}) custom-call(bf16[8,264,256]{2,1,0:T(8,128)(2,1)S(1)} %all-to-all-done.g_ref, bf16[576,256]{1,0:T(8,128)(2,1)S(1)} %bitcast.22, ...), custom_call_target="tpu_custom_call" | custom-call | tf_op jit(solution)/shard_map/project/pallas_call | solution.py:66
  44.1 0.0 copy-start.9
  44.1 1.0 copy-done.9
  45.1 0.0 collective-permute-done.pkvt_ref
  45.1 0.0 copy-done.3
  45.1 0.0 copy-done.5
  45.1 0.0 copy-done.7
  45.1 0.0 copy-done.8
  45.1 0.0 copy-start.10
  45.2 1.2 %copy-done.10 = bf16[256,2048]{1,0:T(8,128)(2,1)S(1)} copy-done((bf16[256,2048]{1,0:T(8,128)(2,1)S(1)}, bf16[256,2048]{1,0:T(8,128)(2,1)}, u32[]{:S(2)}) %copy-start.10) | copy-done | bytes 1048600
  46.4 0.0 slice-start.2
  46.4 22.9 %attend.1 = (bf16[2048,256]{1,0:T(8,128)(2,1)S(1)}, bf16[3072,256]{1,0:T(8,128)(2,1)S(1)}, bf16[256,2048]{1,0:T(8,128)(2,1)S(1)}, bf16[256,2048]{1,0:T(8,128)(2,...) custom-call(s32[1]{0:T(128)} %bitcast.lead_ref, bf16[576,256]{1,0:T(8,128)(2,1)S(1)} %bitcast.23, ...), custom_call_target="tpu_custom_call" | custom-call | tf_op jit(solution)/shard_map/attend/pallas_call | solution.py:186
  69.3 3.6 %collective-permute-start.1 = (bf16[576,256]{1,0:T(8,128)(2,1)S(1)}, bf16[576,256]{1,0:T(8,128)(2,1)S(1)}, u32[]{:S(2)}, u32[]{:S(2)}) collective-permute-start(bf16[576,256]{1,0:T(8,128)(2,1)S(1)} %get-tuple-element.36), channel_id=1, source_target_pairs={{8,0},{16,8},{24,16},{32,24},{40,32},{48,40},{56,48},{64,56},{72,6... | collective-permute-start | bytes 884744 | tf_op jit(solution)/shard_map/ppermute | solution.py:285
  73.0 0.0 slice-done
  73.0 0.0 slice-done.1
  73.0 0.0 slice-done.2
  73.0 5.4 %gradients.1 = (bf16[1536,256]{1,0:T(8,128)(2,1)S(1)}, f32[512,256]{1,0:T(8,128)S(1)}) custom-call(bf16[3072,256]{1,0:T(8,128)(2,1)S(1)} %get-tuple-element.30.dqt_ref, bf16[256,2048]{1,0:T(8,128)(2,1)S(1)} %get-tuple-element.31.dk_ref, bf16[256,2048]{1,0:T(8,128)(2,1)S(1)} %get-tuple-element.32.dv_ref, bf16[1536,3072]{1,0:T(8,128)(2,1)S(1)} %bitcast.15, ...), custom_call_target="tpu_custom_call" | custom-call | tf_op jit(solution)/shard_map/gradients/pallas_call | solution.py:248
  78.4 0.0 collective-permute-done.1
  78.5 0.1 fusion
  78.5 1.1 %pad_maximum_fusion = bf16[8,264,256]{2,1,0:T(8,128)(2,1)} fusion(bf16[8,72,256]{2,1,0:T(8,128)(2,1)S(1)} %bitcast.26, bf16[8,192,256]{2,1,0:T(8,128)(2,1)S(1)} %bitcast.25), kind=kLoop, calls=%fused_computation.1 | loop fusion | flops 2162688 | bytes 2162688 | tf_op jit(solution)/shard_map/concatenate | solution.py:289
  79.6 4.1 %all-to-all-start.1 = ((bf16[8,264,256]{2,1,0:T(8,128)(2,1)}), bf16[8,264,256]{2,1,0:T(8,128)(2,1)S(1)}, u32[]{:S(2)}, u32[]{:S(2)}) async-start(bf16[8,264,256]{2,1,0:T(8,128)(2,1)} %pad_maximum_fusion), calls=%async_computation.1 | async-start | bytes 2162688 | tf_op jit(solution)/shard_map/all_to_all | solution.py:292
  83.7 1.4 %copy.12 = bf16[256,2048]{1,0:T(8,128)(2,1)} copy(bf16[256,2048]{0,1:T(8,128)(2,1)S(1)} %bitcast.24) | data formatting | bytes 2097152
  85.1 14.7 %all-to-all-done.1 = bf16[8,264,256]{2,1,0:T(8,128)(2,1)S(1)} async-done(((bf16[8,264,256]{2,1,0:T(8,128)(2,1)}), bf16[8,264,256]{2,1,0:T(8,128)(2,1)S(1)}, u32[]{:S(2)}, u32[]{:S(2)}) %all-to-all-start.1) | async-done | bytes 1081376 | tf_op jit(solution)/shard_map/all_to_all | solution.py:292
  99.8 0.1 convert_reduce_fusion
  100.0 0.6 slice_bitcast_fusion.1
  100.6 0.7 slice_bitcast_fusion
  (2 shorter events, 0.0 us)
Async XLA Ops:
  2.6 10.2 %copy-start.1 = (bf16[512,2048]{1,0:T(8,128)(2,1)S(1)}, bf16[512,2048]{1,0:T(8,128)(2,1)}, u32[]{:S(2)}) copy-start(bf16[512,2048]{1,0:T(8,128)(2,1)} %wk_ref.5) | copy-start | bytes 6291460
  2.6 24.1 %all-to-all-start = ((bf16[8,264,256]{2,1,0:T(8,128)(2,1)}), bf16[8,264,256]{2,1,0:T(8,128)(2,1)S(1)}, u32[]{:S(2)}, u32[]{:S(2)}) async-start(bf16[8,264,256]{2,1,0:T(8,128)(2,1)} %broadcast_in_dim.3), calls=%async_computation | async-start | bytes 2162688 | tf_op jit(solution)/shard_map/all_to_all | solution.py:275
  26.7 18.4 %collective-permute-start = (bf16[576,256]{1,0:T(8,128)(2,1)S(1)}, bf16[576,256]{1,0:T(8,128)(2,1)}, u32[]{:S(2)}, u32[]{:S(2)}) collective-permute-start(bf16[576,256]{1,0:T(8,128)(2,1)S(1)} %bitcast.21), channel_id=1, source_target_pairs={{0,8},{8,16},{16,24},{24,32},{32,40},{40,48},{48,56},{56,64},{64,7... | collective-permute-start | bytes 884744 | tf_op jit(solution)/shard_map/ppermute | solution.py:279
  28.7 3.7 %copy-start = (bf16[1536,3072]{1,0:T(8,128)(2,1)S(1)}, bf16[1536,3072]{1,0:T(8,128)(2,1)}, u32[]{:S(2)}) copy-start(bf16[1536,3072]{1,0:T(8,128)(2,1)} %wq_ref.3) | copy-start | bytes 28311556
  32.3 1.6 %copy-start.2 = (bf16[512,2048]{1,0:T(8,128)(2,1)S(1)}, bf16[512,2048]{1,0:T(8,128)(2,1)}, u32[]{:S(2)}) copy-start(bf16[512,2048]{1,0:T(8,128)(2,1)} %wv_ref.5) | copy-start | bytes 6291460
  33.9 1.6 %copy-start.4 = (bf16[512,2048]{0,1:T(8,128)(2,1)S(1)}, bf16[512,2048]{0,1:T(8,128)(2,1)}, u32[]{:S(2)}) copy-start(bf16[512,2048]{0,1:T(8,128)(2,1)} %copy.9) | copy-start | bytes 6291460
  35.5 1.6 %copy-start.6 = (bf16[512,2048]{0,1:T(8,128)(2,1)S(1)}, bf16[512,2048]{0,1:T(8,128)(2,1)}, u32[]{:S(2)}) copy-start(bf16[512,2048]{0,1:T(8,128)(2,1)} %copy.10) | copy-start | bytes 6291460
  37.1 8.0 %copy-start.3 = (bf16[512,2048]{1,0:T(8,128)(2,1)S(1)}, bf16[512,2048]{1,0:T(8,128)(2,1)}, u32[]{:S(2)}) copy-start(bf16[512,2048]{1,0:T(8,128)(2,1)} %wv_ref.5) | copy-start | bytes 6291460
  37.1 8.0 %copy-start.5 = (bf16[512,2048]{0,1:T(8,128)(2,1)S(1)}, bf16[512,2048]{0,1:T(8,128)(2,1)}, u32[]{:S(2)}) copy-start(bf16[512,2048]{0,1:T(8,128)(2,1)} %copy.9) | copy-start | bytes 6291460
  37.1 8.0 %copy-start.7 = (bf16[512,2048]{0,1:T(8,128)(2,1)S(1)}, bf16[512,2048]{0,1:T(8,128)(2,1)}, u32[]{:S(2)}) copy-start(bf16[512,2048]{0,1:T(8,128)(2,1)} %copy.10) | copy-start | bytes 6291460
  37.1 8.0 %copy-start.8 = (bf16[256,2048]{0,1:T(8,128)(2,1)S(1)}, bf16[256,2048]{0,1:T(8,128)(2,1)}, u32[]{:S(2)}) copy-start(bf16[256,2048]{0,1:T(8,128)(2,1)} %copy.11) | copy-start | bytes 3145732
  37.1 35.8 %slice-start = ((s8[9437184]{0:T(1024)(128)(4,1)}), s8[4194304]{0:T(1024)(128)(4,1)S(1)}, s32[]{:S(2)}) async-start(s8[9437184]{0:T(1024)(128)(4,1)} %bitcast.14), calls=%async_computation.2 | async-start | bytes 8388608
  37.1 35.8 %slice-start.1 = ((s8[9437184]{0:T(1024)(128)(4,1)}), s8[1048576]{0:T(1024)(128)(4,1)S(1)}, s32[]{:S(2)}) async-start(s8[9437184]{0:T(1024)(128)(4,1)} %bitcast.14), calls=%async_computation.3 | async-start | bytes 2097152
  44.1 1.0 copy-start.9
  45.1 1.2 %copy-start.10 = (bf16[256,2048]{1,0:T(8,128)(2,1)S(1)}, bf16[256,2048]{1,0:T(8,128)(2,1)}, u32[]{:S(2)}) copy-start(bf16[256,2048]{1,0:T(8,128)(2,1)} %copy-done.9) | copy-start | bytes 3145732
  46.4 26.6 %slice-start.2 = ((s8[9437184]{0:T(1024)(128)(4,1)}), s8[4194304]{0:T(1024)(128)(4,1)S(1)}, s32[]{:S(2)}) async-start(s8[9437184]{0:T(1024)(128)(4,1)} %bitcast.14), calls=%async_computation.4 | async-start | bytes 8388608
  69.3 9.1 %collective-permute-start.1 = (bf16[576,256]{1,0:T(8,128)(2,1)S(1)}, bf16[576,256]{1,0:T(8,128)(2,1)S(1)}, u32[]{:S(2)}, u32[]{:S(2)}) collective-permute-start(bf16[576,256]{1,0:T(8,128)(2,1)S(1)} %get-tuple-element.36), channel_id=1, source_target_pairs={{8,0},{16,8},{24,16},{32,24},{40,32},{48,40},{56,48},{64,56},{72,6... | collective-permute-start | bytes 884744 | tf_op jit(solution)/shard_map/ppermute | solution.py:285
  79.6 20.2 %all-to-all-start.1 = ((bf16[8,264,256]{2,1,0:T(8,128)(2,1)}), bf16[8,264,256]{2,1,0:T(8,128)(2,1)S(1)}, u32[]{:S(2)}, u32[]{:S(2)}) async-start(bf16[8,264,256]{2,1,0:T(8,128)(2,1)} %pad_maximum_fusion), calls=%async_computation.1 | async-start | bytes 2162688 | tf_op jit(solution)/shard_map/all_to_all | solution.py:292

commit v3 on v0

v3 whole, which is shorter than its diff:
```python
import math

import jax
import jax.numpy as jnp
from jax import lax
from jax.experimental import pallas as pl
from jax.experimental.pallas import tpu as pltpu
from jax.sharding import PartitionSpec as P

QL = 1536
KVL = 512
ROPE = 64
NOPE = 128
VDIM = 128
WIDTH = NOPE + ROPE
PAD = 256
HEAD_DEV = 16
TOK = 256
HALF = TOK // 2
PEERS = 8
Q_ROWS = QL // PEERS
KV_ROWS = (KVL + ROPE) // PEERS
SCALE = WIDTH ** (-0.5)
EXPONENT = SCALE / math.log(2.0)
HIDDEN = -1e30
MIB = 1024 * 1024

NN = (((1,), (0,)), ((), ()))
NT = (((1,), (1,)), ((), ()))
BF16 = jnp.bfloat16
F32 = jnp.float32


def mm(a, b, dims=NN):
    return lax.dot_general(a, b, dims, preferred_element_type=F32)


def kernel_call(body, name, out_shape, *args, mib=16, scratch=(), spaces=None):
    vmem = pl.BlockSpec(memory_space=pltpu.VMEM)
    if spaces is None:
        spaces = [pltpu.VMEM] * len(args)
    args = [
        pltpu.with_memory_space_constraint(a, pltpu.VMEM) if s is pltpu.VMEM else a
        for a, s in zip(args, spaces)
    ]
    return pl.pallas_call(
        body,
        in_specs=[pl.BlockSpec(memory_space=s) for s in spaces],
        out_specs=[vmem] * len(out_shape),
        out_shape=[pltpu.VMEM(shape, dtype) for shape, dtype in out_shape],
        scratch_shapes=list(scratch),
        compiler_params=pltpu.CompilerParams(vmem_limit_bytes=mib * MIB),
        name=name,
    )(*args)


def stage_kernel(*refs):
    n = len(refs) // 2
    sems = refs[-1]
    copies = [
        pltpu.make_async_copy(refs[i], refs[n + i], sems.at[i]) for i in range(n)
    ]
    for copy in copies:
        copy.start()
    for copy in copies:
        copy.wait()


def stage(*arrays):
    return kernel_call(
        stage_kernel,
        "stage",
        [(a.shape, a.dtype) for a in arrays],
        *arrays,
        scratch=[pltpu.SemaphoreType.DMA((len(arrays),))],
        spaces=[pl.ANY] * len(arrays),
    )


P_HEADS = 4


def project_kernel(g_ref, wq_ref, wk_ref, wv_ref, q_ref, k_ref, v_ref, kvt_ref):
    for i in range(PEERS):
        kvt_ref[i * KV_ROWS : (i + 1) * KV_ROWS, :] = g_ref[i, Q_ROWS:, :]
    kv = kvt_ref[:KVL, :].T
    k_ref[...] = mm(kv, wk_ref[...]).astype(BF16)
    v_ref[...] = mm(kv, wv_ref[...]).astype(BF16)
    qlat = g_ref[:, :Q_ROWS, :].reshape(QL, TOK).T
    lane = lax.broadcasted_iota(jnp.int32, (TOK, PAD - WIDTH), 1)
    one = jnp.where(lane == 0, 1.0, 0.0).astype(BF16)
    cols = P_HEADS * WIDTH
    for i in range(HEAD_DEV // P_HEADS):
        queries = mm(qlat, wq_ref[:, i * cols : (i + 1) * cols]).astype(BF16)
        for j in range(P_HEADS):
            h = i * P_HEADS + j
            q_ref[:, h * PAD : (h + 1) * PAD] = jnp.concatenate(
                [queries[:, j * WIDTH : (j + 1) * WIDTH], one], 1
            )


def project(g, wq, wk, wv):
    return kernel_call(
        project_kernel,
        "project",
        [
            ((TOK, HEAD_DEV * PAD), BF16),
            ((TOK, HEAD_DEV * NOPE), BF16),
            ((TOK, HEAD_DEV * VDIM), BF16),
            ((KVL + ROPE, TOK), BF16),
        ],
        g, wq, wk, wv,
    )


def attend_kernel(lead_ref, kvt_ref, pkvt_ref, q_ref, k_ref, v_ref, do_ref, wk_ref, wv_ref,
                  out_ref, dqt_ref, dk_ref, dv_ref, early_ref, own_rope_ref,
                  kp, vp, dkp, dvp):
    pkv = pkvt_ref[:KVL, :].T
    kp[...] = mm(pkv, wk_ref[...]).astype(BF16)
    vp[...] = mm(pkv, wv_ref[...]).astype(BF16)
    ropes_t = jnp.concatenate([pkvt_ref[KVL:, :], kvt_ref[KVL:, :]], 1)
    at_row = lax.broadcasted_iota(jnp.int32, (ROPE, 2 * TOK), 0)
    at_key = lax.broadcasted_iota(jnp.int32, (ROPE, 2 * TOK), 1)
    shut = jnp.where(lead_ref[0] > 0, HIDDEN, 0.0)
    marks_t = jnp.where((at_row == 0) & (at_key < TOK), shut, 0.0).astype(BF16)
    ropes = jnp.concatenate([ropes_t, marks_t], 0).T
    key = lax.broadcasted_iota(jnp.int32, (HALF, HALF), 0)
    query = lax.broadcasted_iota(jnp.int32, (HALF, HALF), 1)
    seen = key <= query
    rope_sum = [None]

    def head(h):
        at = slice(h * NOPE, (h + 1) * NOPE)
        q = q_ref[:, h * PAD : (h + 1) * PAD]
        keys = jnp.concatenate([kp[:, at], k_ref[:, at]], 0)
        vals = jnp.concatenate([vp[:, at], v_ref[:, at]], 0)
        d_out_h = do_ref[:, at]
        d_out_t = d_out_h.T
        scores = mm(jnp.concatenate([keys, ropes], 1), q, NT)
        yield
        s_p = scores[:TOK]
        s_a = jnp.concatenate(
            [
                jnp.where(seen, scores[TOK : TOK + HALF, :HALF], HIDDEN),
                scores[TOK : TOK + HALF, HALF:],
            ],
            1,
        )
        s_b = jnp.where(seen, scores[TOK + HALF :, HALF:], HIDDEN)
        top = jnp.maximum(
            jnp.max(s_p, 0, keepdims=True), jnp.max(s_a, 0, keepdims=True)
        )
        top_b = jnp.maximum(top[:, HALF:], jnp.max(s_b, 0, keepdims=True))
        top = jnp.concatenate([top[:, :HALF], top_b], 1)
        yield
        e_p = jnp.exp2((s_p - top) * EXPONENT)
        e_a = jnp.exp2((s_a - top) * EXPONENT)
        e_b = jnp.exp2((s_b - top_b) * EXPONENT)
        total = jnp.sum(e_p, 0, keepdims=True) + jnp.sum(e_a, 0, keepdims=True)
        total = jnp.concatenate(
            [total[:, :HALF], total[:, HALF:] + jnp.sum(e_b, 0, keepdims=True)], 1
        )
        yield
        inv = 1.0 / total
        p_p, p_a, p_b = e_p * inv, e_a * inv, e_b * inv[:, HALF:]
        none = jnp.zeros((HALF, HALF), BF16)
        probs = jnp.concatenate(
            [
                p_p.astype(BF16),
                p_a.astype(BF16),
                jnp.concatenate([none, p_b.astype(BF16)], 1),
            ],
            0,
        )
        yield
        out_t = mm(vals.T, probs).astype(BF16)
        dprob = mm(vals, d_out_t)
        yield
        out_ref[:, at] = out_t.T
        row_dot = jnp.sum(d_out_t.astype(F32) * out_t.astype(F32), 0, keepdims=True)
        yield
        d_p = (p_p * ((dprob[:TOK] - row_dot) * SCALE)).astype(BF16)
        d_a = (p_a * ((dprob[TOK : TOK + HALF] - row_dot) * SCALE)).astype(BF16)
        d_b = (p_b * ((dprob[TOK + HALF :, HALF:] - row_dot[:, HALF:]) * SCALE)).astype(BF16)
        dscore = jnp.concatenate([d_p, d_a, jnp.concatenate([none, d_b], 1)], 0)
        yield
        dqt = mm(jnp.concatenate([keys.T, ropes_t], 0), dscore)
        dk = mm(dscore, q)
        dv = mm(probs, d_out_h)
        yield
        dqt_ref[h * WIDTH : (h + 1) * WIDTH, :] = dqt.astype(BF16)
        dk = dk.astype(BF16)
        dv = dv.astype(BF16)
        dkp[:, at] = dk[:TOK, :NOPE]
        dvp[:, at] = dv[:TOK]
        dk_ref[:, at] = dk[TOK:, :NOPE]
        dv_ref[:, at] = dv[TOK:]
        rope = dk[:, NOPE:].astype(F32)
        rope_sum[0] = rope if rope_sum[0] is None else rope_sum[0] + rope

    skewed(head, HEAD_DEV, LAG)
    early_ref[:KVL, :] = (
        mm(wk_ref[...], dkp[...], NT) + mm(wv_ref[...], dvp[...], NT)
    ).astype(BF16)
    rope_t = rope_sum[0].T
    early_ref[KVL:, :] = rope_t[:ROPE, :TOK].astype(BF16)
    own_rope_ref[...] = rope_t[:ROPE, TOK:]


LAG = 4


def skewed(make, count, lag):
    running = []
    made = 0
    step = 0
    while made < count or running:
        if made < count and step % lag == 0:
            running.append(make(made))
            made += 1
        running = [r for r in running if next(r, True) is None]
        step += 1


def attend(lead, kvt, pkvt, q, k, v, d_out, wk, wv):
    return kernel_call(
        attend_kernel,
        "attend",
        [
            ((TOK, HEAD_DEV * VDIM), BF16),
            ((HEAD_DEV * WIDTH, TOK), BF16),
            ((TOK, HEAD_DEV * NOPE), BF16),
            ((TOK, HEAD_DEV * VDIM), BF16),
            ((KVL + ROPE, TOK), BF16),
            ((ROPE, TOK), F32),
        ],
        lead, kvt, pkvt, q, k, v, d_out, wk, wv,
        scratch=[pltpu.VMEM((TOK, HEAD_DEV * NOPE), BF16)] * 4,
        spaces=[pltpu.SMEM] + [pltpu.VMEM] * 8,
    )


def gradients_kernel(dqt_ref, dk_ref, dv_ref, wq_ref, wk_ref, wv_ref, terms_ref, gkv_ref):
    gkv_ref[...] = mm(wk_ref[...], dk_ref[...], NT) + mm(wv_ref[...], dv_ref[...], NT)
    for i in range(PEERS // 2):
        rows = slice(2 * i * Q_ROWS, 2 * (i + 1) * Q_ROWS)
        part = mm(wq_ref[rows, :], dqt_ref[...]).astype(BF16)
        terms_ref[2 * i, :Q_ROWS, :] = part[:Q_ROWS]
        terms_ref[2 * i + 1, :Q_ROWS, :] = part[Q_ROWS:]


def gradients(dqt, dk, dv, wq, wk, wv):
    return kernel_call(
        gradients_kernel,
        "gradients",
        [((PEERS, Q_ROWS, TOK), BF16), ((KVL, TOK), F32)],
        dqt, dk, dv, wq, wk, wv,
    )


def on_device(q_latent, kv_latent, w_query, w_key, w_value, d_out):
    peers = lax.axis_size("head")
    blocks = lax.axis_size("ctx")
    own = jnp.concatenate([q_latent.T, kv_latent.T], 0)
    copies = jnp.broadcast_to(own, (peers, *own.shape))
    g = lax.all_to_all(copies, "head", 0, 0, tiled=True)
    w_query, w_key, w_value, d_out = stage(w_query, w_key, w_value, d_out)
    g, w_query, w_key, w_value, d_out = lax.optimization_barrier(
        (g, w_query, w_key, w_value, d_out)
    )
    sent = g[:, Q_ROWS:, :].reshape(KVL + ROPE, TOK)
    pkvt = lax.ppermute(sent, "ctx", [(i, i + 1) for i in range(blocks - 1)])
    q, k, v, kvt = project(g, w_query, w_key, w_value)
    lead = (lax.axis_index("ctx") == 0).astype(jnp.int32).reshape(1)
    out, dqt, dk, dv, early, own_rope = attend(
        lead, kvt, pkvt, q, k, v, d_out, w_key, w_value
    )
    later = lax.ppermute(early, "ctx", [(i, i - 1) for i in range(1, blocks)])
    gq, gkv = gradients(dqt, dk, dv, w_query, w_key, w_value)
    own_kv = jnp.concatenate([gkv, own_rope], 0)
    gkv = (own_kv + later.astype(F32)).astype(BF16)
    terms = jnp.concatenate([gq, gkv.reshape(peers, -1, TOK)], 1)
    terms = lax.all_to_all(terms, "head", 0, 0, tiled=True)
    sums = jnp.sum(terms.astype(F32), 0)
    return out, sums[:Q_ROWS].T, sums[Q_ROWS:].T


def solution(mesh):
    return jax.shard_map(
        on_device,
        mesh=mesh,
        in_specs=(
            P("ctx", "head"),
            P("ctx", "head"),
            P(None, "head"),
            P(None, "head"),
            P(None, "head"),
            P("ctx", "head"),
        ),
        out_specs=(P("ctx", "head"), P("ctx", "head"), P("ctx", "head")),
        check_vma=False,
    )
```

time: 141 us -> 86 us (0.61)
  matrix products: 58 us -> 0 us
  Pallas kernels: 0 us -> 22.3 us
  starting transfers between devices: 29.9 us -> 18.2 us
  other arithmetic: 7.7 us -> 2.33 us
  waiting for transfers between devices: 21 us -> 18.4 us
    dot_general x18 -> x0, matrix products: 47.4 us -> none  [the longest x1 7.47 us: on_device(): jnp.dot(collect(q_latent, 'head', 1), w_query, preferred_element_type=jnp...]
    pallas_call x0 -> x4, Pallas kernels: none -> 22.3 us  [kernel_call(): pl.pallas_call(body, in_specs=[pl.BlockSpec(memory_space=s) for s in spac...]
    unnamed x33 -> x29, local copies, waits for them, and re-layouts: 6.84 us -> 19.1 us
    all_to_all x4 -> x2, starting transfers between devices: 24 us -> 12.6 us  [the longest x1 7.77 us: on_device(): g = lax.all_to_all(copies, 'head', 0, 0, tiled=True)]
    sub x1 -> x0, matrix products: 10.6 us -> none  [on_device(): expons = jnp.where(visible, jnp.exp(scores - maxima), jnp.float32(0.0))]
    convert_element_type x3 -> x0, local copies, waits for them, and re-layouts: 4.62 us -> none  [the longest x1 2.59 us: on_device(): queries = queries.astype(jnp.bfloat16).reshape(block_rows, per_dev, width)]
    reshape x2 -> x0, local copies, waits for them, and re-layouts: 4.57 us -> none  [expand(): values.reshape(block_rows, per_dev, VDIM)]
    convert_element_type x2 -> x1, other arithmetic: 4.03 us -> 0.08 us  [on_device(): gkv = (own_kv + later.astype(F32)).astype(BF16)]
  transfers between devices with their start and end apart: 6 -> 4, of which waited for: 4 -> 3; matrix products, arithmetic and copies ran while one was open for 22% -> 1% of each run, Pallas kernels for 0% -> 12%
where the time goes in v3:
time: 86 us; the launch traced here: 84.5 us
  local copies, waits for them, and re-layouts  22.5 us (26%)
  Pallas kernels  22.3 us (26%)
  waiting for transfers between devices  18.4 us (21%)
  starting transfers between devices  18.2 us (21%)
  other arithmetic  2.33 us (3%)
    pallas_call x4, Pallas kernels, kernel_call(): pl.pallas_call(body, in_specs=[pl.BlockSpec(memory_space=s) for s in spac...  22.3 us
    unnamed x29, local copies, waits for them, and re-layouts  19.1 us
    all_to_all x1, waiting for transfers between devices, on_device(): terms = lax.all_to_all(terms, 'head', 0, 0, tiled=True)  15.6 us
    all_to_all x1, starting transfers between devices, on_device(): g = lax.all_to_all(copies, 'head', 0, 0, tiled=True)  7.77 us
    all_to_all x1, starting transfers between devices, on_device(): terms = lax.all_to_all(terms, 'head', 0, 0, tiled=True)  4.81 us
    ppermute x1, starting transfers between devices, on_device(): later = lax.ppermute(early, 'ctx', [(i, i - 1) for i in range(1, blocks)])  3.64 us
    all_to_all x1, waiting for transfers between devices, on_device(): g = lax.all_to_all(copies, 'head', 0, 0, tiled=True)  2.4 us
    ppermute x1, starting transfers between devices, on_device(): pkvt = lax.ppermute(sent, 'ctx', [(i, i + 1) for i in range(blocks - 1)])  1.92 us
  transfers between devices with their start and end apart: 4, of which 3 were waited for; matrix products, arithmetic and copies ran while one was open for 1% of the time, Pallas kernels for 12%

profile of v3, /device:TPU:16, one launch (start us, length us, event | category | flops | bytes accessed | tf_op | source)
XLA Modules:
  0.0 84.5 jit_solution(5206346407941188398)
XLA Ops:
  0.6 0.0 copy-start.8
  0.6 1.0 %pad_maximum_fusion.1 = bf16[264,256]{1,0:T(8,128)(2,1)S(1)} fusion(bf16[72,256]{1,0:T(8,128)(2,1)} %bitcast.14, bf16[192,256]{1,0:T(8,128)(2,1)} %bitcast.13), kind=kLoop, calls=%fused_computation.5 | loop fusion | flops 270336 | bytes 270336 | tf_op jit(solution)/shard_map/concatenate | solution.py:265
  1.7 1.1 %broadcast_in_dim.3 = bf16[8,264,256]{2,1,0:T(8,128)(2,1)} broadcast(bf16[264,256]{1,0:T(8,128)(2,1)S(1)} %pad_maximum_fusion.1), dimensions={1,2} | broadcast | bytes 1216512 | tf_op jit(solution)/shard_map/broadcast_in_dim | solution.py:266
  2.8 7.8 %all-to-all-start = ((bf16[8,264,256]{2,1,0:T(8,128)(2,1)}), bf16[8,264,256]{2,1,0:T(8,128)(2,1)}, u32[]{:S(2)}, u32[]{:S(2)}) async-start(bf16[8,264,256]{2,1,0:T(8,128)(2,1)} %broadcast_in_dim.3), calls=%async_computation | async-start | bytes 2162688 | tf_op jit(solution)/shard_map/all_to_all | solution.py:267
  10.5 0.0 copy-done.8
  10.5 0.0 copy-start.5
  10.5 3.7 %copy-done.5 = bf16[1536,3072]{1,0:T(8,128)(2,1)S(1)} copy-done((bf16[1536,3072]{1,0:T(8,128)(2,1)S(1)}, bf16[1536,3072]{1,0:T(8,128)(2,1)}, u32[]{:S(2)}) %copy-start.5) | copy-done | bytes 9437208
  14.2 0.0 copy-start.6
  14.2 1.6 %copy-done.6 = bf16[512,2048]{1,0:T(8,128)(2,1)S(1)} copy-done((bf16[512,2048]{1,0:T(8,128)(2,1)S(1)}, bf16[512,2048]{1,0:T(8,128)(2,1)}, u32[]{:S(2)}) %copy-start.6) | copy-done | bytes 2097176
  15.8 0.0 copy-start.7
  15.8 1.6 %copy-done.7 = bf16[512,2048]{1,0:T(8,128)(2,1)S(1)} copy-done((bf16[512,2048]{1,0:T(8,128)(2,1)S(1)}, bf16[512,2048]{1,0:T(8,128)(2,1)}, u32[]{:S(2)}) %copy-start.7) | copy-done | bytes 2097176
  17.4 1.0 %stage.1 = (bf16[1536,3072]{1,0:T(8,128)(2,1)S(1)}, bf16[512,2048]{1,0:T(8,128)(2,1)S(1)}, bf16[512,2048]{1,0:T(8,128)(2,1)S(1)}, bf16[256,2048]{1,0:T(8,128)(2,1)S(1)}) custom-call(bf16[1536,3072]{1,0:T(8,128)(2,1)S(1)} %copy-done.5, bf16[512,2048]{1,0:T(8,128)(2,1)S(1)} %copy-done.6, bf16[512,2048]{1,0:T(8,128)(2,1)S(1)} %copy-done.7, ...), custom_call_target="tpu_custom_call" | custom-call | tf_op jit(solution)/shard_map/stage/pallas_call | solution.py:46
  18.4 0.0 copy-start
  18.4 3.7 %copy-done = bf16[1536,3072]{1,0:T(8,128)(2,1)} copy-done((bf16[1536,3072]{1,0:T(8,128)(2,1)}, bf16[1536,3072]{1,0:T(8,128)(2,1)S(1)}, u32[]{:S(2)}) %copy-start) | copy-done | bytes 9437208
  22.1 0.0 copy-start.2
  22.1 1.3 %copy-done.2 = bf16[512,2048]{1,0:T(8,128)(2,1)} copy-done((bf16[512,2048]{1,0:T(8,128)(2,1)}, bf16[512,2048]{1,0:T(8,128)(2,1)S(1)}, u32[]{:S(2)}) %copy-start.2) | copy-done | bytes 2097176
  23.4 0.0 copy-start.9
  23.4 1.0 %copy-done.9 = bf16[256,2048]{1,0:T(8,128)(2,1)} copy-done((bf16[256,2048]{1,0:T(8,128)(2,1)}, bf16[256,2048]{1,0:T(8,128)(2,1)S(1)}, u32[]{:S(2)}) %copy-start.9) | copy-done | bytes 1048600
  24.4 2.4 %all-to-all-done.g_ref = bf16[8,264,256]{2,1,0:T(8,128)(2,1)} async-done(((bf16[8,264,256]{2,1,0:T(8,128)(2,1)}), bf16[8,264,256]{2,1,0:T(8,128)(2,1)}, u32[]{:S(2)}, u32[]{:S(2)}) %all-to-all-start) | async-done | bytes 1081376 | tf_op jit(solution)/shard_map/all_to_all | solution.py:267
  26.8 1.0 %slice.9 = bf16[8,72,256]{2,1,0:T(8,128)(2,1)S(1)} slice(bf16[8,264,256]{2,1,0:T(8,128)(2,1)} %all-to-all-done.g_ref), slice={[0:8], [192:264], [0:256]} | slice | bytes 589824 | tf_op jit(solution)/shard_map/slice | solution.py:272
  27.8 1.9 %collective-permute-start = (bf16[576,256]{1,0:T(8,128)(2,1)S(1)}, bf16[576,256]{1,0:T(8,128)(2,1)S(1)}, u32[]{:S(2)}, u32[]{:S(2)}) collective-permute-start(bf16[576,256]{1,0:T(8,128)(2,1)S(1)} %bitcast.12), channel_id=1, source_target_pairs={{0,8},{8,16},{16,24},{24,32},{32,40},{40,48},{48,56},{56,64},{64,7... | collective-permute-start | bytes 884744 | tf_op jit(solution)/shard_map/ppermute | solution.py:273
  29.7 0.0 copy-start.1
  29.7 3.7 %copy-done.1 = bf16[1536,3072]{1,0:T(8,128)(2,1)S(1)} copy-done((bf16[1536,3072]{1,0:T(8,128)(2,1)S(1)}, bf16[1536,3072]{1,0:T(8,128)(2,1)}, u32[]{:S(2)}) %copy-start.1) | copy-done | bytes 9437208
  33.4 0.0 copy-start.3
  33.4 1.6 %copy-done.3 = bf16[512,2048]{1,0:T(8,128)(2,1)S(1)} copy-done((bf16[512,2048]{1,0:T(8,128)(2,1)S(1)}, bf16[512,2048]{1,0:T(8,128)(2,1)}, u32[]{:S(2)}) %copy-start.3) | copy-done | bytes 2097176
  35.0 0.0 copy-start.4
  35.0 0.0 copy-start.10
  35.0 0.0 slice-start
  35.0 0.0 slice-start.1
  35.0 5.2 %project.1 = (bf16[256,4096]{1,0:T(8,128)(2,1)S(1)}, bf16[256,2048]{1,0:T(8,128)(2,1)S(1)}, bf16[256,2048]{1,0:T(8,128)(2,1)S(1)}, bf16[576,256]{1,0:T(8,128)(2,1)S(1)}) custom-call(bf16[8,264,256]{2,1,0:T(8,128)(2,1)} %all-to-all-done.g_ref, bf16[1536,3072]{1,0:T(8,128)(2,1)S(1)} %copy-done.1, bf16[512,2048]{1,0:T(8,128)(2,1)S(1)} %get-tuple-element.30.wk_ref, ...), custom_call_target="tpu_custom_call" | custom-call | tf_op jit(solution)/shard_map/project/pallas_call | solution.py:46
  40.2 0.0 collective-permute-done.pkvt_ref
  40.2 0.0 copy-done.4
  40.2 0.0 copy-done.10
  40.2 0.0 slice-start.2
  40.2 12.4 %attend.1 = (bf16[256,2048]{1,0:T(8,128)(2,1)S(1)}, bf16[3072,256]{1,0:T(8,128)(2,1)S(1)}, bf16[256,2048]{1,0:T(8,128)(2,1)S(1)}, bf16[256,2048]{1,0:T(8,128)(2,...) custom-call(s32[1]{0:T(128)} %bitcast.lead_ref, bf16[576,256]{1,0:T(8,128)(2,1)S(1)} %get-tuple-element.32.kvt_ref, ...), custom_call_target="tpu_custom_call" | custom-call | tf_op jit(solution)/shard_map/attend/pallas_call | solution.py:46
  52.6 3.6 %collective-permute-start.1 = (bf16[576,256]{1,0:T(8,128)(2,1)S(1)}, bf16[576,256]{1,0:T(8,128)(2,1)S(1)}, u32[]{:S(2)}, u32[]{:S(2)}) collective-permute-start(bf16[576,256]{1,0:T(8,128)(2,1)S(1)} %get-tuple-element.44), channel_id=1, source_target_pairs={{8,0},{16,8},{24,16},{32,24},{40,32},{48,40},{56,48},{64,56},{72,6... | collective-permute-start | bytes 884744 | tf_op jit(solution)/shard_map/ppermute | solution.py:279
  56.3 0.0 slice-done
  56.3 0.0 slice-done.1
  56.3 0.0 slice-done.2
  56.3 3.7 %gradients.1 = (bf16[8,192,256]{2,1,0:T(8,128)(2,1)S(1)}, f32[512,256]{1,0:T(8,128)S(1)}) custom-call(bf16[3072,256]{1,0:T(8,128)(2,1)S(1)} %get-tuple-element.38.dqt_ref, bf16[256,2048]{1,0:T(8,128)(2,1)S(1)} %get-tuple-element.39.dk_ref, bf16[256,2048]{1,0:T(8,128)(2,1)S(1)} %get-tuple-element.40.dv_ref, bf16[1536,3072]{1,0:T(8,128)(2,1)S(1)} %bitcast.10, ...), custom_call_target="tpu_custom_call" | custom-call | tf_op jit(solution)/shard_map/gradients/pallas_call | solution.py:46
  60.0 0.4 collective-permute-done.1
  60.5 0.1 fusion
  60.6 1.1 %pad_maximum_fusion = bf16[8,264,256]{2,1,0:T(8,128)(2,1)} fusion(bf16[8,72,256]{2,1,0:T(8,128)(2,1)S(1)} %bitcast.11, bf16[8,192,256]{2,1,0:T(8,128)(2,1)S(1)} %get-tuple-element.41), kind=kLoop, calls=%fused_computation.1 | loop fusion | flops 2162688 | bytes 2162688 | tf_op jit(solution)/shard_map/concatenate | solution.py:283
  61.7 4.8 %all-to-all-start.1 = ((bf16[8,264,256]{2,1,0:T(8,128)(2,1)}), bf16[8,264,256]{2,1,0:T(8,128)(2,1)S(1)}, u32[]{:S(2)}, u32[]{:S(2)}) async-start(bf16[8,264,256]{2,1,0:T(8,128)(2,1)} %pad_maximum_fusion), calls=%async_computation.1 | async-start | bytes 2162688 | tf_op jit(solution)/shard_map/all_to_all | solution.py:284
  66.5 1.0 %copy.9 = bf16[256,2048]{1,0:T(8,128)(2,1)} copy(bf16[256,2048]{1,0:T(8,128)(2,1)S(1)} %get-tuple-element.45) | data formatting | bytes 2097152
  67.5 15.6 %all-to-all-done.1 = bf16[8,264,256]{2,1,0:T(8,128)(2,1)S(1)} async-done(((bf16[8,264,256]{2,1,0:T(8,128)(2,1)}), bf16[8,264,256]{2,1,0:T(8,128)(2,1)S(1)}, u32[]{:S(2)}, u32[]{:S(2)}) %all-to-all-start.1) | async-done | bytes 1081376 | tf_op jit(solution)/shard_map/all_to_all | solution.py:284
  83.0 0.1 convert_reduce_fusion
  83.2 0.6 slice_bitcast_fusion.1
  83.8 0.7 slice_bitcast_fusion
  (1 shorter events, 0.0 us)
Async XLA Ops:
  0.6 9.9 %copy-start.8 = (bf16[256,2048]{1,0:T(8,128)(2,1)S(1)}, bf16[256,2048]{1,0:T(8,128)(2,1)}, u32[]{:S(2)}) copy-start(bf16[256,2048]{1,0:T(8,128)(2,1)} %refs_3_.1) | copy-start | bytes 3145732
  2.8 24.0 %all-to-all-start = ((bf16[8,264,256]{2,1,0:T(8,128)(2,1)}), bf16[8,264,256]{2,1,0:T(8,128)(2,1)}, u32[]{:S(2)}, u32[]{:S(2)}) async-start(bf16[8,264,256]{2,1,0:T(8,128)(2,1)} %broadcast_in_dim.3), calls=%async_computation | async-start | bytes 2162688 | tf_op jit(solution)/shard_map/all_to_all | solution.py:267
  10.5 3.7 %copy-start.5 = (bf16[1536,3072]{1,0:T(8,128)(2,1)S(1)}, bf16[1536,3072]{1,0:T(8,128)(2,1)}, u32[]{:S(2)}) copy-start(bf16[1536,3072]{1,0:T(8,128)(2,1)} %refs_0_.1) | copy-start | bytes 28311556
  14.2 1.6 %copy-start.6 = (bf16[512,2048]{1,0:T(8,128)(2,1)S(1)}, bf16[512,2048]{1,0:T(8,128)(2,1)}, u32[]{:S(2)}) copy-start(bf16[512,2048]{1,0:T(8,128)(2,1)} %refs_1_.1) | copy-start | bytes 6291460
  15.8 1.6 %copy-start.7 = (bf16[512,2048]{1,0:T(8,128)(2,1)S(1)}, bf16[512,2048]{1,0:T(8,128)(2,1)}, u32[]{:S(2)}) copy-start(bf16[512,2048]{1,0:T(8,128)(2,1)} %refs_2_.1) | copy-start | bytes 6291460
  18.4 3.7 %copy-start = (bf16[1536,3072]{1,0:T(8,128)(2,1)}, bf16[1536,3072]{1,0:T(8,128)(2,1)S(1)}, u32[]{:S(2)}) copy-start(bf16[1536,3072]{1,0:T(8,128)(2,1)S(1)} %get-tuple-element.29.wq_ref) | copy-start | bytes 28311556
  22.1 1.3 %copy-start.2 = (bf16[512,2048]{1,0:T(8,128)(2,1)}, bf16[512,2048]{1,0:T(8,128)(2,1)S(1)}, u32[]{:S(2)}) copy-start(bf16[512,2048]{1,0:T(8,128)(2,1)S(1)} %get-tuple-element.31.wv_ref) | copy-start | bytes 6291460
  23.4 1.0 %copy-start.9 = (bf16[256,2048]{1,0:T(8,128)(2,1)}, bf16[256,2048]{1,0:T(8,128)(2,1)S(1)}, u32[]{:S(2)}) copy-start(bf16[256,2048]{1,0:T(8,128)(2,1)S(1)} %get-tuple-element.36.do_ref) | copy-start | bytes 3145732
  27.8 12.4 %collective-permute-start = (bf16[576,256]{1,0:T(8,128)(2,1)S(1)}, bf16[576,256]{1,0:T(8,128)(2,1)S(1)}, u32[]{:S(2)}, u32[]{:S(2)}) collective-permute-start(bf16[576,256]{1,0:T(8,128)(2,1)S(1)} %bitcast.12), channel_id=1, source_target_pairs={{0,8},{8,16},{16,24},{24,32},{32,40},{40,48},{48,56},{56,64},{64,7... | collective-permute-start | bytes 884744 | tf_op jit(solution)/shard_map/ppermute | solution.py:273
  29.7 3.7 %copy-start.1 = (bf16[1536,3072]{1,0:T(8,128)(2,1)S(1)}, bf16[1536,3072]{1,0:T(8,128)(2,1)}, u32[]{:S(2)}) copy-start(bf16[1536,3072]{1,0:T(8,128)(2,1)} %copy-done) | copy-start | bytes 28311556
  33.4 1.6 %copy-start.3 = (bf16[512,2048]{1,0:T(8,128)(2,1)S(1)}, bf16[512,2048]{1,0:T(8,128)(2,1)}, u32[]{:S(2)}) copy-start(bf16[512,2048]{1,0:T(8,128)(2,1)} %copy-done.2) | copy-start | bytes 6291460
  35.0 5.2 %copy-start.4 = (bf16[512,2048]{1,0:T(8,128)(2,1)S(1)}, bf16[512,2048]{1,0:T(8,128)(2,1)}, u32[]{:S(2)}) copy-start(bf16[512,2048]{1,0:T(8,128)(2,1)} %copy-done.2) | copy-start | bytes 6291460
  35.0 5.2 %copy-start.10 = (bf16[256,2048]{1,0:T(8,128)(2,1)S(1)}, bf16[256,2048]{1,0:T(8,128)(2,1)}, u32[]{:S(2)}) copy-start(bf16[256,2048]{1,0:T(8,128)(2,1)} %copy-done.9) | copy-start | bytes 3145732
  35.0 21.3 %slice-start = ((s8[9437184]{0:T(1024)(128)(4,1)}), s8[1048576]{0:T(1024)(128)(4,1)S(1)}, s32[]{:S(2)}) async-start(s8[9437184]{0:T(1024)(128)(4,1)} %bitcast.9), calls=%async_computation.2 | async-start | bytes 2097152
  35.0 21.3 %slice-start.1 = ((s8[9437184]{0:T(1024)(128)(4,1)}), s8[4194304]{0:T(1024)(128)(4,1)S(1)}, s32[]{:S(2)}) async-start(s8[9437184]{0:T(1024)(128)(4,1)} %bitcast.9), calls=%async_computation.3 | async-start | bytes 8388608
  40.2 16.1 %slice-start.2 = ((s8[9437184]{0:T(1024)(128)(4,1)}), s8[4194304]{0:T(1024)(128)(4,1)S(1)}, s32[]{:S(2)}) async-start(s8[9437184]{0:T(1024)(128)(4,1)} %bitcast.9), calls=%async_computation.4 | async-start | bytes 8388608
  52.6 7.9 %collective-permute-start.1 = (bf16[576,256]{1,0:T(8,128)(2,1)S(1)}, bf16[576,256]{1,0:T(8,128)(2,1)S(1)}, u32[]{:S(2)}, u32[]{:S(2)}) collective-permute-start(bf16[576,256]{1,0:T(8,128)(2,1)S(1)} %get-tuple-element.44), channel_id=1, source_target_pairs={{8,0},{16,8},{24,16},{32,24},{40,32},{48,40},{56,48},{64,56},{72,6... | collective-permute-start | bytes 884744 | tf_op jit(solution)/shard_map/ppermute | solution.py:279
  61.7 21.4 %all-to-all-start.1 = ((bf16[8,264,256]{2,1,0:T(8,128)(2,1)}), bf16[8,264,256]{2,1,0:T(8,128)(2,1)S(1)}, u32[]{:S(2)}, u32[]{:S(2)}) async-start(bf16[8,264,256]{2,1,0:T(8,128)(2,1)} %pad_maximum_fusion), calls=%async_computation.1 | async-start | bytes 2162688 | tf_op jit(solution)/shard_map/all_to_all | solution.py:284

commit v4 on v3

--- a/solution.py
+++ b/solution.py
@@ -40,12 +40,12 @@
     if spaces is None:
         spaces = [pltpu.VMEM] * len(args)
     args = [
-        pltpu.with_memory_space_constraint(a, pltpu.VMEM) if s is pltpu.VMEM else a
+        pltpu.with_memory_space_constraint(a, s) if s in (pltpu.VMEM, pltpu.HBM) else a
         for a, s in zip(args, spaces)
     ]
     return pl.pallas_call(
         body,
-        in_specs=[pl.BlockSpec(memory_space=s) for s in spaces],
+        in_specs=[pl.BlockSpec(memory_space=s or pltpu.VMEM) for s in spaces],
         out_specs=[vmem] * len(out_shape),
         out_shape=[pltpu.VMEM(shape, dtype) for shape, dtype in out_shape],
         scratch_shapes=list(scratch),
@@ -54,52 +54,51 @@
     )(*args)
 
 
-def stage_kernel(*refs):
-    n = len(refs) // 2
-    sems = refs[-1]
-    copies = [
-        pltpu.make_async_copy(refs[i], refs[n + i], sems.at[i]) for i in range(n)
+P_HEADS = 4
+P_STEPS = HEAD_DEV // P_HEADS
+
+
+def project_kernel(g_ref, wq_hbm, wk_hbm, wv_hbm, do_hbm,
+                   q_ref, k_ref, v_ref, kvt_ref, wk_ref, wv_ref, do_ref, wq_ref, sems):
+    cols = P_HEADS * WIDTH
+    part = lambda i: slice(i * cols, (i + 1) * cols)
+    wq_in = [
+        pltpu.make_async_copy(wq_hbm.at[:, part(i)], wq_ref.at[:, part(i)], sems.at[i])
+        for i in range(P_STEPS)
     ]
-    for copy in copies:
+    wk_in = pltpu.make_async_copy(wk_hbm, wk_ref, sems.at[P_STEPS])
+    wv_in = pltpu.make_async_copy(wv_hbm, wv_ref, sems.at[P_STEPS + 1])
+    do_in = pltpu.make_async_copy(do_hbm, do_ref, sems.at[P_STEPS + 2])
+    order = [wk_in, *wq_in[:1], wv_in, *wq_in[1:], do_in]
+    for copy in order:
         copy.start()
-    for copy in copies:
-        copy.wait()
-
-
-def stage(*arrays):
-    return kernel_call(
-        stage_kernel,
-        "stage",
-        [(a.shape, a.dtype) for a in arrays],
-        *arrays,
-        scratch=[pltpu.SemaphoreType.DMA((len(arrays),))],
-        spaces=[pl.ANY] * len(arrays),
-    )
-
-
-P_HEADS = 4
-
-
-def project_kernel(g_ref, wq_ref, wk_ref, wv_ref, q_ref, k_ref, v_ref, kvt_ref):
     for i in range(PEERS):
         kvt_ref[i * KV_ROWS : (i + 1) * KV_ROWS, :] = g_ref[i, Q_ROWS:, :]
     kv = kvt_ref[:KVL, :].T
-    k_ref[...] = mm(kv, wk_ref[...]).astype(BF16)
-    v_ref[...] = mm(kv, wv_ref[...]).astype(BF16)
     qlat = g_ref[:, :Q_ROWS, :].reshape(QL, TOK).T
     lane = lax.broadcasted_iota(jnp.int32, (TOK, PAD - WIDTH), 1)
     one = jnp.where(lane == 0, 1.0, 0.0).astype(BF16)
-    cols = P_HEADS * WIDTH
-    for i in range(HEAD_DEV // P_HEADS):
-        queries = mm(qlat, wq_ref[:, i * cols : (i + 1) * cols]).astype(BF16)
+
+    def project_queries(i):
+        wq_in[i].wait()
+        queries = mm(qlat, wq_ref[:, part(i)]).astype(BF16)
         for j in range(P_HEADS):
             h = i * P_HEADS + j
             q_ref[:, h * PAD : (h + 1) * PAD] = jnp.concatenate(
                 [queries[:, j * WIDTH : (j + 1) * WIDTH], one], 1
             )
 
-
-def project(g, wq, wk, wv):
+    wk_in.wait()
+    k_ref[...] = mm(kv, wk_ref[...]).astype(BF16)
+    project_queries(0)
+    wv_in.wait()
+    v_ref[...] = mm(kv, wv_ref[...]).astype(BF16)
+    for i in range(1, P_STEPS):
+        project_queries(i)
+    do_in.wait()
+
+
+def project(g, wq, wk, wv, d_out):
     return kernel_call(
         project_kernel,
         "project",
@@ -108,8 +107,14 @@
             ((TOK, HEAD_DEV * NOPE), BF16),
             ((TOK, HEAD_DEV * VDIM), BF16),
             ((KVL + ROPE, TOK), BF16),
+            (wk.shape, BF16),
+            (wv.shape, BF16),
+            (d_out.shape, BF16),
         ],
-        g, wq, wk, wv,
+        g, wq, wk, wv, d_out,
+        mib=20,
+        scratch=[pltpu.VMEM(wq.shape, BF16), pltpu.SemaphoreType.DMA((P_STEPS + 3,))],
+        spaces=[None] + [pltpu.HBM] * 4,
     )
 
 
@@ -241,13 +246,24 @@
     )
 
 
-def gradients_kernel(dqt_ref, dk_ref, dv_ref, wq_ref, wk_ref, wv_ref, terms_ref, gkv_ref):
+G_STEPS = PEERS // 2
+
+
+def gradients_kernel(dqt_ref, dk_ref, dv_ref, wq_hbm, wk_ref, wv_ref,
+                     terms_ref, gkv_ref, wq_ref, sems):
+    part = lambda i: slice(2 * i * Q_ROWS, 2 * (i + 1) * Q_ROWS)
+    wq_in = [
+        pltpu.make_async_copy(wq_hbm.at[part(i), :], wq_ref.at[part(i), :], sems.at[i])
+        for i in range(G_STEPS)
+    ]
+    for copy in wq_in:
+        copy.start()
     gkv_ref[...] = mm(wk_ref[...], dk_ref[...], NT) + mm(wv_ref[...], dv_ref[...], NT)
-    for i in range(PEERS // 2):
-        rows = slice(2 * i * Q_ROWS, 2 * (i + 1) * Q_ROWS)
-        part = mm(wq_ref[rows, :], dqt_ref[...]).astype(BF16)
-        terms_ref[2 * i, :Q_ROWS, :] = part[:Q_ROWS]
-        terms_ref[2 * i + 1, :Q_ROWS, :] = part[Q_ROWS:]
+    for i in range(G_STEPS):
+        wq_in[i].wait()
+        rows = mm(wq_ref[part(i), :], dqt_ref[...]).astype(BF16)
+        terms_ref[2 * i, :Q_ROWS, :] = rows[:Q_ROWS]
+        terms_ref[2 * i + 1, :Q_ROWS, :] = rows[Q_ROWS:]
 
 
 def gradients(dqt, dk, dv, wq, wk, wv):
@@ -256,34 +272,64 @@
         "gradients",
         [((PEERS, Q_ROWS, TOK), BF16), ((KVL, TOK), F32)],
         dqt, dk, dv, wq, wk, wv,
-    )
+        mib=16,
+        scratch=[pltpu.VMEM(wq.shape, BF16), pltpu.SemaphoreType.DMA((G_STEPS,))],
+        spaces=[pltpu.VMEM] * 3 + [pltpu.HBM] + [pltpu.VMEM] * 2,
+    )
+
+
+def pack_kernel(q_ref, kv_ref, out_ref):
+    for i in range(PEERS):
+        out_ref[i, :Q_ROWS, :] = q_ref[...]
+        out_ref[i, Q_ROWS:, :] = kv_ref[...]
+
+
+def pack(q_t, kv_t):
+    return pl.pallas_call(
+        pack_kernel,
+        out_shape=jax.ShapeDtypeStruct((PEERS, Q_ROWS + KV_ROWS, TOK), BF16),
+        name="pack",
+    )(q_t, kv_t)
+
+
+def total_kernel(terms_ref, q_ref, kv_ref):
+    sums = jnp.sum(terms_ref[...].astype(F32), 0)
+    q_ref[...] = sums[:Q_ROWS]
+    kv_ref[...] = sums[Q_ROWS:]
+
+
+def total(terms):
+    return pl.pallas_call(
+        total_kernel,
+        out_shape=[
+            jax.ShapeDtypeStruct((Q_ROWS, TOK), F32),
+            jax.ShapeDtypeStruct((KV_ROWS, TOK), F32),
+        ],
+        in_specs=[pl.BlockSpec(memory_space=pltpu.VMEM)],
+        name="total",
+    )(pltpu.with_memory_space_constraint(terms, pltpu.VMEM))
 
 
 def on_device(q_latent, kv_latent, w_query, w_key, w_value, d_out):
     peers = lax.axis_size("head")
     blocks = lax.axis_size("ctx")
-    own = jnp.concatenate([q_latent.T, kv_latent.T], 0)
-    copies = jnp.broadcast_to(own, (peers, *own.shape))
+    copies = pack(q_latent.T, kv_latent.T)
     g = lax.all_to_all(copies, "head", 0, 0, tiled=True)
-    w_query, w_key, w_value, d_out = stage(w_query, w_key, w_value, d_out)
-    g, w_query, w_key, w_value, d_out = lax.optimization_barrier(
-        (g, w_query, w_key, w_value, d_out)
-    )
     sent = g[:, Q_ROWS:, :].reshape(KVL + ROPE, TOK)
     pkvt = lax.ppermute(sent, "ctx", [(i, i + 1) for i in range(blocks - 1)])
-    q, k, v, kvt = project(g, w_query, w_key, w_value)
+    q, k, v, kvt, wk_in, wv_in, do_in = project(g, w_query, w_key, w_value, d_out)
     lead = (lax.axis_index("ctx") == 0).astype(jnp.int32).reshape(1)
     out, dqt, dk, dv, early, own_rope = attend(
-        lead, kvt, pkvt, q, k, v, d_out, w_key, w_value
+        lead, kvt, pkvt, q, k, v, do_in, wk_in, wv_in
     )
     later = lax.ppermute(early, "ctx", [(i, i - 1) for i in range(1, blocks)])
-    gq, gkv = gradients(dqt, dk, dv, w_query, w_key, w_value)
+    gq, gkv = gradients(dqt, dk, dv, w_query, wk_in, wv_in)
     own_kv = jnp.concatenate([gkv, own_rope], 0)
     gkv = (own_kv + later.astype(F32)).astype(BF16)
     terms = jnp.concatenate([gq, gkv.reshape(peers, -1, TOK)], 1)
     terms = lax.all_to_all(terms, "head", 0, 0, tiled=True)
-    sums = jnp.sum(terms.astype(F32), 0)
-    return out, sums[:Q_ROWS].T, sums[Q_ROWS:].T
+    gq, gkv = total(terms)
+    return out, gq.T, gkv.T
 
 
 def solution(mesh):

time: 86 us -> 83.3 us (0.969); the launches traced: 84.5 us -> 83 us
  blocking collectives: 0 us -> 25.5 us
  local copies, waits for them, and re-layouts: 22.5 us -> 0.99 us
  starting transfers between devices: 18.2 us -> 9.12 us
  Pallas kernels: 22.3 us -> 30.4 us
  waiting for transfers between devices: 18.4 us -> 15.1 us
  other arithmetic: 2.33 us -> 1.12 us
    all_to_all x0 -> x1, blocking collectives: none -> 25.5 us  [on_device(): g = lax.all_to_all(copies, 'head', 0, 0, tiled=True)]
    unnamed x29 -> x1, local copies, waits for them, and re-layouts: 19.1 us -> 0.97 us
    pallas_call x4 -> x5, Pallas kernels: 22.3 us -> 30.4 us  [the longest x3 27.7 us: kernel_call(): pl.pallas_call(body, in_specs=[pl.BlockSpec(memory_space=s or pltpu.VMEM)...]
    all_to_all x1 -> x0, starting transfers between devices: 7.77 us -> none  [on_device(): g = lax.all_to_all(copies, 'head', 0, 0, tiled=True)]
    all_to_all x1 -> x0, waiting for transfers between devices: 2.4 us -> none  [on_device(): g = lax.all_to_all(copies, 'head', 0, 0, tiled=True)]
    transpose x2 -> x0, local copies, waits for them, and re-layouts: 1.33 us -> none  [on_device(): return (out, sums[:Q_ROWS].T, sums[Q_ROWS:].T)]
    all_to_all x1, starting transfers between devices: 4.81 us -> 3.56 us  [on_device(): terms = lax.all_to_all(terms, 'head', 0, 0, tiled=True)]
    broadcast_in_dim x1 -> x0, local copies, waits for them, and re-layouts: 1.1 us -> none  [on_device(): copies = jnp.broadcast_to(own, (peers, *own.shape))]
  transfers between devices with their start and end apart: 4 -> 3, of which waited for: 3 -> 1; matrix products, arithmetic and copies ran while one was open for 1% -> 1% of each run, Pallas kernels for 12% -> 18%
where the time goes in v4:
time: 83.3 us; the launch traced here: 83 us
  Pallas kernels  30.4 us (36%)
  blocking collectives  25.5 us (31%)
  waiting for transfers between devices  15.1 us (18%)
  starting transfers between devices  9.12 us (11%)
  other arithmetic  1.12 us (1%)
  local copies, waits for them, and re-layouts  0.99 us (1%)
    pallas_call x3, Pallas kernels, kernel_call(): pl.pallas_call(body, in_specs=[pl.BlockSpec(memory_space=s or pltpu.VMEM)...  27.7 us
    all_to_all x1, blocking collectives, on_device(): g = lax.all_to_all(copies, 'head', 0, 0, tiled=True)  25.5 us
    all_to_all x1, waiting for transfers between devices, on_device(): terms = lax.all_to_all(terms, 'head', 0, 0, tiled=True)  15.1 us
    ppermute x1, starting transfers between devices, on_device(): later = lax.ppermute(early, 'ctx', [(i, i - 1) for i in range(1, blocks)])  3.64 us
    all_to_all x1, starting transfers between devices, on_device(): terms = lax.all_to_all(terms, 'head', 0, 0, tiled=True)  3.56 us
    pallas_call x1, Pallas kernels, pack(): pl.pallas_call(pack_kernel, out_shape=jax.ShapeDtypeStruct((PEERS, Q_ROWS...  1.94 us
    ppermute x1, starting transfers between devices, on_device(): pkvt = lax.ppermute(sent, 'ctx', [(i, i + 1) for i in range(blocks - 1)])  1.92 us
  transfers between devices with their start and end apart: 3, of which 1 were waited for; matrix products, arithmetic and copies ran while one was open for 1% of the time, Pallas kernels for 18%

profile of v4, /device:TPU:16, one launch (start us, length us, event | category | flops | bytes accessed | tf_op | source)
XLA Modules:
  0.0 83.0 jit_solution(3629334097973550716)
XLA Ops:
  0.6 1.9 %pack.1 = bf16[8,264,256]{2,1,0:T(8,128)(2,1)} custom-call(bf16[192,256]{1,0:T(8,128)(2,1)} %bitcast.9, bf16[72,256]{1,0:T(8,128)(2,1)} %bitcast.10), custom_call_target="tpu_custom_call" | custom-call | tf_op jit(solution)/shard_map/pack/pallas_call | solution.py:288
  2.6 25.5 %all_to_all.10.g_ref = bf16[8,264,256]{2,1,0:T(8,128)(2,1)S(1)} all-to-all(bf16[8,264,256]{2,1,0:T(8,128)(2,1)} %pack.1), channel_id=1, replica_groups=mesh['ctx'=16,'head'=8] {'head'}, dimensions={0} | all-to-all | bytes 2162688 | tf_op jit(solution)/shard_map/all_to_all | solution.py:317
  28.1 1.9 %collective-permute-start = (bf16[576,256]{1,0:T(8,128)(2,1)S(1)}, bf16[576,256]{1,0:T(8,128)(2,1)S(1)}, u32[]{:S(2)}, u32[]{:S(2)}) collective-permute-start(bf16[576,256]{1,0:T(8,128)(2,1)S(1)} %bitcast.8), channel_id=1, source_target_pairs={{0,8},{8,16},{16,24},{24,32},{32,40},{40,48},{48,56},{56,64},{64,7... | collective-permute-start | bytes 884744 | tf_op jit(solution)/shard_map/ppermute | solution.py:319
  30.1 7.5 %project.1 = (bf16[256,4096]{1,0:T(8,128)(2,1)S(1)}, bf16[256,2048]{1,0:T(8,128)(2,1)S(1)}, bf16[256,2048]{1,0:T(8,128)(2,1)S(1)}, bf16[576,256]{1,0:T(8,128)(2,...) custom-call(bf16[8,264,256]{2,1,0:T(8,128)(2,1)S(1)} %all_to_all.10.g_ref, ...), custom_call_target="tpu_custom_call" | custom-call | tf_op jit(solution)/shard_map/project/pallas_call | solution.py:46
  37.6 0.0 collective-permute-done.pkvt_ref
  37.6 12.4 %attend.1 = (bf16[256,2048]{1,0:T(8,128)(2,1)S(1)}, bf16[3072,256]{1,0:T(8,128)(2,1)S(1)}, bf16[256,2048]{1,0:T(8,128)(2,1)S(1)}, bf16[256,2048]{1,0:T(8,128)(2,...) custom-call(s32[1]{0:T(128)} %bitcast.lead_ref, bf16[576,256]{1,0:T(8,128)(2,1)S(1)} %get-tuple-element.20.kvt_ref, ...), custom_call_target="tpu_custom_call" | custom-call | tf_op jit(solution)/shard_map/attend/pallas_call | solution.py:46
  50.0 3.6 %collective-permute-start.1 = (bf16[576,256]{1,0:T(8,128)(2,1)S(1)}, bf16[576,256]{1,0:T(8,128)(2,1)S(1)}, u32[]{:S(2)}, u32[]{:S(2)}) collective-permute-start(bf16[576,256]{1,0:T(8,128)(2,1)S(1)} %get-tuple-element.34), channel_id=1, source_target_pairs={{8,0},{16,8},{24,16},{32,24},{40,32},{48,40},{56,48},{64,56},{72,6... | collective-permute-start | bytes 884744 | tf_op jit(solution)/shard_map/ppermute | solution.py:325
  53.7 7.7 %gradients.1 = (bf16[8,192,256]{2,1,0:T(8,128)(2,1)S(1)}, f32[512,256]{1,0:T(8,128)S(1)}) custom-call(bf16[3072,256]{1,0:T(8,128)(2,1)S(1)} %get-tuple-element.28.dqt_ref, bf16[256,2048]{1,0:T(8,128)(2,1)S(1)} %get-tuple-element.29.dk_ref, bf16[256,2048]{1,0:T(8,128)(2,1)S(1)} %get-tuple-element.30.dv_ref, bf16[1536,3072]{1,0:T(8,128)(2,1)} %wq_hbm.3, ...), custom_call_target="tpu_custom_call" | custom-call | tf_op jit(solution)/shard_map/gradients/pallas_call | solution.py:46
  61.4 0.0 collective-permute-done.1
  61.4 0.1 fusion
  61.5 1.0 %pad_maximum_fusion = bf16[8,264,256]{2,1,0:T(8,128)(2,1)} fusion(bf16[8,72,256]{2,1,0:T(8,128)(2,1)S(1)} %bitcast.7, bf16[8,192,256]{2,1,0:T(8,128)(2,1)S(1)} %get-tuple-element.31), kind=kLoop, calls=%fused_computation | loop fusion | flops 2162688 | bytes 2162688 | tf_op jit(solution)/shard_map/concatenate | solution.py:329
  62.5 3.6 %all-to-all-start.1 = ((bf16[8,264,256]{2,1,0:T(8,128)(2,1)}), bf16[8,264,256]{2,1,0:T(8,128)(2,1)S(1)}, u32[]{:S(2)}, u32[]{:S(2)}) async-start(bf16[8,264,256]{2,1,0:T(8,128)(2,1)} %pad_maximum_fusion), calls=%async_computation.1 | async-start | bytes 2162688 | tf_op jit(solution)/shard_map/all_to_all | solution.py:330
  66.1 1.0 %copy.9 = bf16[256,2048]{1,0:T(8,128)(2,1)} copy(bf16[256,2048]{1,0:T(8,128)(2,1)S(1)} %get-tuple-element.37) | data formatting | bytes 2097152
  67.1 15.1 %all-to-all-done.1.terms_ref = bf16[8,264,256]{2,1,0:T(8,128)(2,1)S(1)} async-done(((bf16[8,264,256]{2,1,0:T(8,128)(2,1)}), bf16[8,264,256]{2,1,0:T(8,128)(2,1)S(1)}, u32[]{:S(2)}, u32[]{:S(2)}) %all-to-all-start.1) | async-done | bytes 1081376 | tf_op jit(solution)/shard_map/all_to_all | solution.py:330
  82.2 0.8 total.1
  (1 shorter events, 0.0 us)
Async XLA Ops:
  28.1 9.5 %collective-permute-start = (bf16[576,256]{1,0:T(8,128)(2,1)S(1)}, bf16[576,256]{1,0:T(8,128)(2,1)S(1)}, u32[]{:S(2)}, u32[]{:S(2)}) collective-permute-start(bf16[576,256]{1,0:T(8,128)(2,1)S(1)} %bitcast.8), channel_id=1, source_target_pairs={{0,8},{8,16},{16,24},{24,32},{32,40},{40,48},{48,56},{56,64},{64,7... | collective-permute-start | bytes 884744 | tf_op jit(solution)/shard_map/ppermute | solution.py:319
  50.0 11.4 %collective-permute-start.1 = (bf16[576,256]{1,0:T(8,128)(2,1)S(1)}, bf16[576,256]{1,0:T(8,128)(2,1)S(1)}, u32[]{:S(2)}, u32[]{:S(2)}) collective-permute-start(bf16[576,256]{1,0:T(8,128)(2,1)S(1)} %get-tuple-element.34), channel_id=1, source_target_pairs={{8,0},{16,8},{24,16},{32,24},{40,32},{48,40},{56,48},{64,56},{72,6... | collective-permute-start | bytes 884744 | tf_op jit(solution)/shard_map/ppermute | solution.py:325
  62.5 19.7 %all-to-all-start.1 = ((bf16[8,264,256]{2,1,0:T(8,128)(2,1)}), bf16[8,264,256]{2,1,0:T(8,128)(2,1)S(1)}, u32[]{:S(2)}, u32[]{:S(2)}) async-start(bf16[8,264,256]{2,1,0:T(8,128)(2,1)} %pad_maximum_fusion), calls=%async_computation.1 | async-start | bytes 2162688 | tf_op jit(solution)/shard_map/all_to_all | solution.py:330

commit v5 on v4

--- a/solution.py
+++ b/solution.py
@@ -35,8 +35,8 @@
     return lax.dot_general(a, b, dims, preferred_element_type=F32)
 
 
-def kernel_call(body, name, out_shape, *args, mib=16, scratch=(), spaces=None):
-    vmem = pl.BlockSpec(memory_space=pltpu.VMEM)
+def kernel_call(body, name, out_shape, *args, mib=16, scratch=(), spaces=None, hbm_outs=0):
+    outs = [pltpu.HBM] * hbm_outs + [pltpu.VMEM] * (len(out_shape) - hbm_outs)
     if spaces is None:
         spaces = [pltpu.VMEM] * len(args)
     args = [
@@ -46,8 +46,8 @@
     return pl.pallas_call(
         body,
         in_specs=[pl.BlockSpec(memory_space=s or pltpu.VMEM) for s in spaces],
-        out_specs=[vmem] * len(out_shape),
-        out_shape=[pltpu.VMEM(shape, dtype) for shape, dtype in out_shape],
+        out_specs=[pl.BlockSpec(memory_space=s) for s in outs],
+        out_shape=[s(shape, dtype) for s, (shape, dtype) in zip(outs, out_shape)],
         scratch_shapes=list(scratch),
         compiler_params=pltpu.CompilerParams(vmem_limit_bytes=mib * MIB),
         name=name,
@@ -69,9 +69,15 @@
     wk_in = pltpu.make_async_copy(wk_hbm, wk_ref, sems.at[P_STEPS])
     wv_in = pltpu.make_async_copy(wv_hbm, wv_ref, sems.at[P_STEPS + 1])
     do_in = pltpu.make_async_copy(do_hbm, do_ref, sems.at[P_STEPS + 2])
-    order = [wk_in, *wq_in[:1], wv_in, *wq_in[1:], do_in]
-    for copy in order:
-        copy.start()
+    order = [wk_in, wq_in[0], wv_in, *wq_in[1:], do_in]
+    order[0].start()
+    order[1].start()
+
+    def arrived(i):
+        order[i].wait()
+        if i + 2 < len(order):
+            order[i + 2].start()
+
     for i in range(PEERS):
         kvt_ref[i * KV_ROWS : (i + 1) * KV_ROWS, :] = g_ref[i, Q_ROWS:, :]
     kv = kvt_ref[:KVL, :].T
@@ -80,7 +86,6 @@
     one = jnp.where(lane == 0, 1.0, 0.0).astype(BF16)
 
     def project_queries(i):
-        wq_in[i].wait()
         queries = mm(qlat, wq_ref[:, part(i)]).astype(BF16)
         for j in range(P_HEADS):
             h = i * P_HEADS + j
@@ -88,14 +93,16 @@
                 [queries[:, j * WIDTH : (j + 1) * WIDTH], one], 1
             )
 
-    wk_in.wait()
+    arrived(0)
     k_ref[...] = mm(kv, wk_ref[...]).astype(BF16)
+    arrived(1)
     project_queries(0)
-    wv_in.wait()
+    arrived(2)
     v_ref[...] = mm(kv, wv_ref[...]).astype(BF16)
     for i in range(1, P_STEPS):
+        arrived(2 + i)
         project_queries(i)
-    do_in.wait()
+    arrived(2 + P_STEPS)
 
 
 def project(g, wq, wk, wv, d_out):
@@ -118,9 +125,20 @@
     )
 
 
-def attend_kernel(lead_ref, kvt_ref, pkvt_ref, q_ref, k_ref, v_ref, do_ref, wk_ref, wv_ref,
-                  out_ref, dqt_ref, dk_ref, dv_ref, early_ref, own_rope_ref,
-                  kp, vp, dkp, dvp):
+def attend_kernel(lead_ref, kvt_ref, pkvt_ref, q_ref, k_ref, v_ref, do_ref, wk_ref, wv_ref, wq_hbm,
+                  out_hbm, dqt_ref, dk_ref, dv_ref, early_ref, own_rope_ref, wq_ref,
+                  kp, vp, dkp, dvp, out_ref, sems):
+    wq_in = pltpu.make_async_copy(wq_hbm, wq_ref, sems.at[O_STEPS])
+    wq_in.start()
+    wide = HEAD_DEV * VDIM // O_STEPS
+    out_copies = [
+        pltpu.make_async_copy(
+            out_ref.at[:, i * wide : (i + 1) * wide],
+            out_hbm.at[:, i * wide : (i + 1) * wide],
+            sems.at[i],
+        )
+        for i in range(O_STEPS)
+    ]
     pkv = pkvt_ref[:KVL, :].T
     kp[...] = mm(pkv, wk_ref[...]).astype(BF16)
     vp[...] = mm(pkv, wv_ref[...]).astype(BF16)
@@ -203,6 +221,8 @@
         dv_ref[:, at] = dv[TOK:]
         rope = dk[:, NOPE:].astype(F32)
         rope_sum[0] = rope if rope_sum[0] is None else rope_sum[0] + rope
+        if (h + 1) % (HEAD_DEV // O_STEPS) == 0:
+            out_copies[h // (HEAD_DEV // O_STEPS)].start()
 
     skewed(head, HEAD_DEV, LAG)
     early_ref[:KVL, :] = (
@@ -211,9 +231,13 @@
     rope_t = rope_sum[0].T
     early_ref[KVL:, :] = rope_t[:ROPE, :TOK].astype(BF16)
     own_rope_ref[...] = rope_t[:ROPE, TOK:]
+    for copy in out_copies:
+        copy.wait()
+    wq_in.wait()
 
 
 LAG = 4
+O_STEPS = 4
 
 
 def skewed(make, count, lag):
@@ -228,7 +252,7 @@
         step += 1
 
 
-def attend(lead, kvt, pkvt, q, k, v, d_out, wk, wv):
+def attend(lead, kvt, pkvt, q, k, v, d_out, wk, wv, wq):
     return kernel_call(
         attend_kernel,
         "attend",
@@ -239,29 +263,25 @@
             ((TOK, HEAD_DEV * VDIM), BF16),
             ((KVL + ROPE, TOK), BF16),
             ((ROPE, TOK), F32),
+            (wq.shape, BF16),
         ],
-        lead, kvt, pkvt, q, k, v, d_out, wk, wv,
-        scratch=[pltpu.VMEM((TOK, HEAD_DEV * NOPE), BF16)] * 4,
-        spaces=[pltpu.SMEM] + [pltpu.VMEM] * 8,
+        lead, kvt, pkvt, q, k, v, d_out, wk, wv, wq,
+        mib=20,
+        scratch=[pltpu.VMEM((TOK, HEAD_DEV * NOPE), BF16)] * 5
+        + [pltpu.SemaphoreType.DMA((O_STEPS + 1,))],
+        spaces=[pltpu.SMEM] + [pltpu.VMEM] * 8 + [pltpu.HBM],
+        hbm_outs=1,
     )
 
 
 G_STEPS = PEERS // 2
 
 
-def gradients_kernel(dqt_ref, dk_ref, dv_ref, wq_hbm, wk_ref, wv_ref,
-                     terms_ref, gkv_ref, wq_ref, sems):
-    part = lambda i: slice(2 * i * Q_ROWS, 2 * (i + 1) * Q_ROWS)
-    wq_in = [
-        pltpu.make_async_copy(wq_hbm.at[part(i), :], wq_ref.at[part(i), :], sems.at[i])
-        for i in range(G_STEPS)
-    ]
-    for copy in wq_in:
-        copy.start()
+def gradients_kernel(dqt_ref, dk_ref, dv_ref, wq_ref, wk_ref, wv_ref, terms_ref, gkv_ref):
     gkv_ref[...] = mm(wk_ref[...], dk_ref[...], NT) + mm(wv_ref[...], dv_ref[...], NT)
     for i in range(G_STEPS):
-        wq_in[i].wait()
-        rows = mm(wq_ref[part(i), :], dqt_ref[...]).astype(BF16)
+        part = slice(2 * i * Q_ROWS, 2 * (i + 1) * Q_ROWS)
+        rows = mm(wq_ref[part, :], dqt_ref[...]).astype(BF16)
         terms_ref[2 * i, :Q_ROWS, :] = rows[:Q_ROWS]
         terms_ref[2 * i + 1, :Q_ROWS, :] = rows[Q_ROWS:]
 
@@ -272,24 +292,8 @@
         "gradients",
         [((PEERS, Q_ROWS, TOK), BF16), ((KVL, TOK), F32)],
         dqt, dk, dv, wq, wk, wv,
-        mib=16,
-        scratch=[pltpu.VMEM(wq.shape, BF16), pltpu.SemaphoreType.DMA((G_STEPS,))],
-        spaces=[pltpu.VMEM] * 3 + [pltpu.HBM] + [pltpu.VMEM] * 2,
-    )
-
-
-def pack_kernel(q_ref, kv_ref, out_ref):
-    for i in range(PEERS):
-        out_ref[i, :Q_ROWS, :] = q_ref[...]
-        out_ref[i, Q_ROWS:, :] = kv_ref[...]
-
-
-def pack(q_t, kv_t):
-    return pl.pallas_call(
-        pack_kernel,
-        out_shape=jax.ShapeDtypeStruct((PEERS, Q_ROWS + KV_ROWS, TOK), BF16),
-        name="pack",
-    )(q_t, kv_t)
+        mib=8,
+    )
 
 
 def total_kernel(terms_ref, q_ref, kv_ref):
@@ -313,17 +317,18 @@
 def on_device(q_latent, kv_latent, w_query, w_key, w_value, d_out):
     peers = lax.axis_size("head")
     blocks = lax.axis_size("ctx")
-    copies = pack(q_latent.T, kv_latent.T)
+    own = jnp.concatenate([q_latent.T, kv_latent.T], 0)
+    copies = jnp.broadcast_to(own, (peers, *own.shape))
     g = lax.all_to_all(copies, "head", 0, 0, tiled=True)
     sent = g[:, Q_ROWS:, :].reshape(KVL + ROPE, TOK)
     pkvt = lax.ppermute(sent, "ctx", [(i, i + 1) for i in range(blocks - 1)])
     q, k, v, kvt, wk_in, wv_in, do_in = project(g, w_query, w_key, w_value, d_out)
     lead = (lax.axis_index("ctx") == 0).astype(jnp.int32).reshape(1)
-    out, dqt, dk, dv, early, own_rope = attend(
-        lead, kvt, pkvt, q, k, v, do_in, wk_in, wv_in
+    out, dqt, dk, dv, early, own_rope, wq_in = attend(
+        lead, kvt, pkvt, q, k, v, do_in, wk_in, wv_in, w_query
     )
     later = lax.ppermute(early, "ctx", [(i, i - 1) for i in range(1, blocks)])
-    gq, gkv = gradients(dqt, dk, dv, w_query, wk_in, wv_in)
+    gq, gkv = gradients(dqt, dk, dv, wq_in, wk_in, wv_in)
     own_kv = jnp.concatenate([gkv, own_rope], 0)
     gkv = (own_kv + later.astype(F32)).astype(BF16)
     terms = jnp.concatenate([gq, gkv.reshape(peers, -1, TOK)], 1)

time: 83.3 us -> 80.5 us (0.966)
  blocking collectives: 25.5 us -> 46.3 us
  waiting for transfers between devices: 15.1 us -> 0.51 us
  Pallas kernels: 30.4 us -> 25.2 us
  starting transfers between devices: 9.12 us -> 5.56 us
  local copies, waits for them, and re-layouts: 0.99 us -> 0.09 us
    all_to_all x0 -> x1, blocking collectives: none -> 20.9 us  [on_device(): terms = lax.all_to_all(terms, 'head', 0, 0, tiled=True)]
    all_to_all x1 -> x0, waiting for transfers between devices: 15.1 us -> none  [on_device(): terms = lax.all_to_all(terms, 'head', 0, 0, tiled=True)]
    all_to_all x1 -> x0, starting transfers between devices: 3.56 us -> none  [on_device(): terms = lax.all_to_all(terms, 'head', 0, 0, tiled=True)]
    pallas_call x3, Pallas kernels: 27.7 us -> 24.4 us  [kernel_call(): pl.pallas_call(body, in_specs=[pl.BlockSpec(memory_space=s or pltpu.VMEM)...]
    pallas_call x1 -> x0, Pallas kernels: 1.94 us -> none  [pack(): pl.pallas_call(pack_kernel, out_shape=jax.ShapeDtypeStruct((PEERS, Q_ROWS...]
    unnamed x1 -> x0, local copies, waits for them, and re-layouts: 0.97 us -> none
    concatenate x1, other arithmetic: 1.04 us -> 0.07 us  [on_device(): terms = jnp.concatenate([gq, gkv.reshape(peers, -1, TOK)], 1)]
    concatenate x0 -> x1, other arithmetic: none -> 0.93 us  [on_device(): own = jnp.concatenate([q_latent.T, kv_latent.T], 0)]
  transfers between devices with their start and end apart: 3 -> 2, of which waited for: 1 -> 1; matrix products, arithmetic and copies ran while one was open for 1% -> 0% of each run, Pallas kernels for 18% -> 14%
where the time goes in v5:
time: 80.5 us; the launch traced here: 79.4 us
  blocking collectives  46.3 us (58%)
  Pallas kernels  25.2 us (31%)
  starting transfers between devices  5.56 us (7%)
  other arithmetic  1.07 us (1%)
    all_to_all x1, blocking collectives, on_device(): g = lax.all_to_all(copies, 'head', 0, 0, tiled=True)  25.3 us
    pallas_call x3, Pallas kernels, kernel_call(): pl.pallas_call(body, in_specs=[pl.BlockSpec(memory_space=s or pltpu.VMEM)...  24.4 us
    all_to_all x1, blocking collectives, on_device(): terms = lax.all_to_all(terms, 'head', 0, 0, tiled=True)  20.9 us
    ppermute x1, starting transfers between devices, on_device(): later = lax.ppermute(early, 'ctx', [(i, i - 1) for i in range(1, blocks)])  3.64 us
    ppermute x1, starting transfers between devices, on_device(): pkvt = lax.ppermute(sent, 'ctx', [(i, i + 1) for i in range(blocks - 1)])  1.92 us
  transfers between devices with their start and end apart: 2, of which 1 were waited for; matrix products, arithmetic and copies ran while one was open for 0% of the time, Pallas kernels for 14%

profile of v5, /device:TPU:16, one launch (start us, length us, event | category | flops | bytes accessed | tf_op | source)
XLA Modules:
  0.0 79.4 jit_solution(14249049310807986005)
XLA Ops:
  0.6 0.9 %pad_maximum_fusion.1 = bf16[264,256]{1,0:T(8,128)(2,1)S(1)} fusion(bf16[72,256]{1,0:T(8,128)(2,1)} %bitcast.10, bf16[192,256]{1,0:T(8,128)(2,1)} %bitcast.9), kind=kLoop, calls=%fused_computation.3 | loop fusion | flops 270336 | bytes 270336 | tf_op jit(solution)/shard_map/concatenate | solution.py:320
  1.6 0.1 broadcast_in_dim.3
  1.6 25.3 %all_to_all.10.g_ref = bf16[8,264,256]{2,1,0:T(8,128)(2,1)S(1)} all-to-all(bf16[8,264,256]{2,1,0:T(8,128)(2,1)S(1)} %broadcast_in_dim.3), channel_id=1, replica_groups=mesh['ctx'=16,'head'=8] {'head'}, dimensions={0} | all-to-all | bytes 2162688 | tf_op jit(solution)/shard_map/all_to_all | solution.py:322
  27.0 1.9 %collective-permute-start = (bf16[576,256]{1,0:T(8,128)(2,1)S(1)}, bf16[576,256]{1,0:T(8,128)(2,1)S(1)}, u32[]{:S(2)}, u32[]{:S(2)}) collective-permute-start(bf16[576,256]{1,0:T(8,128)(2,1)S(1)} %bitcast.8), channel_id=1, source_target_pairs={{0,8},{8,16},{16,24},{24,32},{32,40},{40,48},{48,56},{56,64},{64,7... | collective-permute-start | bytes 884744 | tf_op jit(solution)/shard_map/ppermute | solution.py:324
  28.9 7.5 %project.1 = (bf16[256,4096]{1,0:T(8,128)(2,1)S(1)}, bf16[256,2048]{1,0:T(8,128)(2,1)S(1)}, bf16[256,2048]{1,0:T(8,128)(2,1)S(1)}, bf16[576,256]{1,0:T(8,128)(2,...) custom-call(bf16[8,264,256]{2,1,0:T(8,128)(2,1)S(1)} %all_to_all.10.g_ref, ...), custom_call_target="tpu_custom_call" | custom-call | tf_op jit(solution)/shard_map/project/pallas_call | solution.py:46
  36.5 0.0 collective-permute-done.pkvt_ref
  36.5 13.1 %attend.1 = (bf16[256,2048]{1,0:T(8,128)(2,1)}, bf16[3072,256]{1,0:T(8,128)(2,1)S(1)}, bf16[256,2048]{1,0:T(8,128)(2,1)S(1)}, bf16[256,2048]{1,0:T(8,128)(2,1)S(...) custom-call(s32[1]{0:T(128)} %bitcast.lead_ref, ...), custom_call_target="tpu_custom_call" | custom-call | tf_op jit(solution)/shard_map/attend/pallas_call | solution.py:46
  49.6 3.6 %collective-permute-start.1 = (bf16[576,256]{1,0:T(8,128)(2,1)S(1)}, bf16[576,256]{1,0:T(8,128)(2,1)S(1)}, u32[]{:S(2)}, u32[]{:S(2)}) collective-permute-start(bf16[576,256]{1,0:T(8,128)(2,1)S(1)} %get-tuple-element.36), channel_id=1, source_target_pairs={{8,0},{16,8},{24,16},{32,24},{40,32},{48,40},{56,48},{64,56},{72,6... | collective-permute-start | bytes 884744 | tf_op jit(solution)/shard_map/ppermute | solution.py:330
  53.3 3.7 %gradients.1 = (bf16[8,192,256]{2,1,0:T(8,128)(2,1)S(1)}, f32[512,256]{1,0:T(8,128)S(1)}) custom-call(bf16[3072,256]{1,0:T(8,128)(2,1)S(1)} %get-tuple-element.29.dqt_ref, bf16[256,2048]{1,0:T(8,128)(2,1)S(1)} %get-tuple-element.30.dk_ref, bf16[256,2048]{1,0:T(8,128)(2,1)S(1)} %get-tuple-element.31.dv_ref, bf16[1536,3072]{1,0:T(8,128)(2,1)S(1)} %get-tuple-element.32.wq_ref, ...), custom_call_target="tpu_custom_call" | custom-call | tf_op jit(solution)/shard_map/gradients/pallas_call | solution.py:46
  57.0 0.5 collective-permute-done.1
  57.5 0.1 fusion
  57.6 0.1 pad_maximum_fusion
  57.7 20.9 %all_to_all.11.terms_ref = bf16[8,264,256]{2,1,0:T(8,128)(2,1)S(1)} all-to-all(bf16[8,264,256]{2,1,0:T(8,128)(2,1)S(1)} %pad_maximum_fusion), channel_id=1, replica_groups=mesh['ctx'=16,'head'=8] {'head'}, dimensions={0} | all-to-all | bytes 2162688 | tf_op jit(solution)/shard_map/all_to_all | solution.py:335
  78.6 0.8 %total.1 = (f32[192,256]{1,0:T(8,128)}, f32[72,256]{1,0:T(8,128)}) custom-call(bf16[8,264,256]{2,1,0:T(8,128)(2,1)S(1)} %all_to_all.11.terms_ref), custom_call_target="tpu_custom_call" | custom-call | tf_op jit(solution)/shard_map/total/pallas_call | solution.py:306
  (1 shorter events, 0.0 us)
Async XLA Ops:
  27.0 9.5 %collective-permute-start = (bf16[576,256]{1,0:T(8,128)(2,1)S(1)}, bf16[576,256]{1,0:T(8,128)(2,1)S(1)}, u32[]{:S(2)}, u32[]{:S(2)}) collective-permute-start(bf16[576,256]{1,0:T(8,128)(2,1)S(1)} %bitcast.8), channel_id=1, source_target_pairs={{0,8},{8,16},{16,24},{24,32},{32,40},{40,48},{48,56},{56,64},{64,7... | collective-permute-start | bytes 884744 | tf_op jit(solution)/shard_map/ppermute | solution.py:324
  49.6 7.9 %collective-permute-start.1 = (bf16[576,256]{1,0:T(8,128)(2,1)S(1)}, bf16[576,256]{1,0:T(8,128)(2,1)S(1)}, u32[]{:S(2)}, u32[]{:S(2)}) collective-permute-start(bf16[576,256]{1,0:T(8,128)(2,1)S(1)} %get-tuple-element.36), channel_id=1, source_target_pairs={{8,0},{16,8},{24,16},{32,24},{40,32},{48,40},{56,48},{64,56},{72,6... | collective-permute-start | bytes 884744 | tf_op jit(solution)/shard_map/ppermute | solution.py:330

commit v6 on v5

--- a/solution.py
+++ b/solution.py
@@ -126,8 +126,8 @@
 
 
 def attend_kernel(lead_ref, kvt_ref, pkvt_ref, q_ref, k_ref, v_ref, do_ref, wk_ref, wv_ref, wq_hbm,
-                  out_hbm, dqt_ref, dk_ref, dv_ref, early_ref, own_rope_ref, wq_ref,
-                  kp, vp, dkp, dvp, out_ref, sems):
+                  out_hbm, ds_ref, po_ref, kp, early_ref, wq_ref,
+                  vp, dkp, dvp, out_ref, sems):
     wq_in = pltpu.make_async_copy(wq_hbm, wq_ref, sems.at[O_STEPS])
     wq_in.start()
     wide = HEAD_DEV * VDIM // O_STEPS
@@ -208,17 +208,14 @@
         d_b = (p_b * ((dprob[TOK + HALF :, HALF:] - row_dot[:, HALF:]) * SCALE)).astype(BF16)
         dscore = jnp.concatenate([d_p, d_a, jnp.concatenate([none, d_b], 1)], 0)
         yield
-        dqt = mm(jnp.concatenate([keys.T, ropes_t], 0), dscore)
-        dk = mm(dscore, q)
-        dv = mm(probs, d_out_h)
-        yield
-        dqt_ref[h * WIDTH : (h + 1) * WIDTH, :] = dqt.astype(BF16)
+        ds_ref[h] = dscore
+        po_ref[h] = probs[TOK:]
+        dk = mm(dscore[:TOK], q)
+        dv = mm(probs[:TOK], d_out_h)
+        yield
         dk = dk.astype(BF16)
-        dv = dv.astype(BF16)
-        dkp[:, at] = dk[:TOK, :NOPE]
-        dvp[:, at] = dv[:TOK]
-        dk_ref[:, at] = dk[TOK:, :NOPE]
-        dv_ref[:, at] = dv[TOK:]
+        dkp[:, at] = dk[:, :NOPE]
+        dvp[:, at] = dv.astype(BF16)
         rope = dk[:, NOPE:].astype(F32)
         rope_sum[0] = rope if rope_sum[0] is None else rope_sum[0] + rope
         if (h + 1) % (HEAD_DEV // O_STEPS) == 0:
@@ -228,9 +225,7 @@
     early_ref[:KVL, :] = (
         mm(wk_ref[...], dkp[...], NT) + mm(wv_ref[...], dvp[...], NT)
     ).astype(BF16)
-    rope_t = rope_sum[0].T
-    early_ref[KVL:, :] = rope_t[:ROPE, :TOK].astype(BF16)
-    own_rope_ref[...] = rope_t[:ROPE, TOK:]
+    early_ref[KVL:, :] = rope_sum[0].T[:ROPE].astype(BF16)
     for copy in out_copies:
         copy.wait()
     wq_in.wait()
@@ -258,16 +253,15 @@
         "attend",
         [
             ((TOK, HEAD_DEV * VDIM), BF16),
-            ((HEAD_DEV * WIDTH, TOK), BF16),
+            ((HEAD_DEV, 2 * TOK, TOK), BF16),
+            ((HEAD_DEV, TOK, TOK), BF16),
             ((TOK, HEAD_DEV * NOPE), BF16),
-            ((TOK, HEAD_DEV * VDIM), BF16),
             ((KVL + ROPE, TOK), BF16),
-            ((ROPE, TOK), F32),
             (wq.shape, BF16),
         ],
         lead, kvt, pkvt, q, k, v, d_out, wk, wv, wq,
         mib=20,
-        scratch=[pltpu.VMEM((TOK, HEAD_DEV * NOPE), BF16)] * 5
+        scratch=[pltpu.VMEM((TOK, HEAD_DEV * NOPE), BF16)] * 4
         + [pltpu.SemaphoreType.DMA((O_STEPS + 1,))],
         spaces=[pltpu.SMEM] + [pltpu.VMEM] * 8 + [pltpu.HBM],
         hbm_outs=1,
@@ -277,22 +271,41 @@
 G_STEPS = PEERS // 2
 
 
-def gradients_kernel(dqt_ref, dk_ref, dv_ref, wq_ref, wk_ref, wv_ref, terms_ref, gkv_ref):
-    gkv_ref[...] = mm(wk_ref[...], dk_ref[...], NT) + mm(wv_ref[...], dv_ref[...], NT)
+def gradients_kernel(ds_ref, po_ref, kp_ref, k_ref, kvt_ref, pkvt_ref, q_ref, do_ref,
+                     wq_ref, wk_ref, wv_ref, terms_ref, gkv_ref, dqt, dko, dvo):
+    ropes_t = jnp.concatenate([pkvt_ref[KVL:, :], kvt_ref[KVL:, :]], 1)
+    rope_sum = None
+    for h in range(HEAD_DEV):
+        at = slice(h * NOPE, (h + 1) * NOPE)
+        keys_t = jnp.concatenate([kp_ref[:, at], k_ref[:, at]], 0).T
+        dqt[h * WIDTH : (h + 1) * WIDTH, :] = mm(
+            jnp.concatenate([keys_t, ropes_t], 0), ds_ref[h]
+        ).astype(BF16)
+        dk = mm(ds_ref[h, TOK:, :], q_ref[:, h * PAD : (h + 1) * PAD]).astype(BF16)
+        dko[:, at] = dk[:, :NOPE]
+        dvo[:, at] = mm(po_ref[h], do_ref[:, at]).astype(BF16)
+        rope = dk[:, NOPE:].astype(F32)
+        rope_sum = rope if rope_sum is None else rope_sum + rope
+    gkv_ref[:KVL, :] = mm(wk_ref[...], dko[...], NT) + mm(wv_ref[...], dvo[...], NT)
+    gkv_ref[KVL:, :] = rope_sum.T[:ROPE]
     for i in range(G_STEPS):
         part = slice(2 * i * Q_ROWS, 2 * (i + 1) * Q_ROWS)
-        rows = mm(wq_ref[part, :], dqt_ref[...]).astype(BF16)
+        rows = mm(wq_ref[part, :], dqt[...]).astype(BF16)
         terms_ref[2 * i, :Q_ROWS, :] = rows[:Q_ROWS]
         terms_ref[2 * i + 1, :Q_ROWS, :] = rows[Q_ROWS:]
 
 
-def gradients(dqt, dk, dv, wq, wk, wv):
+def gradients(ds, po, kp, k, kvt, pkvt, q, d_out, wq, wk, wv):
     return kernel_call(
         gradients_kernel,
         "gradients",
-        [((PEERS, Q_ROWS, TOK), BF16), ((KVL, TOK), F32)],
-        dqt, dk, dv, wq, wk, wv,
-        mib=8,
+        [((PEERS, Q_ROWS, TOK), BF16), ((KVL + ROPE, TOK), F32)],
+        ds, po, kp, k, kvt, pkvt, q, d_out, wq, wk, wv,
+        scratch=[
+            pltpu.VMEM((HEAD_DEV * WIDTH, TOK), BF16),
+            pltpu.VMEM((TOK, HEAD_DEV * NOPE), BF16),
+            pltpu.VMEM((TOK, HEAD_DEV * VDIM), BF16),
+        ],
     )
 
 
@@ -324,13 +337,14 @@
     pkvt = lax.ppermute(sent, "ctx", [(i, i + 1) for i in range(blocks - 1)])
     q, k, v, kvt, wk_in, wv_in, do_in = project(g, w_query, w_key, w_value, d_out)
     lead = (lax.axis_index("ctx") == 0).astype(jnp.int32).reshape(1)
-    out, dqt, dk, dv, early, own_rope, wq_in = attend(
+    out, ds, po, kp, early, wq_in = attend(
         lead, kvt, pkvt, q, k, v, do_in, wk_in, wv_in, w_query
     )
     later = lax.ppermute(early, "ctx", [(i, i - 1) for i in range(1, blocks)])
-    gq, gkv = gradients(dqt, dk, dv, wq_in, wk_in, wv_in)
-    own_kv = jnp.concatenate([gkv, own_rope], 0)
-    gkv = (own_kv + later.astype(F32)).astype(BF16)
+    gq, gkv = gradients(
+        ds, po, kp, k, kvt, pkvt, q, do_in, wq_in, wk_in, wv_in
+    )
+    gkv = (gkv + later.astype(F32)).astype(BF16)
     terms = jnp.concatenate([gq, gkv.reshape(peers, -1, TOK)], 1)
     terms = lax.all_to_all(terms, "head", 0, 0, tiled=True)
     gq, gkv = total(terms)

time: 80.5 us -> 81 us (level)
  Pallas kernels: 25.2 us -> 26.4 us
    pallas_call x3, Pallas kernels: 24.4 us -> 25.6 us  [kernel_call(): pl.pallas_call(body, in_specs=[pl.BlockSpec(memory_space=s or pltpu.VMEM)...]
  transfers between devices with their start and end apart: 2 -> 2, of which waited for: 1 -> 0; matrix products, arithmetic and copies ran while one was open for 0% -> 0% of each run, Pallas kernels for 14% -> 17%
where the time goes in v6:
time: 81 us; the launch traced here: 79.9 us
  blocking collectives  46 us (57%)
  Pallas kernels  26.4 us (33%)
  starting transfers between devices  5.56 us (7%)
  other arithmetic  1.07 us (1%)
    pallas_call x3, Pallas kernels, kernel_call(): pl.pallas_call(body, in_specs=[pl.BlockSpec(memory_space=s or pltpu.VMEM)...  25.6 us
    all_to_all x1, blocking collectives, on_device(): g = lax.all_to_all(copies, 'head', 0, 0, tiled=True)  25.3 us
    all_to_all x1, blocking collectives, on_device(): terms = lax.all_to_all(terms, 'head', 0, 0, tiled=True)  20.7 us
    ppermute x1, starting transfers between devices, on_device(): later = lax.ppermute(early, 'ctx', [(i, i - 1) for i in range(1, blocks)])  3.64 us
    ppermute x1, starting transfers between devices, on_device(): pkvt = lax.ppermute(sent, 'ctx', [(i, i + 1) for i in range(blocks - 1)])  1.92 us
  transfers between devices with their start and end apart: 2, of which 0 were waited for; matrix products, arithmetic and copies ran while one was open for 0% of the time, Pallas kernels for 17%

profile of v6, /device:TPU:16, one launch (start us, length us, event | category | flops | bytes accessed | tf_op | source)
XLA Modules:
  0.0 79.9 jit_solution(7571913422937512797)
XLA Ops:
  0.6 0.9 %pad_maximum_fusion.1 = bf16[264,256]{1,0:T(8,128)(2,1)S(1)} fusion(bf16[72,256]{1,0:T(8,128)(2,1)} %bitcast.10, bf16[192,256]{1,0:T(8,128)(2,1)} %bitcast.9), kind=kLoop, calls=%fused_computation.2 | loop fusion | flops 270336 | bytes 270336 | tf_op jit(solution)/shard_map/concatenate | solution.py:333
  1.6 0.1 broadcast_in_dim.3
  1.6 25.3 %all_to_all.10.g_ref = bf16[8,264,256]{2,1,0:T(8,128)(2,1)S(1)} all-to-all(bf16[8,264,256]{2,1,0:T(8,128)(2,1)S(1)} %broadcast_in_dim.3), channel_id=1, replica_groups=mesh['ctx'=16,'head'=8] {'head'}, dimensions={0} | all-to-all | bytes 2162688 | tf_op jit(solution)/shard_map/all_to_all | solution.py:335
  27.0 1.9 %collective-permute-start = (bf16[576,256]{1,0:T(8,128)(2,1)S(1)}, bf16[576,256]{1,0:T(8,128)(2,1)S(1)}, u32[]{:S(2)}, u32[]{:S(2)}) collective-permute-start(bf16[576,256]{1,0:T(8,128)(2,1)S(1)} %bitcast.8), channel_id=1, source_target_pairs={{0,8},{8,16},{16,24},{24,32},{32,40},{40,48},{48,56},{56,64},{64,7... | collective-permute-start | bytes 884744 | tf_op jit(solution)/shard_map/ppermute | solution.py:337
  28.9 7.5 %project.1 = (bf16[256,4096]{1,0:T(8,128)(2,1)S(1)}, bf16[256,2048]{1,0:T(8,128)(2,1)S(1)}, bf16[256,2048]{1,0:T(8,128)(2,1)S(1)}, bf16[576,256]{1,0:T(8,128)(2,...) custom-call(bf16[8,264,256]{2,1,0:T(8,128)(2,1)S(1)} %all_to_all.10.g_ref, ...), custom_call_target="tpu_custom_call" | custom-call | tf_op jit(solution)/shard_map/project/pallas_call | solution.py:46
  36.5 0.0 collective-permute-done.pkvt_ref
  36.5 12.4 %attend.1 = (bf16[256,2048]{1,0:T(8,128)(2,1)}, bf16[16,512,256]{2,1,0:T(8,128)(2,1)S(1)}, bf16[16,256,256]{2,1,0:T(8,128)(2,1)S(1)}, bf16[256,2048]{1,0:T(8,128...) custom-call(s32[1]{0:T(128)} %bitcast.lead_ref, ...), custom_call_target="tpu_custom_call" | custom-call | tf_op jit(solution)/shard_map/attend/pallas_call | solution.py:46
  48.9 3.6 %collective-permute-start.1 = (bf16[576,256]{1,0:T(8,128)(2,1)S(1)}, bf16[576,256]{1,0:T(8,128)(2,1)S(1)}, u32[]{:S(2)}, u32[]{:S(2)}) collective-permute-start(bf16[576,256]{1,0:T(8,128)(2,1)S(1)} %get-tuple-element.34), channel_id=1, source_target_pairs={{8,0},{16,8},{24,16},{32,24},{40,32},{48,40},{56,48},{64,56},{72,6... | collective-permute-start | bytes 884744 | tf_op jit(solution)/shard_map/ppermute | solution.py:343
  52.6 5.7 %gradients.1 = (bf16[8,192,256]{2,1,0:T(8,128)(2,1)S(1)}, f32[576,256]{1,0:T(8,128)S(1)}) custom-call(bf16[16,512,256]{2,1,0:T(8,128)(2,1)S(1)} %get-tuple-element.28.ds_ref, bf16[16,256,256]{2,1,0:T(8,128)(2,1)S(1)} %get-tuple-element.29.po_ref, bf16[256,2048]{1,0:T(8,128)(2,1)S(1)} %get-tuple-element.30.kp_ref, ...), custom_call_target="tpu_custom_call" | custom-call | tf_op jit(solution)/shard_map/gradients/pallas_call | solution.py:46
  58.3 0.0 collective-permute-done.1
  58.3 0.1 add_convert_fusion
  58.3 0.1 pad_maximum_fusion
  58.4 20.7 %all_to_all.11.terms_ref = bf16[8,264,256]{2,1,0:T(8,128)(2,1)S(1)} all-to-all(bf16[8,264,256]{2,1,0:T(8,128)(2,1)S(1)} %pad_maximum_fusion), channel_id=1, replica_groups=mesh['ctx'=16,'head'=8] {'head'}, dimensions={0} | all-to-all | bytes 2162688 | tf_op jit(solution)/shard_map/all_to_all | solution.py:349
  79.1 0.8 total.1
  (1 shorter events, 0.0 us)
Async XLA Ops:
  27.0 9.5 %collective-permute-start = (bf16[576,256]{1,0:T(8,128)(2,1)S(1)}, bf16[576,256]{1,0:T(8,128)(2,1)S(1)}, u32[]{:S(2)}, u32[]{:S(2)}) collective-permute-start(bf16[576,256]{1,0:T(8,128)(2,1)S(1)} %bitcast.8), channel_id=1, source_target_pairs={{0,8},{8,16},{16,24},{24,32},{32,40},{40,48},{48,56},{56,64},{64,7... | collective-permute-start | bytes 884744 | tf_op jit(solution)/shard_map/ppermute | solution.py:337
  48.9 9.3 %collective-permute-start.1 = (bf16[576,256]{1,0:T(8,128)(2,1)S(1)}, bf16[576,256]{1,0:T(8,128)(2,1)S(1)}, u32[]{:S(2)}, u32[]{:S(2)}) collective-permute-start(bf16[576,256]{1,0:T(8,128)(2,1)S(1)} %get-tuple-element.34), channel_id=1, source_target_pairs={{8,0},{16,8},{24,16},{32,24},{40,32},{48,40},{56,48},{64,56},{72,6... | collective-permute-start | bytes 884744 | tf_op jit(solution)/shard_map/ppermute | solution.py:343

commit v7 on v6

--- a/solution.py
+++ b/solution.py
@@ -58,18 +58,16 @@
 P_STEPS = HEAD_DEV // P_HEADS
 
 
-def project_kernel(g_ref, wq_hbm, wk_hbm, wv_hbm, do_hbm,
-                   q_ref, k_ref, v_ref, kvt_ref, wk_ref, wv_ref, do_ref, wq_ref, sems):
+def project_kernel(g_ref, wq_hbm, wk_ref, wv_hbm,
+                   q_ref, k_ref, v_ref, kvt_ref, wv_ref, wq_ref, sems):
     cols = P_HEADS * WIDTH
     part = lambda i: slice(i * cols, (i + 1) * cols)
     wq_in = [
         pltpu.make_async_copy(wq_hbm.at[:, part(i)], wq_ref.at[:, part(i)], sems.at[i])
         for i in range(P_STEPS)
     ]
-    wk_in = pltpu.make_async_copy(wk_hbm, wk_ref, sems.at[P_STEPS])
-    wv_in = pltpu.make_async_copy(wv_hbm, wv_ref, sems.at[P_STEPS + 1])
-    do_in = pltpu.make_async_copy(do_hbm, do_ref, sems.at[P_STEPS + 2])
-    order = [wk_in, wq_in[0], wv_in, *wq_in[1:], do_in]
+    wv_in = pltpu.make_async_copy(wv_hbm, wv_ref, sems.at[P_STEPS])
+    order = [wq_in[0], wv_in, *wq_in[1:]]
     order[0].start()
     order[1].start()
 
@@ -93,19 +91,17 @@
                 [queries[:, j * WIDTH : (j + 1) * WIDTH], one], 1
             )
 
+    k_ref[...] = mm(kv, wk_ref[...]).astype(BF16)
     arrived(0)
-    k_ref[...] = mm(kv, wk_ref[...]).astype(BF16)
+    project_queries(0)
     arrived(1)
-    project_queries(0)
-    arrived(2)
     v_ref[...] = mm(kv, wv_ref[...]).astype(BF16)
     for i in range(1, P_STEPS):
-        arrived(2 + i)
+        arrived(1 + i)
         project_queries(i)
-    arrived(2 + P_STEPS)
-
-
-def project(g, wq, wk, wv, d_out):
+
+
+def project(g, wq, wk, wv):
     return kernel_call(
         project_kernel,
         "project",
@@ -114,14 +110,12 @@
             ((TOK, HEAD_DEV * NOPE), BF16),
             ((TOK, HEAD_DEV * VDIM), BF16),
             ((KVL + ROPE, TOK), BF16),
-            (wk.shape, BF16),
             (wv.shape, BF16),
-            (d_out.shape, BF16),
         ],
-        g, wq, wk, wv, d_out,
+        g, wq, wk, wv,
         mib=20,
-        scratch=[pltpu.VMEM(wq.shape, BF16), pltpu.SemaphoreType.DMA((P_STEPS + 3,))],
-        spaces=[None] + [pltpu.HBM] * 4,
+        scratch=[pltpu.VMEM(wq.shape, BF16), pltpu.SemaphoreType.DMA((P_STEPS + 1,))],
+        spaces=[None, pltpu.HBM, pltpu.VMEM, pltpu.HBM],
     )
 
 
@@ -186,26 +180,26 @@
         )
         yield
         inv = 1.0 / total
-        p_p, p_a, p_b = e_p * inv, e_a * inv, e_b * inv[:, HALF:]
+        invs = inv * SCALE
         none = jnp.zeros((HALF, HALF), BF16)
         probs = jnp.concatenate(
             [
-                p_p.astype(BF16),
-                p_a.astype(BF16),
-                jnp.concatenate([none, p_b.astype(BF16)], 1),
+                (e_p * inv).astype(BF16),
+                (e_a * inv).astype(BF16),
+                jnp.concatenate([none, (e_b * inv[:, HALF:]).astype(BF16)], 1),
             ],
             0,
         )
         yield
         out_t = mm(vals.T, probs).astype(BF16)
-        dprob = mm(vals, d_out_t)
         yield
         out_ref[:, at] = out_t.T
         row_dot = jnp.sum(d_out_t.astype(F32) * out_t.astype(F32), 0, keepdims=True)
         yield
-        d_p = (p_p * ((dprob[:TOK] - row_dot) * SCALE)).astype(BF16)
-        d_a = (p_a * ((dprob[TOK : TOK + HALF] - row_dot) * SCALE)).astype(BF16)
-        d_b = (p_b * ((dprob[TOK + HALF :, HALF:] - row_dot[:, HALF:]) * SCALE)).astype(BF16)
+        dprob = mm(vals, d_out_t)
+        d_p = (e_p * invs * (dprob[:TOK] - row_dot)).astype(BF16)
+        d_a = (e_a * invs * (dprob[TOK : TOK + HALF] - row_dot)).astype(BF16)
+        d_b = (e_b * invs[:, HALF:] * (dprob[TOK + HALF :, HALF:] - row_dot[:, HALF:])).astype(BF16)
         dscore = jnp.concatenate([d_p, d_a, jnp.concatenate([none, d_b], 1)], 0)
         yield
         ds_ref[h] = dscore
@@ -231,7 +225,7 @@
     wq_in.wait()
 
 
-LAG = 4
+LAG = 1
 O_STEPS = 4
 
 
@@ -243,7 +237,7 @@
         if made < count and step % lag == 0:
             running.append(make(made))
             made += 1
-        running = [r for r in running if next(r, True) is None]
+        running = [r for r in running[::-1] if next(r, True) is None][::-1]
         step += 1
 
 
@@ -335,14 +329,14 @@
     g = lax.all_to_all(copies, "head", 0, 0, tiled=True)
     sent = g[:, Q_ROWS:, :].reshape(KVL + ROPE, TOK)
     pkvt = lax.ppermute(sent, "ctx", [(i, i + 1) for i in range(blocks - 1)])
-    q, k, v, kvt, wk_in, wv_in, do_in = project(g, w_query, w_key, w_value, d_out)
+    q, k, v, kvt, wv_in = project(g, w_query, w_key, w_value)
     lead = (lax.axis_index("ctx") == 0).astype(jnp.int32).reshape(1)
     out, ds, po, kp, early, wq_in = attend(
-        lead, kvt, pkvt, q, k, v, do_in, wk_in, wv_in, w_query
+        lead, kvt, pkvt, q, k, v, d_out, w_key, wv_in, w_query
     )
     later = lax.ppermute(early, "ctx", [(i, i - 1) for i in range(1, blocks)])
     gq, gkv = gradients(
-        ds, po, kp, k, kvt, pkvt, q, do_in, wq_in, wk_in, wv_in
+        ds, po, kp, k, kvt, pkvt, q, d_out, wq_in, w_key, wv_in
     )
     gkv = (gkv + later.astype(F32)).astype(BF16)
     terms = jnp.concatenate([gq, gkv.reshape(peers, -1, TOK)], 1)

time: 81 us -> 79.5 us (0.981)
  Pallas kernels: 26.4 us -> 24 us
    pallas_call x3, Pallas kernels: 25.6 us -> 23.2 us  [kernel_call(): pl.pallas_call(body, in_specs=[pl.BlockSpec(memory_space=s or pltpu.VMEM)...]
where the time goes in v7:
time: 79.5 us; the launch traced here: 78.4 us
  blocking collectives  46 us (58%)
  Pallas kernels  24 us (30%)
  starting transfers between devices  5.55 us (7%)
  other arithmetic  1.21 us (2%)
  local copies, waits for them, and re-layouts  0.82 us (1%)
    all_to_all x1, blocking collectives, on_device(): g = lax.all_to_all(copies, 'head', 0, 0, tiled=True)  25.3 us
    pallas_call x3, Pallas kernels, kernel_call(): pl.pallas_call(body, in_specs=[pl.BlockSpec(memory_space=s or pltpu.VMEM)...  23.2 us
    all_to_all x1, blocking collectives, on_device(): terms = lax.all_to_all(terms, 'head', 0, 0, tiled=True)  20.7 us
    ppermute x1, starting transfers between devices, on_device(): later = lax.ppermute(early, 'ctx', [(i, i - 1) for i in range(1, blocks)])  3.64 us
    ppermute x1, starting transfers between devices, on_device(): pkvt = lax.ppermute(sent, 'ctx', [(i, i + 1) for i in range(blocks - 1)])  1.91 us
  transfers between devices with their start and end apart: 2, of which 0 were waited for; matrix products, arithmetic and copies ran while one was open for 0% of the time, Pallas kernels for 17%

profile of v7, /device:TPU:16, one launch (start us, length us, event | category | flops | bytes accessed | tf_op | source)
XLA Modules:
  0.0 78.4 jit_solution(3607742993673159783)
XLA Ops:
  0.6 0.0 copy-start
  0.6 1.1 %pad_maximum_fusion.1 = bf16[264,256]{1,0:T(8,128)(2,1)S(1)} fusion(bf16[72,256]{1,0:T(8,128)(2,1)} %bitcast.9, bf16[192,256]{1,0:T(8,128)(2,1)} %bitcast.8), kind=kLoop, calls=%fused_computation.2 | loop fusion | flops 270336 | bytes 270336 | tf_op jit(solution)/shard_map/concatenate | solution.py:327
  1.7 0.1 broadcast_in_dim.3
  1.8 25.3 %all_to_all.10.g_ref = bf16[8,264,256]{2,1,0:T(8,128)(2,1)S(1)} all-to-all(bf16[8,264,256]{2,1,0:T(8,128)(2,1)S(1)} %broadcast_in_dim.3), channel_id=1, replica_groups=mesh['ctx'=16,'head'=8] {'head'}, dimensions={0} | all-to-all | bytes 2162688 | tf_op jit(solution)/shard_map/all_to_all | solution.py:329
  27.1 0.7 slice.4
  27.9 1.9 %collective-permute-start = (bf16[576,256]{1,0:T(8,128)(2,1)}, bf16[576,256]{1,0:T(8,128)(2,1)S(1)}, u32[]{:S(2)}, u32[]{:S(2)}) collective-permute-start(bf16[576,256]{1,0:T(8,128)(2,1)} %bitcast.3), channel_id=1, source_target_pairs={{0,8},{8,16},{16,24},{24,32},{32,40},{40,48},{48,56},{56,64},{64,7... | collective-permute-start | bytes 884744 | tf_op jit(solution)/shard_map/ppermute | solution.py:331
  29.8 0.0 copy-done
  29.8 0.0 copy-start.1
  29.8 7.5 %project.1 = (bf16[256,4096]{1,0:T(8,128)(2,1)S(1)}, bf16[256,2048]{1,0:T(8,128)(2,1)S(1)}, bf16[256,2048]{1,0:T(8,128)(2,1)S(1)}, bf16[576,256]{1,0:T(8,128)(2,1)S(1)}, bf16[512,2048]{1,0:T(8,128)(2,1)S(1)}) custom-call(bf16[8,264,256]{2,1,0:T(8,128)(2,1)S(1)} %all_to_all.10.g_ref, bf16[1536,3072]{1,0:T(8,128)(2,1)} %wq_hbm.3, ...), custom_call_target="tpu_custom_call" | custom-call | tf_op jit(solution)/shard_map/project/pallas_call | solution.py:46
  37.3 0.0 collective-permute-done.pkvt_ref
  37.3 0.0 copy-done.1
  37.3 10.1 %attend.1 = (bf16[256,2048]{1,0:T(8,128)(2,1)}, bf16[16,512,256]{2,1,0:T(8,128)(2,1)S(1)}, bf16[16,256,256]{2,1,0:T(8,128)(2,1)S(1)}, bf16[256,2048]{1,0:T(8,128...) custom-call(s32[1]{0:T(128)} %bitcast.lead_ref, ...), custom_call_target="tpu_custom_call" | custom-call | tf_op jit(solution)/shard_map/attend/pallas_call | solution.py:46
  47.4 3.6 %collective-permute-start.1 = (bf16[576,256]{1,0:T(8,128)(2,1)S(1)}, bf16[576,256]{1,0:T(8,128)(2,1)S(1)}, u32[]{:S(2)}, u32[]{:S(2)}) collective-permute-start(bf16[576,256]{1,0:T(8,128)(2,1)S(1)} %get-tuple-element.30), channel_id=1, source_target_pairs={{8,0},{16,8},{24,16},{32,24},{40,32},{48,40},{56,48},{64,56},{72,6... | collective-permute-start | bytes 884744 | tf_op jit(solution)/shard_map/ppermute | solution.py:337
  51.1 5.7 %gradients.1 = (bf16[8,192,256]{2,1,0:T(8,128)(2,1)S(1)}, f32[576,256]{1,0:T(8,128)S(1)}) custom-call(bf16[16,512,256]{2,1,0:T(8,128)(2,1)S(1)} %get-tuple-element.24.ds_ref, bf16[16,256,256]{2,1,0:T(8,128)(2,1)S(1)} %get-tuple-element.25.po_ref, bf16[256,2048]{1,0:T(8,128)(2,1)S(1)} %get-tuple-element.26.kp_ref, ...), custom_call_target="tpu_custom_call" | custom-call | tf_op jit(solution)/shard_map/gradients/pallas_call | solution.py:46
  56.7 0.0 collective-permute-done.1
  56.7 0.1 add_convert_fusion
  56.8 0.1 pad_maximum_fusion
  56.9 20.7 %all_to_all.11.terms_ref = bf16[8,264,256]{2,1,0:T(8,128)(2,1)S(1)} all-to-all(bf16[8,264,256]{2,1,0:T(8,128)(2,1)S(1)} %pad_maximum_fusion), channel_id=1, replica_groups=mesh['ctx'=16,'head'=8] {'head'}, dimensions={0} | all-to-all | bytes 2162688 | tf_op jit(solution)/shard_map/all_to_all | solution.py:343
  77.6 0.8 %total.1 = (f32[192,256]{1,0:T(8,128)}, f32[72,256]{1,0:T(8,128)}) custom-call(bf16[8,264,256]{2,1,0:T(8,128)(2,1)S(1)} %all_to_all.11.terms_ref), custom_call_target="tpu_custom_call" | custom-call | tf_op jit(solution)/shard_map/total/pallas_call | solution.py:313
Async XLA Ops:
  0.6 29.2 %copy-start = (bf16[512,2048]{1,0:T(8,128)(2,1)S(1)}, bf16[512,2048]{1,0:T(8,128)(2,1)}, u32[]{:S(2)}) copy-start(bf16[512,2048]{1,0:T(8,128)(2,1)} %wk_ref.5) | copy-start | bytes 6291460
  27.9 9.5 %collective-permute-start = (bf16[576,256]{1,0:T(8,128)(2,1)}, bf16[576,256]{1,0:T(8,128)(2,1)S(1)}, u32[]{:S(2)}, u32[]{:S(2)}) collective-permute-start(bf16[576,256]{1,0:T(8,128)(2,1)} %bitcast.3), channel_id=1, source_target_pairs={{0,8},{8,16},{16,24},{24,32},{32,40},{40,48},{48,56},{56,64},{64,7... | collective-permute-start | bytes 884744 | tf_op jit(solution)/shard_map/ppermute | solution.py:331
  29.8 7.5 %copy-start.1 = (bf16[256,2048]{1,0:T(8,128)(2,1)S(1)}, bf16[256,2048]{1,0:T(8,128)(2,1)}, u32[]{:S(2)}) copy-start(bf16[256,2048]{1,0:T(8,128)(2,1)} %do_ref.3) | copy-start | bytes 3145732
  47.4 9.3 %collective-permute-start.1 = (bf16[576,256]{1,0:T(8,128)(2,1)S(1)}, bf16[576,256]{1,0:T(8,128)(2,1)S(1)}, u32[]{:S(2)}, u32[]{:S(2)}) collective-permute-start(bf16[576,256]{1,0:T(8,128)(2,1)S(1)} %get-tuple-element.30), channel_id=1, source_target_pairs={{8,0},{16,8},{24,16},{32,24},{40,32},{48,40},{56,48},{64,56},{72,6... | collective-permute-start | bytes 884744 | tf_op jit(solution)/shard_map/ppermute | solution.py:337

commit v8 on v7

--- a/solution.py
+++ b/solution.py
@@ -67,14 +67,14 @@
         for i in range(P_STEPS)
     ]
     wv_in = pltpu.make_async_copy(wv_hbm, wv_ref, sems.at[P_STEPS])
-    order = [wq_in[0], wv_in, *wq_in[1:]]
-    order[0].start()
-    order[1].start()
+    order = [wv_in, *wq_in]
+    for copy in order[:3]:
+        copy.start()
 
     def arrived(i):
         order[i].wait()
-        if i + 2 < len(order):
-            order[i + 2].start()
+        if i + 3 < len(order):
+            order[i + 3].start()
 
     for i in range(PEERS):
         kvt_ref[i * KV_ROWS : (i + 1) * KV_ROWS, :] = g_ref[i, Q_ROWS:, :]
@@ -93,10 +93,8 @@
 
     k_ref[...] = mm(kv, wk_ref[...]).astype(BF16)
     arrived(0)
-    project_queries(0)
-    arrived(1)
     v_ref[...] = mm(kv, wv_ref[...]).astype(BF16)
-    for i in range(1, P_STEPS):
+    for i in range(P_STEPS):
         arrived(1 + i)
         project_queries(i)
 
@@ -121,7 +119,7 @@
 
 def attend_kernel(lead_ref, kvt_ref, pkvt_ref, q_ref, k_ref, v_ref, do_ref, wk_ref, wv_ref, wq_hbm,
                   out_hbm, ds_ref, po_ref, kp, early_ref, wq_ref,
-                  vp, dkp, dvp, out_ref, sems):
+                  vp, dkp, dvp, out_ref, acc, sems):
     wq_in = pltpu.make_async_copy(wq_hbm, wq_ref, sems.at[O_STEPS])
     wq_in.start()
     wide = HEAD_DEV * VDIM // O_STEPS
@@ -134,8 +132,31 @@
         for i in range(O_STEPS)
     ]
     pkv = pkvt_ref[:KVL, :].T
-    kp[...] = mm(pkv, wk_ref[...]).astype(BF16)
-    vp[...] = mm(pkv, wv_ref[...]).astype(BF16)
+
+    def expand(h):
+        at = slice(h * NOPE, (h + PREV_HEADS) * NOPE)
+        kp[:, at] = mm(pkv, wk_ref[:, at]).astype(BF16)
+        vp[:, at] = mm(pkv, wv_ref[:, at]).astype(BF16)
+
+    def before(h):
+        if h == 0:
+            expand(0)
+        if h % PREV_HEADS == 0 and h + PREV_HEADS < HEAD_DEV:
+            expand(h + PREV_HEADS)
+
+    def after(h):
+        if h + 1 not in EARLY_PARTS:
+            return
+        i = EARLY_PARTS.index(h + 1)
+        at = slice(NOPE * (EARLY_PARTS[i - 1] if i else 0), NOPE * (h + 1))
+        part = mm(wk_ref[:, at], dkp[:, at], NT) + mm(wv_ref[:, at], dvp[:, at], NT)
+        if i:
+            part = part + acc[...]
+        if h + 1 == HEAD_DEV:
+            early_ref[:KVL, :] = part.astype(BF16)
+        else:
+            acc[...] = part
+
     ropes_t = jnp.concatenate([pkvt_ref[KVL:, :], kvt_ref[KVL:, :]], 1)
     at_row = lax.broadcasted_iota(jnp.int32, (ROPE, 2 * TOK), 0)
     at_key = lax.broadcasted_iota(jnp.int32, (ROPE, 2 * TOK), 1)
@@ -215,30 +236,30 @@
         if (h + 1) % (HEAD_DEV // O_STEPS) == 0:
             out_copies[h // (HEAD_DEV // O_STEPS)].start()
 
-    skewed(head, HEAD_DEV, LAG)
-    early_ref[:KVL, :] = (
-        mm(wk_ref[...], dkp[...], NT) + mm(wv_ref[...], dvp[...], NT)
-    ).astype(BF16)
+    skewed(head, before, after)
     early_ref[KVL:, :] = rope_sum[0].T[:ROPE].astype(BF16)
     for copy in out_copies:
         copy.wait()
     wq_in.wait()
 
 
-LAG = 1
 O_STEPS = 4
-
-
-def skewed(make, count, lag):
+PREV_HEADS = 2
+EARLY_PARTS = (10, 14, 16)
+
+
+def skewed(make, before, after):
     running = []
-    made = 0
-    step = 0
-    while made < count or running:
-        if made < count and step % lag == 0:
+    made = done = 0
+    while done < HEAD_DEV:
+        if made < HEAD_DEV:
+            before(made)
             running.append(make(made))
             made += 1
         running = [r for r in running[::-1] if next(r, True) is None][::-1]
-        step += 1
+        while done < made - len(running):
+            after(done)
+            done += 1
 
 
 def attend(lead, kvt, pkvt, q, k, v, d_out, wk, wv, wq):
@@ -256,7 +277,7 @@
         lead, kvt, pkvt, q, k, v, d_out, wk, wv, wq,
         mib=20,
         scratch=[pltpu.VMEM((TOK, HEAD_DEV * NOPE), BF16)] * 4
-        + [pltpu.SemaphoreType.DMA((O_STEPS + 1,))],
+        + [pltpu.VMEM((KVL, TOK), F32), pltpu.SemaphoreType.DMA((O_STEPS + 1,))],
         spaces=[pltpu.SMEM] + [pltpu.VMEM] * 8 + [pltpu.HBM],
         hbm_outs=1,
     )

time: 79.5 us -> 77.7 us (0.977)
  Pallas kernels: 24 us -> 22.1 us
    pallas_call x3, Pallas kernels: 23.2 us -> 21.3 us  [kernel_call(): pl.pallas_call(body, in_specs=[pl.BlockSpec(memory_space=s or pltpu.VMEM)...]
  transfers between devices with their start and end apart: 2 -> 2, of which waited for: 0 -> 0; matrix products, arithmetic and copies ran while one was open for 0% -> 0% of each run, Pallas kernels for 17% -> 16%
where the time goes in v8:
time: 77.7 us; the launch traced here: 76.4 us
  blocking collectives  45.8 us (59%)
  Pallas kernels  22.1 us (28%)
  starting transfers between devices  5.73 us (7%)
  other arithmetic  1.21 us (2%)
  local copies, waits for them, and re-layouts  0.82 us (1%)
    all_to_all x1, blocking collectives, on_device(): g = lax.all_to_all(copies, 'head', 0, 0, tiled=True)  25.3 us
    pallas_call x3, Pallas kernels, kernel_call(): pl.pallas_call(body, in_specs=[pl.BlockSpec(memory_space=s or pltpu.VMEM)...  21.3 us
    all_to_all x1, blocking collectives, on_device(): terms = lax.all_to_all(terms, 'head', 0, 0, tiled=True)  20.5 us
    ppermute x1, starting transfers between devices, on_device(): later = lax.ppermute(early, 'ctx', [(i, i - 1) for i in range(1, blocks)])  3.82 us
    ppermute x1, starting transfers between devices, on_device(): pkvt = lax.ppermute(sent, 'ctx', [(i, i + 1) for i in range(blocks - 1)])  1.91 us
  transfers between devices with their start and end apart: 2, of which 0 were waited for; matrix products, arithmetic and copies ran while one was open for 0% of the time, Pallas kernels for 16%

profile of v8, /device:TPU:16, one launch (start us, length us, event | category | flops | bytes accessed | tf_op | source)
XLA Modules:
  0.0 76.4 jit_solution(5248937655612696956)
XLA Ops:
  0.6 0.0 copy-start
  0.6 1.1 %pad_maximum_fusion.1 = bf16[264,256]{1,0:T(8,128)(2,1)S(1)} fusion(bf16[72,256]{1,0:T(8,128)(2,1)} %bitcast.9, bf16[192,256]{1,0:T(8,128)(2,1)} %bitcast.8), kind=kLoop, calls=%fused_computation.2 | loop fusion | flops 270336 | bytes 270336 | tf_op jit(solution)/shard_map/concatenate | solution.py:348
  1.7 0.1 broadcast_in_dim.3
  1.8 25.3 %all_to_all.10.g_ref = bf16[8,264,256]{2,1,0:T(8,128)(2,1)S(1)} all-to-all(bf16[8,264,256]{2,1,0:T(8,128)(2,1)S(1)} %broadcast_in_dim.3), channel_id=1, replica_groups=mesh['ctx'=16,'head'=8] {'head'}, dimensions={0} | all-to-all | bytes 2162688 | tf_op jit(solution)/shard_map/all_to_all | solution.py:350
  27.1 0.7 slice.4
  27.9 1.9 %collective-permute-start = (bf16[576,256]{1,0:T(8,128)(2,1)}, bf16[576,256]{1,0:T(8,128)(2,1)S(1)}, u32[]{:S(2)}, u32[]{:S(2)}) collective-permute-start(bf16[576,256]{1,0:T(8,128)(2,1)} %bitcast.3), channel_id=1, source_target_pairs={{0,8},{8,16},{16,24},{24,32},{32,40},{40,48},{48,56},{56,64},{64,7... | collective-permute-start | bytes 884744 | tf_op jit(solution)/shard_map/ppermute | solution.py:352
  29.8 0.0 copy-done
  29.8 0.0 copy-start.1
  29.8 6.6 %project.1 = (bf16[256,4096]{1,0:T(8,128)(2,1)S(1)}, bf16[256,2048]{1,0:T(8,128)(2,1)S(1)}, bf16[256,2048]{1,0:T(8,128)(2,1)S(1)}, bf16[576,256]{1,0:T(8,128)(2,1)S(1)}, bf16[512,2048]{1,0:T(8,128)(2,1)S(1)}) custom-call(bf16[8,264,256]{2,1,0:T(8,128)(2,1)S(1)} %all_to_all.10.g_ref, bf16[1536,3072]{1,0:T(8,128)(2,1)} %wq_hbm.3, ...), custom_call_target="tpu_custom_call" | custom-call | tf_op jit(solution)/shard_map/project/pallas_call | solution.py:46
  36.5 0.0 collective-permute-done.pkvt_ref
  36.5 0.0 copy-done.1
  36.5 9.0 %attend.1 = (bf16[256,2048]{1,0:T(8,128)(2,1)}, bf16[16,512,256]{2,1,0:T(8,128)(2,1)S(1)}, bf16[16,256,256]{2,1,0:T(8,128)(2,1)S(1)}, bf16[256,2048]{1,0:T(8,128...) custom-call(s32[1]{0:T(128)} %bitcast.lead_ref, ...), custom_call_target="tpu_custom_call" | custom-call | tf_op jit(solution)/shard_map/attend/pallas_call | solution.py:46
  45.5 3.8 %collective-permute-start.1 = (bf16[576,256]{1,0:T(8,128)(2,1)S(1)}, bf16[576,256]{1,0:T(8,128)(2,1)S(1)}, u32[]{:S(2)}, u32[]{:S(2)}) collective-permute-start(bf16[576,256]{1,0:T(8,128)(2,1)S(1)} %get-tuple-element.30), channel_id=1, source_target_pairs={{8,0},{16,8},{24,16},{32,24},{40,32},{48,40},{56,48},{64,56},{72,6... | collective-permute-start | bytes 884744 | tf_op jit(solution)/shard_map/ppermute | solution.py:358
  49.3 5.7 %gradients.1 = (bf16[8,192,256]{2,1,0:T(8,128)(2,1)S(1)}, f32[576,256]{1,0:T(8,128)S(1)}) custom-call(bf16[16,512,256]{2,1,0:T(8,128)(2,1)S(1)} %get-tuple-element.24.ds_ref, bf16[16,256,256]{2,1,0:T(8,128)(2,1)S(1)} %get-tuple-element.25.po_ref, bf16[256,2048]{1,0:T(8,128)(2,1)S(1)} %get-tuple-element.26.kp_ref, ...), custom_call_target="tpu_custom_call" | custom-call | tf_op jit(solution)/shard_map/gradients/pallas_call | solution.py:46
  55.0 0.0 collective-permute-done.1
  55.0 0.1 add_convert_fusion
  55.1 0.1 pad_maximum_fusion
  55.1 20.5 %all_to_all.11.terms_ref = bf16[8,264,256]{2,1,0:T(8,128)(2,1)S(1)} all-to-all(bf16[8,264,256]{2,1,0:T(8,128)(2,1)S(1)} %pad_maximum_fusion), channel_id=1, replica_groups=mesh['ctx'=16,'head'=8] {'head'}, dimensions={0} | all-to-all | bytes 2162688 | tf_op jit(solution)/shard_map/all_to_all | solution.py:364
  75.6 0.8 %total.1 = (f32[192,256]{1,0:T(8,128)}, f32[72,256]{1,0:T(8,128)}) custom-call(bf16[8,264,256]{2,1,0:T(8,128)(2,1)S(1)} %all_to_all.11.terms_ref), custom_call_target="tpu_custom_call" | custom-call | tf_op jit(solution)/shard_map/total/pallas_call | solution.py:334
Async XLA Ops:
  0.6 29.2 %copy-start = (bf16[512,2048]{1,0:T(8,128)(2,1)S(1)}, bf16[512,2048]{1,0:T(8,128)(2,1)}, u32[]{:S(2)}) copy-start(bf16[512,2048]{1,0:T(8,128)(2,1)} %wk_ref.5) | copy-start | bytes 6291460
  27.9 8.6 %collective-permute-start = (bf16[576,256]{1,0:T(8,128)(2,1)}, bf16[576,256]{1,0:T(8,128)(2,1)S(1)}, u32[]{:S(2)}, u32[]{:S(2)}) collective-permute-start(bf16[576,256]{1,0:T(8,128)(2,1)} %bitcast.3), channel_id=1, source_target_pairs={{0,8},{8,16},{16,24},{24,32},{32,40},{40,48},{48,56},{56,64},{64,7... | collective-permute-start | bytes 884744 | tf_op jit(solution)/shard_map/ppermute | solution.py:352
  29.8 6.7 %copy-start.1 = (bf16[256,2048]{1,0:T(8,128)(2,1)S(1)}, bf16[256,2048]{1,0:T(8,128)(2,1)}, u32[]{:S(2)}) copy-start(bf16[256,2048]{1,0:T(8,128)(2,1)} %do_ref.3) | copy-start | bytes 3145732
  45.5 9.5 %collective-permute-start.1 = (bf16[576,256]{1,0:T(8,128)(2,1)S(1)}, bf16[576,256]{1,0:T(8,128)(2,1)S(1)}, u32[]{:S(2)}, u32[]{:S(2)}) collective-permute-start(bf16[576,256]{1,0:T(8,128)(2,1)S(1)} %get-tuple-element.30), channel_id=1, source_target_pairs={{8,0},{16,8},{24,16},{32,24},{40,32},{48,40},{56,48},{64,56},{72,6... | collective-permute-start | bytes 884744 | tf_op jit(solution)/shard_map/ppermute | solution.py:358

commit v9 on v8

--- a/solution.py
+++ b/solution.py
@@ -58,8 +58,8 @@
 P_STEPS = HEAD_DEV // P_HEADS
 
 
-def project_kernel(g_ref, wq_hbm, wk_ref, wv_hbm,
-                   q_ref, k_ref, v_ref, kvt_ref, wv_ref, wq_ref, sems):
+def project_kernel(g_ref, kvt_ref, wq_hbm, wk_ref, wv_hbm,
+                   q_ref, k_ref, v_ref, wv_ref, wq_ref, sems):
     cols = P_HEADS * WIDTH
     part = lambda i: slice(i * cols, (i + 1) * cols)
     wq_in = [
@@ -76,8 +76,6 @@
         if i + 3 < len(order):
             order[i + 3].start()
 
-    for i in range(PEERS):
-        kvt_ref[i * KV_ROWS : (i + 1) * KV_ROWS, :] = g_ref[i, Q_ROWS:, :]
     kv = kvt_ref[:KVL, :].T
     qlat = g_ref[:, :Q_ROWS, :].reshape(QL, TOK).T
     lane = lax.broadcasted_iota(jnp.int32, (TOK, PAD - WIDTH), 1)
@@ -99,7 +97,7 @@
         project_queries(i)
 
 
-def project(g, wq, wk, wv):
+def project(g, kvt, wq, wk, wv):
     return kernel_call(
         project_kernel,
         "project",
@@ -107,13 +105,12 @@
             ((TOK, HEAD_DEV * PAD), BF16),
             ((TOK, HEAD_DEV * NOPE), BF16),
             ((TOK, HEAD_DEV * VDIM), BF16),
-            ((KVL + ROPE, TOK), BF16),
             (wv.shape, BF16),
         ],
-        g, wq, wk, wv,
+        g, kvt, wq, wk, wv,
         mib=20,
         scratch=[pltpu.VMEM(wq.shape, BF16), pltpu.SemaphoreType.DMA((P_STEPS + 1,))],
-        spaces=[None, pltpu.HBM, pltpu.VMEM, pltpu.HBM],
+        spaces=[None, pltpu.VMEM, pltpu.HBM, pltpu.VMEM, pltpu.HBM],
     )
 
 
@@ -348,9 +345,9 @@
     own = jnp.concatenate([q_latent.T, kv_latent.T], 0)
     copies = jnp.broadcast_to(own, (peers, *own.shape))
     g = lax.all_to_all(copies, "head", 0, 0, tiled=True)
-    sent = g[:, Q_ROWS:, :].reshape(KVL + ROPE, TOK)
-    pkvt = lax.ppermute(sent, "ctx", [(i, i + 1) for i in range(blocks - 1)])
-    q, k, v, kvt, wv_in = project(g, w_query, w_key, w_value)
+    kvt = g[:, Q_ROWS:, :].reshape(KVL + ROPE, TOK)
+    pkvt = lax.ppermute(kvt, "ctx", [(i, i + 1) for i in range(blocks - 1)])
+    q, k, v, wv_in = project(g, kvt, w_query, w_key, w_value)
     lead = (lax.axis_index("ctx") == 0).astype(jnp.int32).reshape(1)
     out, ds, po, kp, early, wq_in = attend(
         lead, kvt, pkvt, q, k, v, d_out, w_key, wv_in, w_query

time: 77.7 us -> 78.3 us (level)
  Pallas kernels: 22.1 us -> 24 us
    pallas_call x3, Pallas kernels: 21.3 us -> 23.2 us  [kernel_call(): pl.pallas_call(body, in_specs=[pl.BlockSpec(memory_space=s or pltpu.VMEM)...]
  transfers between devices with their start and end apart: 2 -> 2, of which waited for: 0 -> 0; matrix products, arithmetic and copies ran while one was open for 0% -> 0% of each run, Pallas kernels for 16% -> 17%
where the time goes in v9:
time: 78.3 us; the launch traced here: 77.4 us
  blocking collectives  45.6 us (58%)
  Pallas kernels  24 us (31%)
  starting transfers between devices  5.74 us (7%)
  other arithmetic  1.21 us (2%)
    all_to_all x1, blocking collectives, on_device(): g = lax.all_to_all(copies, 'head', 0, 0, tiled=True)  25.3 us
    pallas_call x3, Pallas kernels, kernel_call(): pl.pallas_call(body, in_specs=[pl.BlockSpec(memory_space=s or pltpu.VMEM)...  23.2 us
    all_to_all x1, blocking collectives, on_device(): terms = lax.all_to_all(terms, 'head', 0, 0, tiled=True)  20.3 us
    ppermute x1, starting transfers between devices, on_device(): later = lax.ppermute(early, 'ctx', [(i, i - 1) for i in range(1, blocks)])  3.82 us
    ppermute x1, starting transfers between devices, on_device(): pkvt = lax.ppermute(kvt, 'ctx', [(i, i + 1) for i in range(blocks - 1)])  1.92 us
  transfers between devices with their start and end apart: 2, of which 0 were waited for; matrix products, arithmetic and copies ran while one was open for 0% of the time, Pallas kernels for 17%

profile of v9, /device:TPU:16, one launch (start us, length us, event | category | flops | bytes accessed | tf_op | source)
XLA Modules:
  0.0 77.4 jit_solution(13124749744550471279)
XLA Ops:
  0.6 0.0 copy-start
  0.6 1.1 %pad_maximum_fusion.1 = bf16[264,256]{1,0:T(8,128)(2,1)S(1)} fusion(bf16[72,256]{1,0:T(8,128)(2,1)} %bitcast.13, bf16[192,256]{1,0:T(8,128)(2,1)} %bitcast.12), kind=kLoop, calls=%fused_computation.2 | loop fusion | flops 270336 | bytes 270336 | tf_op jit(solution)/shard_map/concatenate | solution.py:345
  1.7 0.1 broadcast_in_dim.3
  1.8 25.3 %all_to_all.10.g_ref = bf16[8,264,256]{2,1,0:T(8,128)(2,1)S(1)} all-to-all(bf16[8,264,256]{2,1,0:T(8,128)(2,1)S(1)} %broadcast_in_dim.3), channel_id=1, replica_groups=mesh['ctx'=16,'head'=8] {'head'}, dimensions={0} | all-to-all | bytes 2162688 | tf_op jit(solution)/shard_map/all_to_all | solution.py:347
  27.1 1.9 %collective-permute-start = (bf16[576,256]{1,0:T(8,128)(2,1)S(1)}, bf16[576,256]{1,0:T(8,128)(2,1)}, u32[]{:S(2)}, u32[]{:S(2)}) collective-permute-start(bf16[576,256]{1,0:T(8,128)(2,1)S(1)} %bitcast.7), channel_id=1, source_target_pairs={{0,8},{8,16},{16,24},{24,32},{32,40},{40,48},{48,56},{56,64},{64,7... | collective-permute-start | bytes 884744 | tf_op jit(solution)/shard_map/ppermute | solution.py:349
  29.1 0.0 copy-done
  29.1 0.0 copy-start.1
  29.1 6.6 %project.1 = (bf16[256,4096]{1,0:T(8,128)(2,1)S(1)}, bf16[256,2048]{1,0:T(8,128)(2,1)S(1)}, bf16[256,2048]{1,0:T(8,128)(2,1)S(1)}, bf16[512,2048]{1,0:T(8,128)(2,1)S(1)}) custom-call(bf16[8,264,256]{2,1,0:T(8,128)(2,1)S(1)} %all_to_all.10.g_ref, bf16[576,256]{1,0:T(8,128)(2,1)S(1)} %bitcast.8, bf16[1536,3072]{1,0:T(8,128)(2,1)} %wq_hbm.3, ...), custom_call_target="tpu_custom_call" | custom-call | tf_op jit(solution)/shard_map/project/pallas_call | solution.py:46
  35.8 0.0 collective-permute-done.pkvt_ref
  35.8 0.0 copy-done.1
  35.8 9.9 %attend.1 = (bf16[256,2048]{1,0:T(8,128)(2,1)}, bf16[16,512,256]{2,1,0:T(8,128)(2,1)S(1)}, bf16[16,256,256]{2,1,0:T(8,128)(2,1)S(1)}, bf16[256,2048]{1,0:T(8,128...) custom-call(s32[1]{0:T(128)} %bitcast.lead_ref, bf16[576,256]{1,0:T(8,128)(2,1)S(1)} %bitcast.9, ...), custom_call_target="tpu_custom_call" | custom-call | tf_op jit(solution)/shard_map/attend/pallas_call | solution.py:46
  45.7 3.8 %collective-permute-start.1 = (bf16[576,256]{1,0:T(8,128)(2,1)S(1)}, bf16[576,256]{1,0:T(8,128)(2,1)S(1)}, u32[]{:S(2)}, u32[]{:S(2)}) collective-permute-start(bf16[576,256]{1,0:T(8,128)(2,1)S(1)} %get-tuple-element.28), channel_id=1, source_target_pairs={{8,0},{16,8},{24,16},{32,24},{40,32},{48,40},{56,48},{64,56},{72,6... | collective-permute-start | bytes 884744 | tf_op jit(solution)/shard_map/ppermute | solution.py:355
  49.5 6.6 %gradients.1 = (bf16[8,192,256]{2,1,0:T(8,128)(2,1)S(1)}, f32[576,256]{1,0:T(8,128)S(1)}) custom-call(bf16[16,512,256]{2,1,0:T(8,128)(2,1)S(1)} %get-tuple-element.22.ds_ref, bf16[16,256,256]{2,1,0:T(8,128)(2,1)S(1)} %get-tuple-element.23.po_ref, bf16[256,2048]{1,0:T(8,128)(2,1)S(1)} %get-tuple-element.24.kp_ref, ...), custom_call_target="tpu_custom_call" | custom-call | tf_op jit(solution)/shard_map/gradients/pallas_call | solution.py:46
  56.2 0.0 collective-permute-done.1
  56.2 0.1 add_convert_fusion
  56.3 0.1 pad_maximum_fusion
  56.4 20.3 %all_to_all.11.terms_ref = bf16[8,264,256]{2,1,0:T(8,128)(2,1)S(1)} all-to-all(bf16[8,264,256]{2,1,0:T(8,128)(2,1)S(1)} %pad_maximum_fusion), channel_id=1, replica_groups=mesh['ctx'=16,'head'=8] {'head'}, dimensions={0} | all-to-all | bytes 2162688 | tf_op jit(solution)/shard_map/all_to_all | solution.py:361
  76.6 0.8 %total.1 = (f32[192,256]{1,0:T(8,128)}, f32[72,256]{1,0:T(8,128)}) custom-call(bf16[8,264,256]{2,1,0:T(8,128)(2,1)S(1)} %all_to_all.11.terms_ref), custom_call_target="tpu_custom_call" | custom-call | tf_op jit(solution)/shard_map/total/pallas_call | solution.py:331
  (1 shorter events, 0.0 us)
Async XLA Ops:
  0.6 28.5 %copy-start = (bf16[512,2048]{1,0:T(8,128)(2,1)S(1)}, bf16[512,2048]{1,0:T(8,128)(2,1)}, u32[]{:S(2)}) copy-start(bf16[512,2048]{1,0:T(8,128)(2,1)} %wk_ref.5) | copy-start | bytes 6291460
  27.1 8.6 %collective-permute-start = (bf16[576,256]{1,0:T(8,128)(2,1)S(1)}, bf16[576,256]{1,0:T(8,128)(2,1)}, u32[]{:S(2)}, u32[]{:S(2)}) collective-permute-start(bf16[576,256]{1,0:T(8,128)(2,1)S(1)} %bitcast.7), channel_id=1, source_target_pairs={{0,8},{8,16},{16,24},{24,32},{32,40},{40,48},{48,56},{56,64},{64,7... | collective-permute-start | bytes 884744 | tf_op jit(solution)/shard_map/ppermute | solution.py:349
  29.1 6.7 %copy-start.1 = (bf16[256,2048]{1,0:T(8,128)(2,1)S(1)}, bf16[256,2048]{1,0:T(8,128)(2,1)}, u32[]{:S(2)}) copy-start(bf16[256,2048]{1,0:T(8,128)(2,1)} %do_ref.3) | copy-start | bytes 3145732
  45.7 10.5 %collective-permute-start.1 = (bf16[576,256]{1,0:T(8,128)(2,1)S(1)}, bf16[576,256]{1,0:T(8,128)(2,1)S(1)}, u32[]{:S(2)}, u32[]{:S(2)}) collective-permute-start(bf16[576,256]{1,0:T(8,128)(2,1)S(1)} %get-tuple-element.28), channel_id=1, source_target_pairs={{8,0},{16,8},{24,16},{32,24},{40,32},{48,40},{56,48},{64,56},{72,6... | collective-permute-start | bytes 884744 | tf_op jit(solution)/shard_map/ppermute | solution.py:355

commit v10 on v8

--- a/solution.py
+++ b/solution.py
@@ -58,8 +58,8 @@
 P_STEPS = HEAD_DEV // P_HEADS
 
 
-def project_kernel(g_ref, wq_hbm, wk_ref, wv_hbm,
-                   q_ref, k_ref, v_ref, kvt_ref, wv_ref, wq_ref, sems):
+def project_kernel(g_ref, wq_hbm, wk_hbm, wv_hbm,
+                   q_ref, k_ref, v_ref, kvt_ref, wk_ref, wv_ref, wq_ref, sems):
     cols = P_HEADS * WIDTH
     part = lambda i: slice(i * cols, (i + 1) * cols)
     wq_in = [
@@ -67,7 +67,8 @@
         for i in range(P_STEPS)
     ]
     wv_in = pltpu.make_async_copy(wv_hbm, wv_ref, sems.at[P_STEPS])
-    order = [wv_in, *wq_in]
+    wk_in = pltpu.make_async_copy(wk_hbm, wk_ref, sems.at[P_STEPS + 1])
+    order = [wk_in, wv_in, *wq_in]
     for copy in order[:3]:
         copy.start()
 
@@ -91,11 +92,12 @@
                 [queries[:, j * WIDTH : (j + 1) * WIDTH], one], 1
             )
 
+    arrived(0)
     k_ref[...] = mm(kv, wk_ref[...]).astype(BF16)
-    arrived(0)
+    arrived(1)
     v_ref[...] = mm(kv, wv_ref[...]).astype(BF16)
     for i in range(P_STEPS):
-        arrived(1 + i)
+        arrived(2 + i)
         project_queries(i)
 
 
@@ -108,12 +110,13 @@
             ((TOK, HEAD_DEV * NOPE), BF16),
             ((TOK, HEAD_DEV * VDIM), BF16),
             ((KVL + ROPE, TOK), BF16),
+            (wk.shape, BF16),
             (wv.shape, BF16),
         ],
         g, wq, wk, wv,
         mib=20,
-        scratch=[pltpu.VMEM(wq.shape, BF16), pltpu.SemaphoreType.DMA((P_STEPS + 1,))],
-        spaces=[None, pltpu.HBM, pltpu.VMEM, pltpu.HBM],
+        scratch=[pltpu.VMEM(wq.shape, BF16), pltpu.SemaphoreType.DMA((P_STEPS + 2,))],
+        spaces=[None] + [pltpu.HBM] * 3,
     )
 
 
@@ -245,7 +248,7 @@
 
 O_STEPS = 4
 PREV_HEADS = 2
-EARLY_PARTS = (10, 14, 16)
+EARLY_PARTS = (6, 10, 14, 16)
 
 
 def skewed(make, before, after):
@@ -350,14 +353,14 @@
     g = lax.all_to_all(copies, "head", 0, 0, tiled=True)
     sent = g[:, Q_ROWS:, :].reshape(KVL + ROPE, TOK)
     pkvt = lax.ppermute(sent, "ctx", [(i, i + 1) for i in range(blocks - 1)])
-    q, k, v, kvt, wv_in = project(g, w_query, w_key, w_value)
+    q, k, v, kvt, wk_in, wv_in = project(g, w_query, w_key, w_value)
     lead = (lax.axis_index("ctx") == 0).astype(jnp.int32).reshape(1)
     out, ds, po, kp, early, wq_in = attend(
-        lead, kvt, pkvt, q, k, v, d_out, w_key, wv_in, w_query
+        lead, kvt, pkvt, q, k, v, d_out, wk_in, wv_in, w_query
     )
     later = lax.ppermute(early, "ctx", [(i, i - 1) for i in range(1, blocks)])
     gq, gkv = gradients(
-        ds, po, kp, k, kvt, pkvt, q, d_out, wq_in, w_key, wv_in
+        ds, po, kp, k, kvt, pkvt, q, d_out, wq_in, wk_in, wv_in
     )
     gkv = (gkv + later.astype(F32)).astype(BF16)
     terms = jnp.concatenate([gq, gkv.reshape(peers, -1, TOK)], 1)

time: 77.7 us -> 77.4 us (level)
  transfers between devices with their start and end apart: 2 -> 2, of which waited for: 0 -> 0; matrix products, arithmetic and copies ran while one was open for 0% -> 0% of each run, Pallas kernels for 16% -> 17%
where the time goes in v10:
time: 77.4 us; the launch traced here: 76.1 us
  blocking collectives  45.8 us (59%)
  Pallas kernels  22.6 us (29%)
  starting transfers between devices  5.74 us (7%)
  other arithmetic  1.07 us (1%)
    all_to_all x1, blocking collectives, on_device(): g = lax.all_to_all(copies, 'head', 0, 0, tiled=True)  25.3 us
    pallas_call x3, Pallas kernels, kernel_call(): pl.pallas_call(body, in_specs=[pl.BlockSpec(memory_space=s or pltpu.VMEM)...  21.8 us
    all_to_all x1, blocking collectives, on_device(): terms = lax.all_to_all(terms, 'head', 0, 0, tiled=True)  20.5 us
    ppermute x1, starting transfers between devices, on_device(): later = lax.ppermute(early, 'ctx', [(i, i - 1) for i in range(1, blocks)])  3.82 us
    ppermute x1, starting transfers between devices, on_device(): pkvt = lax.ppermute(sent, 'ctx', [(i, i + 1) for i in range(blocks - 1)])  1.92 us
  transfers between devices with their start and end apart: 2, of which 0 were waited for; matrix products, arithmetic and copies ran while one was open for 0% of the time, Pallas kernels for 17%

profile of v10, /device:TPU:16, one launch (start us, length us, event | category | flops | bytes accessed | tf_op | source)
XLA Modules:
  0.0 76.1 jit_solution(12677948957902796271)
XLA Ops:
  0.6 0.9 %pad_maximum_fusion.1 = bf16[264,256]{1,0:T(8,128)(2,1)S(1)} fusion(bf16[72,256]{1,0:T(8,128)(2,1)} %bitcast.10, bf16[192,256]{1,0:T(8,128)(2,1)} %bitcast.9), kind=kLoop, calls=%fused_computation.2 | loop fusion | flops 270336 | bytes 270336 | tf_op jit(solution)/shard_map/concatenate | solution.py:351
  1.6 0.1 broadcast_in_dim.3
  1.6 25.3 %all_to_all.10.g_ref = bf16[8,264,256]{2,1,0:T(8,128)(2,1)S(1)} all-to-all(bf16[8,264,256]{2,1,0:T(8,128)(2,1)S(1)} %broadcast_in_dim.3), channel_id=1, replica_groups=mesh['ctx'=16,'head'=8] {'head'}, dimensions={0} | all-to-all | bytes 2162688 | tf_op jit(solution)/shard_map/all_to_all | solution.py:353
  27.0 1.9 %collective-permute-start = (bf16[576,256]{1,0:T(8,128)(2,1)S(1)}, bf16[576,256]{1,0:T(8,128)(2,1)S(1)}, u32[]{:S(2)}, u32[]{:S(2)}) collective-permute-start(bf16[576,256]{1,0:T(8,128)(2,1)S(1)} %bitcast.8), channel_id=1, source_target_pairs={{0,8},{8,16},{16,24},{24,32},{32,40},{40,48},{48,56},{56,64},{64,7... | collective-permute-start | bytes 884744 | tf_op jit(solution)/shard_map/ppermute | solution.py:355
  28.9 0.0 copy-start
  28.9 7.4 %project.1 = (bf16[256,4096]{1,0:T(8,128)(2,1)S(1)}, bf16[256,2048]{1,0:T(8,128)(2,1)S(1)}, bf16[256,2048]{1,0:T(8,128)(2,1)S(1)}, bf16[576,256]{1,0:T(8,128)(2,...) custom-call(bf16[8,264,256]{2,1,0:T(8,128)(2,1)S(1)} %all_to_all.10.g_ref, ...), custom_call_target="tpu_custom_call" | custom-call | tf_op jit(solution)/shard_map/project/pallas_call | solution.py:46
  36.3 0.0 collective-permute-done.pkvt_ref
  36.3 0.0 copy-done
  36.3 8.8 %attend.1 = (bf16[256,2048]{1,0:T(8,128)(2,1)}, bf16[16,512,256]{2,1,0:T(8,128)(2,1)S(1)}, bf16[16,256,256]{2,1,0:T(8,128)(2,1)S(1)}, bf16[256,2048]{1,0:T(8,128...) custom-call(s32[1]{0:T(128)} %bitcast.lead_ref, ...), custom_call_target="tpu_custom_call" | custom-call | tf_op jit(solution)/shard_map/attend/pallas_call | solution.py:46
  45.1 3.8 %collective-permute-start.1 = (bf16[576,256]{1,0:T(8,128)(2,1)S(1)}, bf16[576,256]{1,0:T(8,128)(2,1)S(1)}, u32[]{:S(2)}, u32[]{:S(2)}) collective-permute-start(bf16[576,256]{1,0:T(8,128)(2,1)S(1)} %get-tuple-element.32), channel_id=1, source_target_pairs={{8,0},{16,8},{24,16},{32,24},{40,32},{48,40},{56,48},{64,56},{72,6... | collective-permute-start | bytes 884744 | tf_op jit(solution)/shard_map/ppermute | solution.py:361
  49.0 5.7 %gradients.1 = (bf16[8,192,256]{2,1,0:T(8,128)(2,1)S(1)}, f32[576,256]{1,0:T(8,128)S(1)}) custom-call(bf16[16,512,256]{2,1,0:T(8,128)(2,1)S(1)} %get-tuple-element.26.ds_ref, bf16[16,256,256]{2,1,0:T(8,128)(2,1)S(1)} %get-tuple-element.27.po_ref, bf16[256,2048]{1,0:T(8,128)(2,1)S(1)} %get-tuple-element.28.kp_ref, ...), custom_call_target="tpu_custom_call" | custom-call | tf_op jit(solution)/shard_map/gradients/pallas_call | solution.py:46
  54.7 0.0 collective-permute-done.1
  54.7 0.1 add_convert_fusion
  54.7 0.1 pad_maximum_fusion
  54.8 20.5 %all_to_all.11.terms_ref = bf16[8,264,256]{2,1,0:T(8,128)(2,1)S(1)} all-to-all(bf16[8,264,256]{2,1,0:T(8,128)(2,1)S(1)} %pad_maximum_fusion), channel_id=1, replica_groups=mesh['ctx'=16,'head'=8] {'head'}, dimensions={0} | all-to-all | bytes 2162688 | tf_op jit(solution)/shard_map/all_to_all | solution.py:367
  75.3 0.8 %total.1 = (f32[192,256]{1,0:T(8,128)}, f32[72,256]{1,0:T(8,128)}) custom-call(bf16[8,264,256]{2,1,0:T(8,128)(2,1)S(1)} %all_to_all.11.terms_ref), custom_call_target="tpu_custom_call" | custom-call | tf_op jit(solution)/shard_map/total/pallas_call | solution.py:337
  (1 shorter events, 0.0 us)
Async XLA Ops:
  27.0 9.3 %collective-permute-start = (bf16[576,256]{1,0:T(8,128)(2,1)S(1)}, bf16[576,256]{1,0:T(8,128)(2,1)S(1)}, u32[]{:S(2)}, u32[]{:S(2)}) collective-permute-start(bf16[576,256]{1,0:T(8,128)(2,1)S(1)} %bitcast.8), channel_id=1, source_target_pairs={{0,8},{8,16},{16,24},{24,32},{32,40},{40,48},{48,56},{56,64},{64,7... | collective-permute-start | bytes 884744 | tf_op jit(solution)/shard_map/ppermute | solution.py:355
  28.9 7.4 %copy-start = (bf16[256,2048]{1,0:T(8,128)(2,1)S(1)}, bf16[256,2048]{1,0:T(8,128)(2,1)}, u32[]{:S(2)}) copy-start(bf16[256,2048]{1,0:T(8,128)(2,1)} %do_ref.3) | copy-start | bytes 3145732
  45.1 9.5 %collective-permute-start.1 = (bf16[576,256]{1,0:T(8,128)(2,1)S(1)}, bf16[576,256]{1,0:T(8,128)(2,1)S(1)}, u32[]{:S(2)}, u32[]{:S(2)}) collective-permute-start(bf16[576,256]{1,0:T(8,128)(2,1)S(1)} %get-tuple-element.32), channel_id=1, source_target_pairs={{8,0},{16,8},{24,16},{32,24},{40,32},{48,40},{56,48},{64,56},{72,6... | collective-permute-start | bytes 884744 | tf_op jit(solution)/shard_map/ppermute | solution.py:361
